TPU v7x, 128 devices: a whole 4x4x4 slice. The times are simulated.
128 devices in a mesh: view: 8 (over y, core), block: 16 (over z, x).
Axes of the slice: x: 4, y: 4, z: 4, core: 2. Of those that a mesh axis runs over, the one named last changes fastest.
Arguments:
- estimate0: float32 [1024, 64, 256], P('block'), may hold values from 0.5 to 1.5
- pieces: bfloat16 [8, 256, 4, 64, 256], P('view', 'block'), may hold values from 0.19921875 to 2
- dest_block: int32 [8, 256, 1], replicated, may hold values from 0 to 15; in each aligned block of 16 rows (0 to 15, 16 to 31, ..., all dimensions but the last counted through in order) at most 2 rows name the same one
- slot_index: int32 [8, 256], replicated, may hold values from 0 to 15
- psf_shift: int32 [8, 3], replicated, may hold values from -3 to 3
- psf_taps: float32 [8, 3, 21], replicated, may hold values from 0.05 to 1
- background: float32 [8], replicated, may hold values from 0.1 to 0.5
Outputs:
- estimate: float32 [1024, 64, 256], P('block')
Inputs may be any that keep to these rules, and one draw needn't show every extreme that they name: `dest_block`: among the 16 pieces held by one device (aligned blocks of 16 rows, views and pieces taken together), no slab is named more than 2 times.
All inputs are finite; a program needn't handle non-finite values.
Results may differ from a plain program's by a relative error of at most 0.0014.
Values may be sent and summed in bfloat16 or wider, within the bound.
No kernel may reach another device: no remote copies, remote signals or barrier semaphores. Data moves between devices by JAX's collectives and lax.ppermute only.
A program may use at most 128 MiB of HBM per device.

v0:
```python
import jax
import jax.numpy as jnp
from jax import lax
from jax.sharding import PartitionSpec as P

CAP = 2
ITERS = 2
HALO = 13


HIGHEST = lax.Precision.HIGHEST


def with_halo(cells, sides, width):
    for axis, dim in sides:
        count = lax.axis_size(axis)
        ends = count - 1
        head = lax.slice_in_dim(cells, 0, width, axis=dim)
        tail = lax.slice_in_dim(cells, cells.shape[dim] - width, cells.shape[dim], axis=dim)
        cells = jnp.concatenate(
            [
                lax.ppermute(tail, axis, [(i, (i + 1) % count) for i in range(ends)]),
                cells,
                lax.ppermute(head, axis, [((i + 1) % count, i) for i in range(ends)]),
            ],
            axis=dim,
        )
    return cells


def band_matrix(kernel, shift, row_count, column_count, lead_offset):
    tap_count = kernel.shape[0]
    radius = (tap_count - 1) // 2
    difference = (
        lax.broadcasted_iota(jnp.int32, (row_count, column_count), 1)
        - lax.broadcasted_iota(jnp.int32, (row_count, column_count), 0)
        - lead_offset
        - shift
        + radius
    )
    tap_hits = difference[:, :, None] == jnp.arange(tap_count, dtype=jnp.int32)[None, None, :]
    return jnp.sum(jnp.where(tap_hits, kernel[None, None, :], 0.0), axis=2)


def column_sums(kernel, shift, length):
    tap_count = kernel.shape[-1]
    radius = (tap_count - 1) // 2
    source = (
        jnp.arange(length, dtype=jnp.int32)[None, :, None]
        - shift[:, None, None]
        - jnp.arange(tap_count, dtype=jnp.int32)[None, None, :]
        + radius
    )
    inside = (source >= 0) & (source < length)
    return jnp.sum(jnp.where(inside, kernel[:, None, :], 0.0), axis=2)


def blur_plane(volume, band_rows, band_columns):
    along_rows = jnp.einsum("yv,zvx->zyx", band_rows, volume, precision=HIGHEST)
    return jnp.einsum("zyv,xv->zyx", along_rows, band_columns, precision=HIGHEST)


def adjoint_plane(volume, band_rows, band_columns):
    along_rows = jnp.einsum("vy,zvx->zyx", band_rows, volume, precision=HIGHEST)
    return jnp.einsum("zyv,vx->zyx", along_rows, band_columns, precision=HIGHEST)


def along_depth(matrix, volume):
    flattened = volume.reshape(volume.shape[0], volume.shape[1] * volume.shape[2])
    result = jnp.dot(matrix, flattened, precision=HIGHEST)
    return result.reshape(matrix.shape[0], volume.shape[1], volume.shape[2])


def shards(estimate0, pieces, dest_block, slot_index, psf_shift, psf_taps, background):
    block_count = lax.axis_size("block")
    my_view = lax.axis_index("view")
    my_block = lax.axis_index("block")
    slab_depth = estimate0.shape[0]
    plane_rows = estimate0.shape[1]
    plane_columns = estimate0.shape[2]
    slot_count = pieces.shape[1]
    piece_depth = pieces.shape[2]
    plane_size = piece_depth * plane_rows * plane_columns
    kernel = psf_taps / jnp.sum(psf_taps, axis=2, keepdims=True)
    own_kernel = lax.dynamic_index_in_dim(kernel, my_view, 0, keepdims=False)
    own_shift = lax.dynamic_index_in_dim(psf_shift, my_view, 0, keepdims=False)
    offset = lax.dynamic_index_in_dim(background, my_view, 0, keepdims=False)
    band_rows = band_matrix(own_kernel[1], own_shift[1], plane_rows, plane_rows, 0)
    band_columns = band_matrix(own_kernel[2], own_shift[2], plane_columns, plane_columns, 0)
    targets = dest_block[:, :, 0]
    global_slot = targets * slot_count + slot_index
    slot_total = block_count * slot_count
    slot_hits = (
        global_slot[:, :, None] == jnp.arange(slot_total, dtype=jnp.int32)[None, None, :]
    ).astype(jnp.int32)
    counts_all = jnp.sum(slot_hits, axis=1)
    view_targets = lax.dynamic_index_in_dim(targets, my_view, 0, keepdims=False).reshape(
        block_count, slot_count
    )
    view_slots = lax.dynamic_index_in_dim(slot_index, my_view, 0, keepdims=False).reshape(
        block_count, slot_count
    )
    earlier = lax.broadcasted_iota(jnp.int32, (slot_count, slot_count), 1) < lax.broadcasted_iota(
        jnp.int32, (slot_count, slot_count), 0
    )
    same_target = view_targets[:, :, None] == view_targets[:, None, :]
    ranks = jnp.sum((same_target & earlier[None, :, :]).astype(jnp.int32), axis=2)
    own_targets = lax.dynamic_index_in_dim(view_targets, my_block, 0, keepdims=False)
    own_ranks = lax.dynamic_index_in_dim(ranks, my_block, 0, keepdims=False)
    buffer_slots = jnp.arange(block_count * CAP, dtype=jnp.int32)
    chooser = (buffer_slots[:, None] == (own_targets * CAP + own_ranks)[None, :]).astype(
        jnp.bfloat16
    )
    outgoing = jnp.dot(
        chooser, pieces[0].reshape(slot_count, plane_size), preferred_element_type=jnp.float32
    )
    outgoing = outgoing.astype(jnp.bfloat16).reshape(block_count, CAP * plane_size)
    incoming = lax.all_to_all(outgoing, "block", split_axis=0, concat_axis=0, tiled=True)
    sources = lax.broadcasted_iota(jnp.int32, (block_count, slot_count), 0)
    column_index = jnp.where(view_targets == my_block, sources * CAP + ranks, -1)
    slot_match = (
        view_slots[:, :, None] == jnp.arange(slot_count, dtype=jnp.int32)[None, None, :]
    ).astype(jnp.float32)
    column_match = (column_index[:, :, None] == buffer_slots[None, None, :]).astype(jnp.float32)
    placement = jnp.einsum("sjt,sjc->tc", slot_match, column_match)
    placed = jnp.dot(
        placement.astype(jnp.bfloat16),
        incoming.reshape(block_count * CAP, plane_size),
        preferred_element_type=jnp.float32,
    )
    view_counts = lax.dynamic_index_in_dim(counts_all, my_view, 0, keepdims=False)
    slab_counts = lax.dynamic_slice_in_dim(view_counts, my_block * slot_count, slot_count)
    average = placed / jnp.maximum(slab_counts, 1).astype(jnp.float32)[:, None]
    average = average.reshape(slab_depth, plane_rows, plane_columns)

    def depth_adjoint(one_kernel, one_shift):
        return band_matrix(one_kernel, one_shift, slab_depth + 2 * HALO, slab_depth, -HALO).T

    plane_mask = jnp.repeat((counts_all > 0).astype(jnp.float32), piece_depth, axis=1)
    padded_mask = jnp.pad(plane_mask, ((0, 0), (HALO, HALO)))
    window = lax.dynamic_slice_in_dim(padded_mask, my_block * slab_depth, slab_depth + 2 * HALO, 1)
    adjoint_all = jax.vmap(depth_adjoint)(kernel[:, 0], psf_shift[:, 0])
    weight_depth = jnp.einsum("vze,ve->vz", adjoint_all, window, precision=HIGHEST)
    weight_rows = column_sums(kernel[:, 1], psf_shift[:, 1], plane_rows)
    weight_columns = column_sums(kernel[:, 2], psf_shift[:, 2], plane_columns)
    weight = jnp.einsum(
        "vz,vy,vx->zyx", weight_depth, weight_rows, weight_columns, precision=HIGHEST
    )
    floor_weight = jnp.maximum(weight, 1.0)
    backward_depth = depth_adjoint(own_kernel[0], own_shift[0])
    rim_width = HALO
    forward_depth = band_matrix(
        own_kernel[0], own_shift[0], slab_depth, slab_depth + 2 * HALO, HALO
    )
    estimate = estimate0
    for iteration in range(ITERS):
        extended = with_halo(estimate.astype(jnp.bfloat16), (("block", 0),), rim_width).astype(
            estimate.dtype
        )
        blurred = blur_plane(along_depth(forward_depth, extended), band_rows, band_columns) + offset
        quotient = average / blurred
        partial_value = adjoint_plane(quotient, band_rows, band_columns)
        widened = with_halo(partial_value.astype(jnp.bfloat16), (("block", 0),), HALO).astype(
            partial_value.dtype
        )
        summed = lax.psum(along_depth(backward_depth, widened), "view")
        estimate = estimate * summed / floor_weight
    return estimate


def solution(mesh):
    return jax.shard_map(
        shards,
        mesh=mesh,
        in_specs=(
            P("block", None, None),
            P("view", "block", None, None, None),
            P(),
            P(),
            P(),
            P(),
            P(),
        ),
        out_specs=P("block", None, None),
        check_vma=False,
    )
```

profile of v0, /device:TPU:0, one launch (start us, length us, event | category | flops | bytes accessed | tf_op | source)
XLA Modules:
  0.0 484.7 jit_solution(14688153526528491038)
XLA Ops:
  6.5 0.7 fusion.65
  7.3 2.2 reshape_squeeze.3
  9.5 0.4 convert_reduce_fusion.1
  10.0 3.2 convolution_convert_fusion
  13.2 9.3 %all_to_all.8 = bf16[16,1,131072]{2,1,0:T(2,128)(2,1)} reshape(bf16[32,65536]{1,0:T(8,128)(2,1)} %convolution_convert_fusion) | data formatting | bytes 8388608 | tf_op jit(solution)/shard_map/all_to_all | solution.py:118
  22.5 0.5 broadcast.163
  23.0 26.4 %reduce.9 = bf16[16,131072]{1,0:T(8,128)(2,1)} reduce(bf16[16,1,131072]{2,1,0:T(2,128)(2,1)} %all_to_all.8, bf16[]{:T(256)} %broadcast.163), dimensions={1}, to_apply=%all_to_all.8.reduce_sub_computation | reduce | bytes 8388610 | tf_op jit(solution)/shard_map/all_to_all | solution.py:118
  49.4 6.6 %reshape.238 = bf16[16,2,65536]{2,1,0:T(2,128)(2,1)} reshape(bf16[16,131072]{1,0:T(8,128)(2,1)} %reduce.9) | data formatting | bytes 8388608
  56.0 8.0 %all-to-all-start = ((bf16[16,2,65536]{2,1,0:T(2,128)(2,1)}), bf16[16,2,65536]{2,1,0:T(2,128)(2,1)}, u32[]{:S(2)}, u32[]{:S(2)}) async-start(bf16[16,2,65536]{2,1,0:T(2,128)(2,1)} %reshape.238), calls=%async_computation | async-start | bytes 8388608 | tf_op jit(solution)/shard_map/all_to_all | solution.py:118
  64.2 2.5 convert_element_type.52
  66.7 0.9 fusion.76
  67.6 3.8 collective-permute-start
  71.4 1.5 collective-permute-start.1
  73.1 0.5 fusion.66
  73.7 0.6 fusion.77
  74.3 0.6 subtract_add_fusion.4
  74.9 0.6 subtract_add_fusion.5
  75.5 0.7 subtract_add_fusion.1
  76.8 0.7 add_select_fusion
  77.5 0.7 convert_bitcast_fusion
  78.1 0.6 dynamic_slice.40
  78.8 0.7 eq.147
  79.6 1.2 select_reduce_fusion.1
  80.8 47.3 %collective-permute-done = bf16[13,64,256]{2,1,0:T(8,128)(2,1)S(1)} collective-permute-done((bf16[13,64,256]{2,1,0:T(8,128)(2,1)}, bf16[13,64,256]{2,1,0:T(8,128)(2,1)S(1)}, u32[]{:S(2)}, u32[]{:S(2)}) %collective-permute-start) | collective-permute-done | bytes 426016 | tf_op jit(solution)/shard_map/ppermute | solution.py:22
  128.1 6.4 %collective-permute-done.1 = bf16[13,64,256]{2,1,0:T(8,128)(2,1)S(1)} collective-permute-done((bf16[13,64,256]{2,1,0:T(8,128)(2,1)}, bf16[13,64,256]{2,1,0:T(8,128)(2,1)S(1)}, u32[]{:S(2)}, u32[]{:S(2)}) %collective-permute-start.1) | collective-permute-done | bytes 426016 | tf_op jit(solution)/shard_map/ppermute | solution.py:24
  135.2 3.2 fusion.24
  138.4 6.7 %fusion.10 = f32[64,256,64]{1,2,0:T(8,128)S(1)} fusion(f32[64,64,256]{2,0,1:T(8,128)S(1)} %fusion.24, f32[64,64]{1,0:T(8,128)S(1)} %select_reduce_fusion.2), kind=kOutput, calls=%fused_computation.19 | convolution fusion | flops 805306368 | bytes 8404992 | tf_op jit(solution)/shard_map/yv,zvx->zyx/dot_general | solution.py:59
  145.1 5.2 %fusion.6 = f32[64,64,256]{2,1,0:T(8,128)} fusion(f32[64,256,64]{1,2,0:T(8,128)S(1)} %fusion.10, f32[256,256]{1,0:T(8,128)S(1)} %select_reduce_fusion.1), kind=kOutput, calls=%fused_computation.14 | convolution fusion | flops 3221225472 | bytes 8650752 | tf_op jit(solution)/shard_map/zyv,xv->zyx/dot_general | solution.py:60
  150.3 12.3 %reshape.239 = bf16[16,1,131072]{2,1,0:T(2,128)(2,1)} reshape(bf16[16,2,65536]{2,1,0:T(2,128)(2,1)} %all-to-all-done) | data formatting | bytes 8388608
  162.6 25.8 %reduce.2 = bf16[16,131072]{1,0:T(8,128)(2,1)} reduce(bf16[16,1,131072]{2,1,0:T(2,128)(2,1)} %reshape.239, bf16[]{:T(256)} %constant.97), dimensions={1}, to_apply=%all_to_all.7.reduce_sub_computation | reduce | bytes 8388610 | tf_op jit(solution)/shard_map/all_to_all | solution.py:118
  188.4 4.6 reshape.208
  193.0 5.2 %convolution_divide_fusion = f32[16,65536]{1,0:T(8,128)} fusion(bf16[32,65536]{1,0:T(8,128)(2,1)} %reshape.208, f32[16]{0:T(128)S(1)} %copy-done.11, s32[16,16]{1,0:T(8,128)S(1)} %copy-done.6, s32[16,16]{1,0:T(8,128)S(1)} %copy-done.7), kind=kOutput, calls=%fused_computation.1 | convolution fusion | flops 68432384 | bytes 8390720 | tf_op jit(solution)/shard_map/dot_general | solution.py:126
  198.2 3.9 reshape.209
  202.0 7.4 %fusion.15 = f32[64,256,64]{1,2,0:T(8,128)S(1)} fusion(f32[64,64,256]{2,1,0:T(8,128)} %reshape.209, f32[64,64,256]{2,1,0:T(8,128)} %fusion.6, f32[]{:T(128)} %bitcast.16, f32[64,64]{1,0:T(8,128)S(1)} %select_reduce_fusion.2), kind=kOutput, calls=%fused_computation.24 | convolution fusion | flops 807403520 | bytes 12599300 | tf_op jit(solution)/shard_map/vy,zvx->zyx/dot_general | solution.py:64
  209.5 3.6 fusion.28
  213.2 1.6 collective-permute-start.2
  214.8 1.3 collective-permute-start.3
  216.1 0.6 subtract_add_fusion.6
  216.9 5.9 %collective-permute-done.2 = bf16[13,64,256]{2,1,0:T(8,128)(2,1)S(1)} collective-permute-done((bf16[13,64,256]{2,1,0:T(8,128)(2,1)S(1)}, bf16[13,64,256]{2,1,0:T(8,128)(2,1)S(1)}, u32[]{:S(2)}, u32[]{:S(2)}) %collective-permute-start.2) | collective-permute-done | bytes 426016 | tf_op jit(solution)/shard_map/ppermute | solution.py:22
  222.9 4.1 collective-permute-done.3
  227.6 5.1 %fusion.22 = f32[64,64,256]{2,0,1:T(8,128)} fusion(bf16[64,256,90]{1,0,2:T(8,128)(2,1)S(1)} %slice_bitcast_fusion.2, f32[90,64]{0,1:T(8,128)S(1)} %select_reduce_fusion.4), kind=kOutput, calls=%fused_computation.32 | convolution fusion | flops 1132462080 | bytes 7166464 | tf_op jit(solution)/shard_map/dot_general | solution.py:70
  233.8 1.0 select_reduce_fusion
  234.8 0.5 fusion.78
  235.3 75.8 %all-reduce.4.cloned.1.call-done = f32[64,64,256]{2,0,1:T(8,128)} async-done(((f32[64,64,256]{2,0,1:T(8,128)}), f32[64,64,256]{2,0,1:T(8,128)}) %all-reduce.4.cloned.1.call-update) | async-done | bytes 4194320 | tf_op jit(solution)/shard_map/psum | solution.py:166
  311.1 10.0 %fusion.72 = (bf16[64,64,256]{2,0,1:T(8,128)(2,1)S(1)}, f32[64,64,256]{2,1,0:T(8,128)}) fusion(f32[64,64,256]{2,0,1:T(8,128)} %all-reduce.4.cloned.1.call-done, f32[64,64,256]{2,1,0:T(8,128)} %param.7, f32[8,256]{1,0:T(8,128)S(1)} %select_reduce_fusion.5, f32[8,64]{1,0:T(8,128)S(1)} %bitcast.152, f32[8,64]{0,1:T(8,128)S(1)} %copy.52), kind=kOutput, calls=%fused_computation.131 | convolution fusion | flops 104890368 | bytes 14692352 | tf_op jit(solution)/shard_map/vz,vy,vx->zyx/dot_general | solution.py:146
  321.4 3.4 collective-permute-start.4
  324.8 1.3 collective-permute-start.5
  326.1 8.1 %collective-permute-done.4 = bf16[13,64,256]{2,0,1:T(8,128)(2,1)S(1)} collective-permute-done((bf16[13,64,256]{2,0,1:T(8,128)(2,1)S(1)}, bf16[13,64,256]{2,0,1:T(8,128)(2,1)S(1)}, u32[]{:S(2)}, u32[]{:S(2)}) %collective-permute-start.4) | collective-permute-done | bytes 426016 | tf_op jit(solution)/shard_map/ppermute | solution.py:22
  334.2 4.1 collective-permute-done.5
  338.4 1.9 pad_maximum_fusion
  340.2 1.7 copy.55
  342.3 3.2 fusion.20
  345.5 6.7 %fusion.8 = f32[64,256,64]{1,2,0:T(8,128)S(1)} fusion(f32[64,64,256]{2,0,1:T(8,128)S(1)} %fusion.20, f32[64,64]{1,0:T(8,128)S(1)} %select_reduce_fusion.2), kind=kOutput, calls=%fused_computation.16 | convolution fusion | flops 805306368 | bytes 8404992 | tf_op jit(solution)/shard_map/yv,zvx->zyx/dot_general | solution.py:59
  352.2 4.0 fusion.2
  356.2 5.3 %fusion.12 = f32[64,256,64]{1,2,0:T(8,128)S(1)} fusion(f32[64,64,256]{2,1,0:T(8,128)S(1)} %copy-done, f32[64,64,256]{2,1,0:T(8,128)S(1)} %fusion.2, f32[]{:T(128)} %bitcast.16, f32[64,64]{1,0:T(8,128)S(1)} %select_reduce_fusion.2), kind=kOutput, calls=%fused_computation.21 | convolution fusion | flops 807403520 | bytes 12599300 | tf_op jit(solution)/shard_map/vy,zvx->zyx/dot_general | solution.py:64
  361.5 3.6 fusion.31
  365.2 3.4 collective-permute-start.6
  368.6 1.3 collective-permute-start.7
  369.9 4.9 %collective-permute-done.6 = bf16[13,64,256]{2,1,0:T(8,128)(2,1)S(1)} collective-permute-done((bf16[13,64,256]{2,1,0:T(8,128)(2,1)S(1)}, bf16[13,64,256]{2,1,0:T(8,128)(2,1)S(1)}, u32[]{:S(2)}, u32[]{:S(2)}) %collective-permute-start.6) | collective-permute-done | bytes 426016 | tf_op jit(solution)/shard_map/ppermute | solution.py:22
  374.8 4.1 collective-permute-done.7
  379.5 5.0 %fusion.18 = f32[64,64,256]{2,0,1:T(8,128)} fusion(bf16[64,256,90]{1,0,2:T(8,128)(2,1)S(1)} %slice_bitcast_fusion, f32[90,64]{0,1:T(8,128)S(1)} %select_reduce_fusion.4), kind=kOutput, calls=%fused_computation.28 | convolution fusion | flops 1132462080 | bytes 7166464 | tf_op jit(solution)/shard_map/dot_general | solution.py:70
  384.5 79.3 %all-reduce.6.cloned.1.call-done = f32[64,64,256]{2,0,1:T(8,128)} async-done(((f32[64,64,256]{2,0,1:T(8,128)}), f32[64,64,256]{2,0,1:T(8,128)}) %all-reduce.6.cloned.1.call-update) | async-done | bytes 4194320 | tf_op jit(solution)/shard_map/psum | solution.py:166
  463.8 9.1 %bitcast_divide_fusion = f32[64,64,256]{2,0,1:T(8,128)S(1)} fusion(f32[64,64,256]{2,0,1:T(8,128)} %all-reduce.6.cloned.1.call-done, f32[64,64,256]{2,1,0:T(8,128)} %get-tuple-element.26, f32[64,64,256]{2,0,1:T(8,128)} %all-reduce.4.cloned.1.call-done, f32[64,64,256]{2,1,0:T(8,128)} %param.7), kind=kLoop, calls=%fused_computation.10 | loop fusion | flops 5242880 | bytes 20971520 | tf_op jit(solution)/shard_map/div | solution.py:167
  472.9 4.4 copy.60
  (70 shorter events, 4.8 us)
Async XLA Ops:
  56.0 94.3 %all-to-all-start = ((bf16[16,2,65536]{2,1,0:T(2,128)(2,1)}), bf16[16,2,65536]{2,1,0:T(2,128)(2,1)}, u32[]{:S(2)}, u32[]{:S(2)}) async-start(bf16[16,2,65536]{2,1,0:T(2,128)(2,1)} %reshape.238), calls=%async_computation | async-start | bytes 8388608 | tf_op jit(solution)/shard_map/all_to_all | solution.py:118
  64.1 8.8 %copy-start.1 = (f32[8,3,21]{2,0,1:T(8,128)S(1)}, f32[8,3,21]{2,0,1:T(8,128)}, u32[]{:S(2)}) copy-start(f32[8,3,21]{2,0,1:T(8,128)} %param.12) | copy-start | bytes 6052
  64.1 9.5 %copy-start.8 = (s32[8,3]{0,1:T(4,128)S(1)}, s32[8,3]{0,1:T(4,128)}, u32[]{:S(2)}) copy-start(s32[8,3]{0,1:T(4,128)} %param.11) | copy-start | bytes 292
  64.1 12.3 %copy-start.4 = (s32[8,256,1]{1,2,0:T(1,128)S(1)}, s32[8,256,1]{1,2,0:T(1,128)}, u32[]{:S(2)}) copy-start(s32[8,256,1]{1,2,0:T(1,128)} %param.9) | copy-start | bytes 24580
  64.1 12.3 %copy-start.5 = (s32[8,256]{1,0:T(8,128)S(1)}, s32[8,256]{1,0:T(8,128)}, u32[]{:S(2)}) copy-start(s32[8,256]{1,0:T(8,128)} %param.10) | copy-start | bytes 24580
  64.1 14.0 %copy-start.12 = (f32[8]{0:T(128)S(1)}, f32[8]{0:T(128)}, u32[]{:S(2)}) copy-start(f32[8]{0:T(128)} %param.13) | copy-start | bytes 100
  64.1 247.0 %all-reduce.4.cloned.1.call-start = ((), (), s32[]{:S(2)}) async-start(), calls=%async_computation.1 | async-start | bytes 8388608 | tf_op jit(solution)/shard_map/psum | solution.py:166
  67.6 60.5 %collective-permute-start = (bf16[13,64,256]{2,1,0:T(8,128)(2,1)}, bf16[13,64,256]{2,1,0:T(8,128)(2,1)S(1)}, u32[]{:S(2)}, u32[]{:S(2)}) collective-permute-start(bf16[13,64,256]{2,1,0:T(8,128)(2,1)} %get-tuple-element.11), channel_id=1, source_target_pairs={{0,1},{1,2},{2,3},{3,4},{4,5},{5,6},{6,7},{7,8},{8,9},{9,10},{10,1... | collective-permute-start | bytes 1277960 | tf_op jit(solution)/shard_map/ppermute | solution.py:22
  71.4 63.2 %collective-permute-start.1 = (bf16[13,64,256]{2,1,0:T(8,128)(2,1)}, bf16[13,64,256]{2,1,0:T(8,128)(2,1)S(1)}, u32[]{:S(2)}, u32[]{:S(2)}) collective-permute-start(bf16[13,64,256]{2,1,0:T(8,128)(2,1)} %get-tuple-element.12), channel_id=1, source_target_pairs={{1,0},{2,1},{3,2},{4,3},{5,4},{6,5},{7,6},{8,7},{9,8},{10,9},{11,1... | collective-permute-start | bytes 1277960 | tf_op jit(solution)/shard_map/ppermute | solution.py:24
  73.6 6.0 %copy-start.9 = (f32[21]{0:T(128)}, f32[21]{0:T(128)S(1)}, u32[]{:S(2)}) copy-start(f32[21]{0:T(128)S(1)} %get-tuple-element.15) | copy-start | bytes 256
  76.8 2.7 copy-start.2
  188.4 4.6 copy-start.6
  188.4 4.6 copy-start.7
  188.4 4.6 copy-start.11
  209.5 7.3 %copy-start.10 = (f32[21]{0:T(128)S(1)}, f32[21]{0:T(128)}, u32[]{:S(2)}) copy-start(f32[21]{0:T(128)} %copy-done.9) | copy-start | bytes 256
  213.2 9.7 %collective-permute-start.2 = (bf16[13,64,256]{2,1,0:T(8,128)(2,1)S(1)}, bf16[13,64,256]{2,1,0:T(8,128)(2,1)S(1)}, u32[]{:S(2)}, u32[]{:S(2)}) collective-permute-start(bf16[13,64,256]{2,1,0:T(8,128)(2,1)S(1)} %get-tuple-element.9), channel_id=1, source_target_pairs={{0,1},{1,2},{2,3},{3,4},{4,5},{5,6},{6,7},{7,8},{8,9},{9,10},{10,1... | collective-permute-start | bytes 1277960 | tf_op jit(solution)/shard_map/ppermute | solution.py:22
  214.8 12.2 %collective-permute-start.3 = (bf16[13,64,256]{2,1,0:T(8,128)(2,1)S(1)}, bf16[13,64,256]{2,1,0:T(8,128)(2,1)S(1)}, u32[]{:S(2)}, u32[]{:S(2)}) collective-permute-start(bf16[13,64,256]{2,1,0:T(8,128)(2,1)S(1)} %get-tuple-element.10), channel_id=1, source_target_pairs={{1,0},{2,1},{3,2},{4,3},{5,4},{6,5},{7,6},{8,7},{9,8},{10,9},{11,1... | collective-permute-start | bytes 1277960 | tf_op jit(solution)/shard_map/ppermute | solution.py:24
  227.6 5.6 %copy-start.3 = (s32[8,256]{1,0:T(8,128)S(1)}, s32[8,256]{1,0:T(8,128)}, u32[]{:S(2)}) copy-start(s32[8,256]{1,0:T(8,128)} %copy-done.2) | copy-start | bytes 24580
  232.7 231.1 %all-reduce.6.cloned.1.call-start = ((), (), s32[]{:S(2)}) async-start(), calls=%async_computation.2 | async-start | bytes 8388608 | tf_op jit(solution)/shard_map/psum | solution.py:166
  321.4 12.8 %collective-permute-start.4 = (bf16[13,64,256]{2,0,1:T(8,128)(2,1)S(1)}, bf16[13,64,256]{2,0,1:T(8,128)(2,1)S(1)}, u32[]{:S(2)}, u32[]{:S(2)}) collective-permute-start(bf16[13,64,256]{2,0,1:T(8,128)(2,1)S(1)} %get-tuple-element.7), channel_id=1, source_target_pairs={{0,1},{1,2},{2,3},{3,4},{4,5},{5,6},{6,7},{7,8},{8,9},{9,10},{10,1... | collective-permute-start | bytes 1277960 | tf_op jit(solution)/shard_map/ppermute | solution.py:22
  324.8 13.6 %collective-permute-start.5 = (bf16[13,64,256]{2,0,1:T(8,128)(2,1)S(1)}, bf16[13,64,256]{2,0,1:T(8,128)(2,1)S(1)}, u32[]{:S(2)}, u32[]{:S(2)}) collective-permute-start(bf16[13,64,256]{2,0,1:T(8,128)(2,1)S(1)} %get-tuple-element.8), channel_id=1, source_target_pairs={{1,0},{2,1},{3,2},{4,3},{5,4},{6,5},{7,6},{8,7},{9,8},{10,9},{11,1... | collective-permute-start | bytes 1277960 | tf_op jit(solution)/shard_map/ppermute | solution.py:24
  352.2 4.0 copy-start
  365.2 9.6 %collective-permute-start.6 = (bf16[13,64,256]{2,1,0:T(8,128)(2,1)S(1)}, bf16[13,64,256]{2,1,0:T(8,128)(2,1)S(1)}, u32[]{:S(2)}, u32[]{:S(2)}) collective-permute-start(bf16[13,64,256]{2,1,0:T(8,128)(2,1)S(1)} %get-tuple-element.5), channel_id=1, source_target_pairs={{0,1},{1,2},{2,3},{3,4},{4,5},{5,6},{6,7},{7,8},{8,9},{9,10},{10,1... | collective-permute-start | bytes 1277960 | tf_op jit(solution)/shard_map/ppermute | solution.py:22
  368.6 10.3 %collective-permute-start.7 = (bf16[13,64,256]{2,1,0:T(8,128)(2,1)S(1)}, bf16[13,64,256]{2,1,0:T(8,128)(2,1)S(1)}, u32[]{:S(2)}, u32[]{:S(2)}) collective-permute-start(bf16[13,64,256]{2,1,0:T(8,128)(2,1)S(1)} %get-tuple-element.6), channel_id=1, source_target_pairs={{1,0},{2,1},{3,2},{4,3},{5,4},{6,5},{7,6},{8,7},{9,8},{10,9},{11,1... | collective-permute-start | bytes 1277960 | tf_op jit(solution)/shard_map/ppermute | solution.py:24
Sparse Core Ops, SparseCore 0:
  232.8 78.2 all-reduce.3
  384.6 79.1 all-reduce.5
where the time goes:
time: 492 us; the launch traced here: 485 us
  waiting for transfers between devices  240 us (49%)
  matrix products  78 us (16%)
  other arithmetic  74.7 us (15%)
  local copies, waits for them, and re-layouts  51.6 us (10%)
  starting transfers between devices  25.6 us (5%)
  between operations  14.4 us (3%)
    psum x2, waiting for transfers between devices, shards(): summed = lax.psum(along_depth(backward_depth, widened), 'view')  155 us
    ppermute x4, waiting for transfers between devices, with_halo(): lax.ppermute(tail, axis, [(i, (i + 1) % count) for i in range(ends)])  66.3 us
    all_to_all x2, other arithmetic, shards(): lax.all_to_all(outgoing, 'block', split_axis=0, concat_axis=0, tiled=True)  52.2 us
    unnamed x28, local copies, waits for them, and re-layouts  19 us
    ppermute x4, waiting for transfers between devices, with_halo(): lax.ppermute(head, axis, [((i + 1) % count, i) for i in range(ends)])  18.9 us
    dot_general x4, matrix products, along_depth(): result = jnp.dot(matrix, flattened, precision=HIGHEST)  16.6 us
    dot_general x2, matrix products, blur_plane(): along_rows = jnp.einsum('yv,zvx->zyx', band_rows, volume, precision=HIGHEST)  13.3 us
    dot_general x2, matrix products, adjoint_plane(): along_rows = jnp.einsum('vy,zvx->zyx', band_rows, volume, precision=HIGHEST)  12.7 us
  transfers between devices with their start and end apart: 11, of which 10 were waited for; matrix products, arithmetic and copies ran while one was open for 6% of the time, Pallas kernels for 0%

commit v1 on v0

v1 whole, which is shorter than its diff:
```python
import jax
import jax.numpy as jnp
from jax import lax
from jax.experimental import pallas as pl
from jax.experimental.pallas import tpu as pltpu
from jax.sharding import PartitionSpec as P

CAP = 2
TAPS = 21
HALO = 16
VIEWS = 8
SLOTS = 16
NY = 64
PART = 32
ROWS = 256

F32 = jnp.float32
BF16 = jnp.bfloat16
I32 = jnp.int32


def lane_block(shape):
    return lax.broadcasted_iota(I32, shape, len(shape) - 1) // PART


def rotate(value, amount):
    return pltpu.roll(value, amount % 128, value.ndim - 1)


def digit_swap(shape):
    row = lax.broadcasted_iota(I32, shape, 0)
    column = lax.broadcasted_iota(I32, shape, 1)
    target = ((row // PART) % 4) * 128 + (row // 128) * PART + row % PART
    return jnp.where(column == target, 1.0, 0.0).astype(BF16)


def vmem(count):
    return [pl.BlockSpec(memory_space=pltpu.VMEM)] * count


def smem(count):
    return [pl.BlockSpec(memory_space=pltpu.SMEM)] * count


def band_kernel(taps_ref, shift_ref, ky_ref, kyt_ref, kx_ref, kxt_ref, bzf_ref, bza_ref):
    radius = (TAPS - 1) // 2

    def fill(difference, view, axis):
        result = jnp.zeros(difference.shape, F32)
        for tap in range(TAPS):
            result = jnp.where(difference == tap, taps_ref[(view * 3 + axis) * TAPS + tap], result)
        return result

    def one_view(view, carry):
        shift_y = shift_ref[view * 3 + 1]
        shift_x = shift_ref[view * 3 + 2]
        row = lax.broadcasted_iota(I32, (NY, ROWS), 0)
        lane = lax.broadcasted_iota(I32, (NY, ROWS), 1)
        offset = lane % NY - row
        forward = fill(offset - shift_y + radius, view, 1)
        backward = fill(-offset - shift_y + radius, view, 1)
        for block in range(4):
            mine = lane // NY == block
            ky_ref[view, block * NY:(block + 1) * NY, :] = jnp.where(mine, forward, 0.0).astype(BF16)
            kyt_ref[view, block * NY:(block + 1) * NY, :] = jnp.where(mine, backward, 0.0).astype(BF16)
        row = lax.broadcasted_iota(I32, (PART, 128), 0)
        lane = lax.broadcasted_iota(I32, (PART, 128), 1)
        for half in range(2):
            base = fill(half * PART + row - (lane % PART + HALO) - shift_x + radius, view, 2)
            for block in range(4):
                first = half * 128 + block * PART
                kx_ref[view, first:first + PART, :] = jnp.where(lane // PART == block, base, 0.0).astype(BF16)
            base = fill(half * PART + lane % PART - (row + HALO) - shift_x + radius, view, 2)
            for block in range(4):
                kxt_ref[view, block * PART:(block + 1) * PART, half * 128:(half + 1) * 128] = jnp.where(
                    lane // PART == block, base, 0.0).astype(BF16)
        row = lax.broadcasted_iota(I32, (16, 48), 0)
        lane = lax.broadcasted_iota(I32, (16, 48), 1)
        bzf_ref[view] = fill(lane - 16 - row - shift_ref[view * 3] + radius, view, 0).astype(BF16)
        return carry

    lax.fori_loop(0, VIEWS, one_view, 0)
    row = lax.broadcasted_iota(I32, (48, 128), 0)
    lane = lax.broadcasted_iota(I32, (48, 128), 1)
    total = jnp.zeros((48, 128), F32)
    for view in range(VIEWS):
        band = fill(row - 16 - lane % 16 - shift_ref[view * 3] + radius, view, 0)
        total = jnp.where(lane // 16 == view, band, total)
    bza_ref[...] = total.astype(BF16)


def build_bands(taps, shifts):
    return pl.pallas_call(
        band_kernel,
        out_shape=(
            jax.ShapeDtypeStruct((VIEWS, ROWS, ROWS), BF16),
            jax.ShapeDtypeStruct((VIEWS, ROWS, ROWS), BF16),
            jax.ShapeDtypeStruct((VIEWS, ROWS, 128), BF16),
            jax.ShapeDtypeStruct((VIEWS, 128, ROWS), BF16),
            jax.ShapeDtypeStruct((VIEWS, 16, 48), BF16),
            jax.ShapeDtypeStruct((48, 128), BF16),
        ),
        in_specs=smem(2),
        out_specs=tuple(vmem(6)),
        name="bands",
    )(taps, shifts)


def pack_kernel(target_ref, pieces_ref, out_ref, swap_ref):
    swap_ref[...] = digit_swap((512, 512))
    count = pieces_ref.shape[0]

    def one_piece(piece, carry):
        target = target_ref[piece]
        rank = jnp.int32(0)
        for other in range(count):
            rank = rank + jnp.where((target_ref[other] == target) & (other < piece), 1, 0)
        slot = target * CAP + rank
        for half in range(2):
            planes = [pieces_ref[piece, q, :, half * 128:(half + 1) * 128] for q in range(4)]
            mixed = jnp.dot(jnp.concatenate(planes, axis=1), swap_ref[...], preferred_element_type=F32)
            for part in range(4):
                out_ref[half * 4 + part, slot] = mixed[:, part * 128:(part + 1) * 128].astype(BF16)
        return carry

    lax.fori_loop(0, count, one_piece, 0)


def pack_pieces(targets, pieces, block_count):
    return pl.pallas_call(
        pack_kernel,
        out_shape=jax.ShapeDtypeStruct((VIEWS, block_count * CAP, NY, 128), BF16),
        in_specs=smem(1) + vmem(1),
        out_specs=vmem(1)[0],
        scratch_shapes=[pltpu.VMEM((512, 512), BF16)],
        name="pack",
    )(targets, pieces)


def window_kernel(index_ref, estimate_ref, main_ref, low_ref, high_ref):
    part = index_ref[0]
    block = lane_block((NY, 128))
    lane = lax.broadcasted_iota(I32, (NY, 128), 1) % PART

    def one_plane(j, carry):
        for half in range(2):
            result = jnp.zeros((NY, 128), F32)
            for h in range(4):
                plane = estimate_ref[h * 16 + j]
                amount = (16 - PART * part - PART * half + PART * h + 512) % 256
                moved = pltpu.roll(plane, amount, 1)[:, :128]
                result = jnp.where(block == h, moved, result)
            column = (part + half) * PART - HALO + lane
            result = jnp.where((column >= 0) & (column < 256), result, 0.0)
            main_ref[half, pl.ds(j, NY, stride=16), :] = result
        return carry

    lax.fori_loop(0, 16, one_plane, 0)
    block = lane_block((16, 128))

    def pack_ends(y, carry):
        rows = pl.ds(y * 16, 16)
        left = main_ref[0, rows, :]
        right = main_ref[1, rows, :]
        low_ref[y] = jnp.where(block == 0, left, rotate(right, 32)).astype(BF16)
        high_ref[y] = jnp.where(block == 3, right, rotate(left, 96)).astype(BF16)
        return carry

    lax.fori_loop(0, NY, pack_ends, 0)


def window_estimate(index, estimate):
    return pl.pallas_call(
        window_kernel,
        out_shape=(
            jax.ShapeDtypeStruct((2, NY * 16, 128), F32),
            jax.ShapeDtypeStruct((NY, 16, 128), BF16),
            jax.ShapeDtypeStruct((NY, 16, 128), BF16),
        ),
        in_specs=smem(1) + vmem(1),
        out_specs=tuple(vmem(3)),
        name="window",
    )(index, estimate)


def tail_kernel(from_low_ref, from_high_ref, tail_ref):
    block = lane_block((16, 128))

    def one_row(y, carry):
        low = from_low_ref[y].astype(F32)
        high = from_high_ref[y].astype(F32)
        result = jnp.where(block == 0, rotate(low, 64), high)
        result = jnp.where(block == 1, rotate(high, 32), result)
        result = jnp.where(block == 2, rotate(low, 96), result)
        result = jnp.where(block == 3, rotate(high, 64), result)
        tail_ref[y] = result
        return carry

    lax.fori_loop(0, NY, one_row, 0)


def build_tail(from_low, from_high):
    return pl.pallas_call(
        tail_kernel,
        out_shape=jax.ShapeDtypeStruct((NY, 16, 128), F32),
        in_specs=vmem(2),
        out_specs=vmem(1)[0],
        name="tail",
    )(from_low, from_high)


def weight_kernel(rows_ref, main_ref, tail_ref, out_main_ref, out_tail_ref):
    def one_row(y, carry):
        for half in range(2):
            total = jnp.zeros((16, 128), F32)
            for view in range(VIEWS):
                total = total + rows_ref[view * NY + y] * main_ref[view, half]
            out_main_ref[half, pl.ds(y * 16, 16), :] = 1.0 / jnp.maximum(total, 1.0)
        total = jnp.zeros((16, 128), F32)
        for view in range(VIEWS):
            total = total + rows_ref[view * NY + y] * tail_ref[view]
        out_tail_ref[y] = 1.0 / jnp.maximum(total, 1.0)
        return carry

    lax.fori_loop(0, NY, one_row, 0)


def build_weights(rows, main, tail):
    return pl.pallas_call(
        weight_kernel,
        out_shape=(
            jax.ShapeDtypeStruct((2, NY * 16, 128), F32),
            jax.ShapeDtypeStruct((NY, 16, 128), F32),
        ),
        in_specs=smem(1) + vmem(2),
        out_specs=tuple(vmem(2)),
        name="weights",
    )(rows, main, tail)


def forward_kernel(main_ref, tail_ref, bzf_ref, ky_ref, kx_ref, out_ref, left_ref, right_ref):
    block = lane_block((16, 128))

    def along_z(y, carry):
        rows = pl.ds(y * 16, 16)
        left = main_ref[0, rows, :]
        right = main_ref[1, rows, :]
        tail = tail_ref[y]
        turned = rotate(tail, 64)
        lower = jnp.concatenate([jnp.where(block == 0, tail, rotate(left, 32)),
                                 jnp.where(block == 0, turned, rotate(right, 32))], axis=1)
        upper = jnp.concatenate([jnp.where(block == 3, turned, rotate(left, 96)),
                                 jnp.where(block == 3, tail, rotate(right, 96))], axis=1)
        stacked = jnp.concatenate([lower, jnp.concatenate([left, right], axis=1), upper], axis=0).astype(BF16)
        blurred = jnp.dot(bzf_ref[...], stacked, preferred_element_type=F32)
        left_ref[pl.ds(y, 128, stride=NY), :] = blurred[:, :128]
        right_ref[pl.ds(y, 128, stride=NY), :] = blurred[:, 128:]
        return carry

    lax.fori_loop(0, NY, along_z, 0, unroll=4)

    def in_plane(group, carry):
        rows = pl.ds(pl.multiple_of(group * ROWS, ROWS), ROWS)
        view = group // 4
        volume = jnp.concatenate([left_ref[rows, :], right_ref[rows, :]], axis=1).astype(BF16)
        along_y = jnp.dot(ky_ref[view], volume, preferred_element_type=F32).astype(BF16)
        out_ref[rows, :] = jnp.dot(along_y, kx_ref[view], preferred_element_type=F32)
        return carry

    lax.fori_loop(0, VIEWS * 4, in_plane, 0, unroll=2)


def forward(main, tail, bzf, ky, kx):
    return pl.pallas_call(
        forward_kernel,
        out_shape=jax.ShapeDtypeStruct((VIEWS * 1024, 128), F32),
        in_specs=vmem(5),
        out_specs=vmem(1)[0],
        scratch_shapes=[pltpu.VMEM((VIEWS * 1024, 128), F32)] * 2,
        name="forward",
    )(main, tail, bzf, ky, kx)


def adjoint_body(average_of, offset_ref, blurred_ref, bza_ref, kyt_ref, kxt_ref, main_ref, tail_ref, to_left_ref,
                 to_right_ref, left_ref, right_ref):
    def in_plane(group, carry):
        rows = pl.ds(pl.multiple_of(group * ROWS, ROWS), ROWS)
        view = group // 4
        quotient = (average_of(group, rows) / (blurred_ref[rows, :] + offset_ref[view])).astype(BF16)
        along_x = jnp.dot(quotient, kxt_ref[view], preferred_element_type=F32).astype(BF16)
        along_y = jnp.dot(kyt_ref[view], along_x, preferred_element_type=F32)
        left_ref[rows, :] = along_y[:, :128]
        right_ref[rows, :] = along_y[:, 128:]
        return carry

    lax.fori_loop(0, VIEWS * 4, in_plane, 0, unroll=2)
    block = lane_block((16, 128))
    low_half = block < 2

    def along_z(y):
        volume = jnp.concatenate([left_ref[pl.ds(y, 128, stride=NY), :],
                                  right_ref[pl.ds(y, 128, stride=NY), :]], axis=1).astype(BF16)
        summed = jnp.dot(bza_ref[...], volume, preferred_element_type=F32)
        mains = []
        for half in range(2):
            lanes = slice(half * 128, (half + 1) * 128)
            lower = jnp.where(block < 3, rotate(summed[:16, lanes], 96), 0.0)
            upper = jnp.where(block > 0, rotate(summed[32:, lanes], 32), 0.0)
            mains.append(summed[16:32, lanes] + lower + upper)
        tail = jnp.where(block == 0, summed[:16, :128], summed[32:, 128:])
        tail = jnp.where(block == 1, rotate(summed[32:, :128], 64), tail)
        tail = jnp.where(block == 2, rotate(summed[:16, 128:], 64), tail)
        return mains, tail

    def pair(y, carry):
        tails = []
        for row in (y, y + NY // 2):
            mains, tail = along_z(row)
            for half in range(2):
                main_ref[half, pl.ds(row * 16, 16), :] = mains[half]
            tail_ref[row] = tail
            to_left_ref[row] = mains[0].astype(BF16)
            to_right_ref[row] = mains[1].astype(BF16)
            tails.append(tail)
        to_left_ref[NY + y] = jnp.where(low_half, tails[0], rotate(tails[1], 64)).astype(BF16)
        to_right_ref[NY + y] = jnp.where(low_half, rotate(tails[0], 64), tails[1]).astype(BF16)
        return carry

    lax.fori_loop(0, NY // 2, pair, 0, unroll=2)


def first_adjoint_kernel(start_ref, order_ref, inverse_ref, offset_ref, incoming_ref, blurred_ref, bza_ref, kyt_ref,
                         kxt_ref, main_ref, tail_ref, to_left_ref, to_right_ref, average_ref, left_ref, right_ref,
                         swap_ref):
    swap_ref[...] = digit_swap((512, 512))

    def average_of(group, rows):
        view = group // 4
        remainder = group % 4
        parts = []
        for h in range(4):
            slot = view * SLOTS + h * 4 + remainder

            def add(position, total):
                return total + incoming_ref[view, order_ref[view * 32 + position]].astype(F32)

            total = lax.fori_loop(start_ref[slot + view], start_ref[slot + view + 1], add, jnp.zeros((NY, 128), F32))
            parts.append((total * inverse_ref[slot]).astype(BF16))
        mixed = jnp.dot(jnp.concatenate(parts, axis=1), swap_ref[...], preferred_element_type=F32)
        average = jnp.concatenate([mixed[:, q * 128:(q + 1) * 128] for q in range(4)], axis=0)
        average_ref[rows, :] = average.astype(BF16)
        return average

    adjoint_body(average_of, offset_ref, blurred_ref, bza_ref, kyt_ref, kxt_ref, main_ref, tail_ref, to_left_ref,
                 to_right_ref, left_ref, right_ref)


def next_adjoint_kernel(offset_ref, average_ref, blurred_ref, bza_ref, kyt_ref, kxt_ref, main_ref, tail_ref,
                        to_left_ref, to_right_ref, left_ref, right_ref):
    def average_of(group, rows):
        return average_ref[rows, :].astype(F32)

    adjoint_body(average_of, offset_ref, blurred_ref, bza_ref, kyt_ref, kxt_ref, main_ref, tail_ref, to_left_ref,
                 to_right_ref, left_ref, right_ref)


PARTIAL_SHAPES = (
    jax.ShapeDtypeStruct((2, NY * 16, 128), F32),
    jax.ShapeDtypeStruct((NY, 16, 128), F32),
    jax.ShapeDtypeStruct((NY + NY // 2, 16, 128), BF16),
    jax.ShapeDtypeStruct((NY + NY // 2, 16, 128), BF16),
)


def first_adjoint(start, order, inverse, offset, incoming, blurred, bza, kyt, kxt):
    return pl.pallas_call(
        first_adjoint_kernel,
        out_shape=PARTIAL_SHAPES + (jax.ShapeDtypeStruct((VIEWS * 1024, 128), BF16),),
        in_specs=smem(4) + vmem(5),
        out_specs=tuple(vmem(5)),
        scratch_shapes=[pltpu.VMEM((VIEWS * 1024, 128), F32)] * 2 + [pltpu.VMEM((512, 512), BF16)],
        name="first_adjoint",
    )(start, order, inverse, offset, incoming, blurred, bza, kyt, kxt)


def next_adjoint(offset, average, blurred, bza, kyt, kxt):
    return pl.pallas_call(
        next_adjoint_kernel,
        out_shape=PARTIAL_SHAPES,
        in_specs=smem(1) + vmem(5),
        out_specs=tuple(vmem(4)),
        scratch_shapes=[pltpu.VMEM((VIEWS * 1024, 128), F32)] * 2,
        name="next_adjoint",
    )(offset, average, blurred, bza, kyt, kxt)


def join_columns_kernel(main_ref, tail_ref, from_left_ref, from_right_ref, out_main_ref, out_tail_ref, low_ref,
                        high_ref):
    block = lane_block((16, 128))
    low_half = block < 2

    def pair(y, carry):
        packed_left = from_left_ref[NY + y].astype(F32)
        packed_right = from_right_ref[NY + y].astype(F32)
        for second, row in enumerate((y, y + NY // 2)):
            rows = pl.ds(row * 16, 16)
            left = main_ref[0, rows, :] + from_left_ref[row].astype(F32)
            right = main_ref[1, rows, :] + from_right_ref[row].astype(F32)
            if second:
                extra = jnp.where(low_half, rotate(packed_left, 64), packed_right)
            else:
                extra = jnp.where(low_half, packed_left, rotate(packed_right, 64))
            tail = tail_ref[row] + extra
            out_main_ref[0, rows, :] = left
            out_main_ref[1, rows, :] = right
            out_tail_ref[row] = tail
            low = jnp.where(block == 1, rotate(left, 32), tail)
            low = jnp.where(block == 3, rotate(right, 96), low)
            high = jnp.where(block == 0, rotate(left, 32), tail)
            high = jnp.where(block == 2, rotate(right, 96), high)
            low_ref[row] = low.astype(BF16)
            high_ref[row] = high.astype(BF16)
        return carry

    lax.fori_loop(0, NY // 2, pair, 0, unroll=2)


def join_columns(main, tail, from_left, from_right):
    return pl.pallas_call(
        join_columns_kernel,
        out_shape=(
            jax.ShapeDtypeStruct((2, NY * 16, 128), F32),
            jax.ShapeDtypeStruct((NY, 16, 128), F32),
            jax.ShapeDtypeStruct((NY, 16, 128), BF16),
            jax.ShapeDtypeStruct((NY, 16, 128), BF16),
        ),
        in_specs=vmem(4),
        out_specs=tuple(vmem(4)),
        name="join_columns",
    )(main, tail, from_left, from_right)


def joined_planes(y, block, main_ref, tail_ref, from_low_ref, from_high_ref):
    rows = pl.ds(y * 16, 16)
    low = from_low_ref[y].astype(F32)
    high = from_high_ref[y].astype(F32)
    left = main_ref[0, rows, :]
    left = left + jnp.where(block == 0, rotate(low, 96), 0.0) + jnp.where(block == 3, rotate(high, 96), 0.0)
    right = main_ref[1, rows, :]
    right = right + jnp.where(block == 0, rotate(low, 32), 0.0) + jnp.where(block == 3, rotate(high, 32), 0.0)
    tail = tail_ref[y] + jnp.where(block % 2 == 0, low, high)
    return left, right, tail


def update_kernel(main_ref, tail_ref, from_low_ref, from_high_ref, estimate_main_ref, estimate_tail_ref,
                  scale_main_ref, scale_tail_ref, out_main_ref, out_tail_ref):
    block = lane_block((16, 128))

    def one_row(y, carry):
        rows = pl.ds(y * 16, 16)
        left, right, tail = joined_planes(y, block, main_ref, tail_ref, from_low_ref, from_high_ref)
        out_main_ref[0, rows, :] = estimate_main_ref[0, rows, :] * left * scale_main_ref[0, rows, :]
        out_main_ref[1, rows, :] = estimate_main_ref[1, rows, :] * right * scale_main_ref[1, rows, :]
        out_tail_ref[y] = estimate_tail_ref[y] * tail * scale_tail_ref[y]
        return carry

    lax.fori_loop(0, NY, one_row, 0, unroll=4)


def update(main, tail, from_low, from_high, estimate_main, estimate_tail, scale_main, scale_tail):
    return pl.pallas_call(
        update_kernel,
        out_shape=(
            jax.ShapeDtypeStruct((2, NY * 16, 128), F32),
            jax.ShapeDtypeStruct((NY, 16, 128), F32),
        ),
        in_specs=vmem(8),
        out_specs=tuple(vmem(2)),
        name="update",
    )(main, tail, from_low, from_high, estimate_main, estimate_tail, scale_main, scale_tail)


def finish_kernel(main_ref, tail_ref, from_low_ref, from_high_ref, estimate_ref, scale_ref, out_ref):
    block = lane_block((16, 128))
    lane = lax.broadcasted_iota(I32, (16, 128), 1) % PART

    def one_row(y, carry):
        rows = pl.ds(y * 16, 16)
        left, right, _ = joined_planes(y, block, main_ref, tail_ref, from_low_ref, from_high_ref)
        left = estimate_ref[0, rows, :] * left * scale_ref[0, rows, :]
        right = estimate_ref[1, rows, :] * right * scale_ref[1, rows, :]
        out_ref[rows, :] = jnp.where(lane < HALO, rotate(left, 112), rotate(right, 16))
        return carry

    lax.fori_loop(0, NY, one_row, 0, unroll=4)


def finish(main, tail, from_low, from_high, estimate, scale):
    return pl.pallas_call(
        finish_kernel,
        out_shape=jax.ShapeDtypeStruct((NY * 16, 128), F32),
        in_specs=vmem(6),
        out_specs=vmem(1)[0],
        name="finish",
    )(main, tail, from_low, from_high, estimate, scale)


def assemble_kernel(index_ref, *refs):
    chunk_refs, out_ref, buffer_ref = refs[:8], refs[8], refs[9]
    part = index_ref[0]
    for step in range(4):
        chip = (part // 2 + step) % 4
        buffer_ref[chip * 2 + part % 2] = chunk_refs[step][...]
        buffer_ref[chip * 2 + 1 - part % 2] = chunk_refs[4 + step][...]
    block = lane_block((NY, 128))

    def one_plane(j, carry):
        for half in range(2):
            chunks = [buffer_ref[half * 4 + k, pl.ds(j, NY, stride=16), :] for k in range(4)]
            for h in range(4):
                result = rotate(chunks[0], -PART * h)
                for k in range(1, 4):
                    result = jnp.where(block == k, rotate(chunks[k], PART * (k - h)), result)
                out_ref[h * 16 + j, :, half * 128:(half + 1) * 128] = result
        return carry

    lax.fori_loop(0, 16, one_plane, 0)


def assemble(index, chunks):
    return pl.pallas_call(
        assemble_kernel,
        out_shape=jax.ShapeDtypeStruct((64, NY, 256), F32),
        in_specs=smem(1) + vmem(8),
        out_specs=vmem(1)[0],
        scratch_shapes=[pltpu.VMEM((VIEWS, NY * 16, 128), F32)],
        name="assemble",
    )(index, *chunks)


def to_neighbours(upward, downward, axis):
    count = lax.axis_size(axis)
    from_low = lax.ppermute(upward, axis, [(i, i + 1) for i in range(count - 1)])
    from_high = lax.ppermute(downward, axis, [(i + 1, i) for i in range(count - 1)])
    return from_low, from_high


def gather_parts(own):
    parts = [own] + [
        lax.ppermute(own, "view", [((i + 2 * step) % VIEWS, i) for i in range(VIEWS)]) for step in (1, 3, 2)
    ]
    parts = [parts[0], parts[1], parts[3], parts[2]]
    return parts, [lax.ppermute(part, "view", [(i, i ^ 1) for i in range(VIEWS)]) for part in parts]


def column_sums(kernel, shift, positions, length):
    radius = (TAPS - 1) // 2
    source = (positions[None, :, None] - shift[:, None, None]
              - jnp.arange(TAPS, dtype=I32)[None, None, :] + radius)
    inside = (source >= 0) & (source < length)
    return jnp.sum(jnp.where(inside, kernel[:, None, :], 0.0), axis=2)


def shards(estimate0, pieces, dest_block, slot_index, psf_shift, psf_taps, background):
    block_count = lax.axis_size("block")
    my_view = lax.axis_index("view")
    my_block = lax.axis_index("block")
    targets = dest_block[:, :, 0].reshape(VIEWS, block_count, SLOTS)
    slots = slot_index.reshape(VIEWS, block_count, SLOTS)

    own_targets = lax.dynamic_slice(targets, (my_view, my_block, 0), (1, 1, SLOTS)).reshape(SLOTS)
    outgoing = pack_pieces(own_targets, pieces[0], block_count)
    incoming = lax.all_to_all(
        outgoing.reshape(VIEWS * block_count, CAP, NY, 128), ("view", "block"), 0, 0, tiled=True
    ).reshape(VIEWS, block_count * CAP, NY, 128)

    kernel = psf_taps / jnp.sum(psf_taps, axis=2, keepdims=True)
    ky, kyt, kx, kxt, bzf, bza = build_bands(kernel.reshape(-1), psf_shift.reshape(-1))
    bzf = bzf.reshape(VIEWS * 16, 48)

    index = my_view.reshape(1).astype(I32)
    main, low, high = window_estimate(index, estimate0)
    from_low, from_high = to_neighbours(high, low, "block")
    tail = build_tail(from_low, from_high)
    blurred = forward(main, tail, bzf, ky, kx)

    earlier = jnp.tril(jnp.ones((SLOTS, SLOTS), jnp.bool_), -1)
    same = (targets[:, :, :, None] == targets[:, :, None, :]) & earlier[None, None]
    ranks = jnp.sum(same.astype(I32), axis=3)
    mine = targets == my_block
    received = jnp.arange(CAP, dtype=I32)
    slot_of = jnp.sum(
        jnp.where(mine[..., None] & (ranks[..., None] == received), slots[..., None] + 1, 0), axis=2
    ).reshape(VIEWS, block_count * CAP) - 1
    slot_ids = jnp.arange(SLOTS, dtype=I32)
    hits = slot_of[:, :, None] == slot_ids
    counts = jnp.sum(hits.astype(I32), axis=1)
    start = jnp.sum(jnp.where((slot_of[:, :, None] >= 0)
                              & (slot_of[:, :, None] < jnp.arange(SLOTS + 1, dtype=I32)), 1, 0), axis=1)
    number = jnp.arange(block_count * CAP, dtype=I32)
    before = (slot_of[:, None, :] >= 0) & (
        (slot_of[:, None, :] < slot_of[:, :, None])
        | ((slot_of[:, None, :] == slot_of[:, :, None]) & (number[None, None, :] < number[None, :, None]))
    )
    position = jnp.where(slot_of >= 0, jnp.sum(before.astype(I32), axis=2), -1)
    order = jnp.sum(jnp.where(position[:, :, None] == number, number[None, :, None], 0), axis=1)
    inverse = 1.0 / jnp.maximum(counts, 1).astype(F32)

    global_slot = (targets * SLOTS + slots).reshape(VIEWS, block_count * SLOTS)
    all_slots = jnp.arange(block_count * SLOTS, dtype=I32)
    occupied = jnp.any(global_slot[:, :, None] == all_slots, axis=1)
    mask = jnp.repeat(occupied.astype(F32), 4, axis=1)
    padded = jnp.pad(mask, ((0, 0), (2 * HALO, 2 * HALO)))
    window = lax.dynamic_slice_in_dim(padded, my_block * 64, 128, 1)
    depth = lax.broadcasted_iota(I32, (96, 128), 0) + HALO - lax.broadcasted_iota(I32, (96, 128), 1)
    tap = depth[None] - psf_shift[:, 0, None, None] + (TAPS - 1) // 2
    weight_depth = jnp.zeros((VIEWS, 96), F32)
    band = jnp.zeros((VIEWS, 96, 128), F32)
    for j in range(TAPS):
        band = jnp.where(tap == j, kernel[:, 0, j, None, None], band)
    weight_depth = jnp.sum(band * window[:, None, :], axis=2)
    weight_rows = column_sums(kernel[:, 1], psf_shift[:, 1], jnp.arange(NY, dtype=I32), NY)
    columns = my_view * PART - HALO + jnp.arange(2 * PART, dtype=I32)
    weight_columns = column_sums(kernel[:, 2], psf_shift[:, 2], columns, 256).reshape(VIEWS, 2, PART)
    by_group = weight_depth.reshape(VIEWS, 6, 16)
    planes = by_group[:, :, :, None, None] * weight_columns[:, None, None, :, :]
    planes = planes.transpose(0, 3, 2, 1, 4)
    weight_main = planes[:, :, :, 1:5].reshape(VIEWS, 2, 16, 128)
    weight_tail = jnp.stack([planes[:, :, :, 0], planes[:, :, :, 5]], axis=3)
    weight_tail = weight_tail.transpose(0, 2, 1, 3, 4).reshape(VIEWS, 16, 128)
    scale_main, scale_tail = build_weights(weight_rows.reshape(-1), weight_main, weight_tail)

    part_main, part_tail, to_left, to_right, average = first_adjoint(
        start.reshape(-1), order.reshape(-1), inverse.reshape(-1), background, incoming, blurred, bza, kyt, kxt)
    from_left, from_right = to_neighbours(to_right, to_left, "view")
    part_main, part_tail, low, high = join_columns(part_main, part_tail, from_left, from_right)
    from_low, from_high = to_neighbours(high, low, "block")
    main, tail = update(part_main, part_tail, from_low, from_high, main, tail, scale_main, scale_tail)

    blurred = forward(main, tail, bzf, ky, kx)
    part_main, part_tail, to_left, to_right = next_adjoint(background, average, blurred, bza, kyt, kxt)
    from_left, from_right = to_neighbours(to_right, to_left, "view")
    part_main, part_tail, low, high = join_columns(part_main, part_tail, from_left, from_right)
    from_low, from_high = to_neighbours(high, low, "block")
    own = finish(part_main, part_tail, from_low, from_high, main, scale_main)

    mine, partners = gather_parts(own)
    return assemble(index, mine + partners)


def solution(mesh):
    return jax.shard_map(
        shards,
        mesh=mesh,
        in_specs=(
            P("block", None, None),
            P("view", "block", None, None, None),
            P(),
            P(),
            P(),
            P(),
            P(),
        ),
        out_specs=P("block", None, None),
        check_vma=False,
    )
```

time: 492 us -> 289 us (0.59)
  the two profiles are of different devices: /device:TPU:0 before, /device:TPU:15 now
where the time goes in v1:
time: 289 us; the launch traced here: 288 us
  Pallas kernels  171 us (59%)
  waiting for transfers between devices  52 us (18%)
  starting transfers between devices  45.6 us (16%)
  local copies, waits for them, and re-layouts  13.1 us (5%)
  other arithmetic  6.2 us (2%)
    pallas_call x2, Pallas kernels, forward(): pl.pallas_call(forward_kernel, out_shape=jax.ShapeDtypeStruct((VIEWS * 10...  42.4 us
    pallas_call x1, Pallas kernels, first_adjoint(): pl.pallas_call(first_adjoint_kernel, out_shape=PARTIAL_SHAPES + (jax.Shap...  38.5 us
    pallas_call x1, Pallas kernels, next_adjoint(): pl.pallas_call(next_adjoint_kernel, out_shape=PARTIAL_SHAPES, in_specs=sm...  24.5 us
    ppermute x3, waiting for transfers between devices, gather_parts(): lax.ppermute(own, 'view', [((i + 2 * step) % VIEWS, i) for i in range(VIE...  20.3 us
    ppermute x5, waiting for transfers between devices, to_neighbours(): lax.ppermute(downward, axis, [(i + 1, i) for i in range(count - 1)])  15.9 us
    ppermute x5, starting transfers between devices, to_neighbours(): lax.ppermute(upward, axis, [(i, i + 1) for i in range(count - 1)])  15.6 us
    pallas_call x1, Pallas kernels, window_estimate(): pl.pallas_call(window_kernel, out_shape=(jax.ShapeDtypeStruct((2, NY * 16...  11.6 us
    all_to_all x1, starting transfers between devices, shards(): lax.all_to_all(outgoing.reshape(VIEWS * block_count, CAP, NY, 128), ('vie...  11.6 us
  transfers between devices with their start and end apart: 18, of which 12 were waited for; matrix products, arithmetic and copies ran while one was open for 5% of the time, Pallas kernels for 16%

profile of v1, /device:TPU:15, one launch (start us, length us, event | category | flops | bytes accessed | tf_op | source)
XLA Modules:
  0.0 287.9 jit_solution(7966321870641101077)
XLA Ops:
  0.0 11.6 %window.1 = (f32[2,1024,128]{2,1,0:T(8,128)}, bf16[64,16,128]{2,1,0:T(8,128)(2,1)}, bf16[64,16,128]{2,1,0:T(8,128)(2,1)}) custom-call(s32[1]{0:T(128)} %bitcast.index_ref, f32[64,64,256]{2,1,0:T(8,128)} %estimate_ref.1), custom_call_target="tpu_custom_call" | custom-call | tf_op jit(solution)/shard_map/window/pallas_call | solution.py:173
  11.6 3.4 %collective-permute-start = (bf16[64,16,128]{2,1,0:T(8,128)(2,1)}, bf16[64,16,128]{2,1,0:T(8,128)(2,1)S(1)}, u32[]{:S(2)}, u32[]{:S(2)}) collective-permute-start(bf16[64,16,128]{2,1,0:T(8,128)(2,1)} %get-tuple-element.36), channel_id=1, source_target_pairs={{0,1},{1,2},{2,3},{3,4},{4,5},{5,6},{6,7},{7,8},{8,9},{9,10},{10,1... | collective-permute-start | bytes 786440 | tf_op jit(solution)/shard_map/ppermute | solution.py:543
  15.1 1.9 collective-permute-start.1
  17.1 0.6 dynamic-slice_bitcast_fusion.target_ref
  17.7 8.5 %pack.1 = bf16[8,32,64,128]{3,2,1,0:T(8,128)(2,1)} custom-call(s32[16]{0:T(128)} %dynamic-slice_bitcast_fusion.target_ref, bf16[16,4,64,256]{3,2,1,0:T(8,128)(2,1)} %bitcast.31), custom_call_target="tpu_custom_call" | custom-call | tf_op jit(solution)/shard_map/pack/pallas_call | solution.py:130
  26.2 11.6 %all-to-all-start = ((bf16[128,2,64,128]{3,2,1,0:T(8,128)(2,1)}), bf16[128,2,64,128]{3,2,1,0:T(8,128)(2,1)}, u32[]{:S(2)}, u32[]{:S(2)}) async-start(bf16[128,2,64,128]{3,2,1,0:T(8,128)(2,1)} %bitcast.30), calls=%async_computation | async-start | bytes 8388608 | tf_op jit(solution)/shard_map/all_to_all | solution.py:573
  38.0 0.7 reshape.214.taps_ref
  38.8 0.7 reshape.215.shift_ref
  39.6 2.5 convert_reduce_fusion
  42.2 0.4 select_reduce_fusion.1
  42.7 0.3 convert_reduce_fusion.1
  43.2 0.7 reshape.210.order_ref
  43.8 0.4 select_reduce_fusion.4
  44.3 0.7 reshape.209.start_ref
  45.2 0.7 div.20.inverse_ref
  45.9 0.4 fusion
  46.6 5.7 %bands.1 = (bf16[8,256,256]{2,1,0:T(8,128)(2,1)}, bf16[8,256,256]{2,1,0:T(8,128)(2,1)}, bf16[8,256,128]{2,1,0:T(8,128)(2,1)}, bf16[8,128,256]{2,1,0:T(8,128)(2,1...) custom-call(f32[504]{0:T(512)} %reshape.214.taps_ref, s32[24]{0:T(128)} %reshape.215.shift_ref), custom_call_target="tpu_custom_call" | custom-call | tf_op jit(solution)/shard_map/bands/pallas_call | solution.py:93
  52.5 0.5 slice_reduce_fusion.20
  53.1 0.8 multiply_reduce_fusion
  53.9 0.7 copy-done.14
  54.6 0.7 copy-done.15
  55.3 6.7 %tail.1.tail_ref.estimate_tail_ref = f32[64,16,128]{2,1,0:T(8,128)} custom-call(bf16[64,16,128]{2,1,0:T(8,128)(2,1)} %copy-done.14, bf16[64,16,128]{2,1,0:T(8,128)(2,1)} %copy-done.15), custom_call_target="tpu_custom_call" | custom-call | tf_op jit(solution)/shard_map/tail/pallas_call | solution.py:203
  62.0 21.2 %forward.2.blurred_ref = f32[8192,128]{1,0:T(8,128)} custom-call(f32[2,1024,128]{2,1,0:T(8,128)} %get-tuple-element.35.main_ref.estimate_main_ref, f32[64,16,128]{2,1,0:T(8,128)} %tail.1.tail_ref.estimate_tail_ref, bf16[128,48]{1,0:T(8,128)(2,1)} %bitcast.33, bf16[8,256,256]{2,1,0:T(8,128)(2,1)} %get-tuple-element.39.ky_ref, ...), custom_call_target="tpu_custom_call" | custom-call | tf_op jit(solution)/shard_map/forward/pallas_call | solution.py:274
  83.2 3.8 %all-to-all-done = bf16[128,2,64,128]{3,2,1,0:T(8,128)(2,1)} async-done(((bf16[128,2,64,128]{3,2,1,0:T(8,128)(2,1)}), bf16[128,2,64,128]{3,2,1,0:T(8,128)(2,1)}, u32[]{:S(2)}, u32[]{:S(2)}) %all-to-all-start) | async-done | bytes 4194336 | tf_op jit(solution)/shard_map/all_to_all | solution.py:573
  87.0 38.5 %first_adjoint.1 = (f32[2,1024,128]{2,1,0:T(8,128)}, f32[64,16,128]{2,1,0:T(8,128)}, bf16[96,16,128]{2,1,0:T(8,128)(2,1)}, bf16[96,16,128]{2,1,0:T(8,128)(2,1)}, bf16[8192,128]{1,0:T(8,128)(2,1)}) custom-call(s32[136]{0:T(256)} %reshape.209.start_ref, s32[256]{0:T(256)} %reshape.210.order_ref, f32[128]{0:T(128)} %div.20.inverse_ref, f32[8]{0:T(128)} %offset_ref.3, ...), custom_call_target="tpu_custom_call" | custom-call | tf_op jit(solution)/shard_map/first_adjoint/pallas_call | solution.py:376
  125.5 3.1 %collective-permute-start.2 = (bf16[96,16,128]{2,1,0:T(8,128)(2,1)}, bf16[96,16,128]{2,1,0:T(8,128)(2,1)S(1)}, u32[]{:S(2)}, u32[]{:S(2)}) collective-permute-start(bf16[96,16,128]{2,1,0:T(8,128)(2,1)} %get-tuple-element.47), channel_id=1, source_target_pairs={{0,16},{16,32},{32,48},{48,64},{64,80},{80,96},{96,112},{1,17},{17... | collective-permute-start | bytes 1179656 | tf_op jit(solution)/shard_map/ppermute | solution.py:543
  128.6 2.2 collective-permute-start.3
  131.6 2.1 collective-permute-done.2.from_left_ref
  133.7 4.3 %collective-permute-done.3.from_right_ref = bf16[96,16,128]{2,1,0:T(8,128)(2,1)S(1)} collective-permute-done((bf16[96,16,128]{2,1,0:T(8,128)(2,1)}, bf16[96,16,128]{2,1,0:T(8,128)(2,1)S(1)}, u32[]{:S(2)}, u32[]{:S(2)}) %collective-permute-start.3) | collective-permute-done | bytes 393248 | tf_op jit(solution)/shard_map/ppermute | solution.py:544
  138.0 0.7 copy-done.7
  138.7 4.2 %join_columns.2 = (f32[2,1024,128]{2,1,0:T(8,128)}, f32[64,16,128]{2,1,0:T(8,128)}, bf16[64,16,128]{2,1,0:T(8,128)(2,1)}, bf16[64,16,128]{2,1,0:T(8,128)(2,1)}) custom-call(f32[2,1024,128]{2,1,0:T(8,128)} %get-tuple-element.45.main_ref, f32[64,16,128]{2,1,0:T(8,128)} %get-tuple-element.46.tail_ref, bf16[96,16,128]{2,1,0:T(8,128)(2,1)} %copy-done.6, ...), custom_call_target="tpu_custom_call" | custom-call | tf_op jit(solution)/shard_map/join_columns/pallas_call | solution.py:429
  142.9 4.0 %collective-permute-start.4 = (bf16[64,16,128]{2,1,0:T(8,128)(2,1)}, bf16[64,16,128]{2,1,0:T(8,128)(2,1)S(1)}, u32[]{:S(2)}, u32[]{:S(2)}) collective-permute-start(bf16[64,16,128]{2,1,0:T(8,128)(2,1)} %get-tuple-element.51), channel_id=1, source_target_pairs={{0,1},{1,2},{2,3},{3,4},{4,5},{5,6},{6,7},{7,8},{8,9},{9,10},{10,1... | collective-permute-start | bytes 786440 | tf_op jit(solution)/shard_map/ppermute | solution.py:543
  146.9 2.1 collective-permute-start.5
  149.7 0.8 reshape.221.tail_ref
  150.6 0.3 reshape.222
  150.9 0.7 copy.72.main_ref
  151.8 0.7 reshape.217.rows_ref
  152.4 4.1 %weights.1 = (f32[2,1024,128]{2,1,0:T(8,128)}, f32[64,16,128]{2,1,0:T(8,128)}) custom-call(f32[512]{0:T(512)} %reshape.217.rows_ref, f32[8,2,16,128]{3,2,1,0:T(8,128)} %copy.72.main_ref, f32[8,16,128]{2,1,0:T(8,128)} %reshape.221.tail_ref), custom_call_target="tpu_custom_call" | custom-call | tf_op jit(solution)/shard_map/weights/pallas_call | solution.py:229
  156.5 2.9 %collective-permute-done.5.from_high_ref = bf16[64,16,128]{2,1,0:T(8,128)(2,1)S(1)} collective-permute-done((bf16[64,16,128]{2,1,0:T(8,128)(2,1)}, bf16[64,16,128]{2,1,0:T(8,128)(2,1)S(1)}, u32[]{:S(2)}, u32[]{:S(2)}) %collective-permute-start.5) | collective-permute-done | bytes 262176 | tf_op jit(solution)/shard_map/ppermute | solution.py:544
  159.4 0.7 copy-done.11
  160.1 5.1 %update.1 = (f32[2,1024,128]{2,1,0:T(8,128)}, f32[64,16,128]{2,1,0:T(8,128)}) custom-call(f32[2,1024,128]{2,1,0:T(8,128)} %get-tuple-element.49.main_ref, f32[64,16,128]{2,1,0:T(8,128)} %get-tuple-element.50.tail_ref, bf16[64,16,128]{2,1,0:T(8,128)(2,1)} %copy-done.10, bf16[64,16,128]{2,1,0:T(8,128)(2,1)} %copy-done.11, ...), custom_call_target="tpu_custom_call" | custom-call | tf_op jit(solution)/shard_map/update/pallas_call | solution.py:471
  165.2 21.2 %forward.3.blurred_ref = f32[8192,128]{1,0:T(8,128)} custom-call(f32[2,1024,128]{2,1,0:T(8,128)} %get-tuple-element.55.main_ref.estimate_ref, f32[64,16,128]{2,1,0:T(8,128)} %get-tuple-element.56.tail_ref, bf16[128,48]{1,0:T(8,128)(2,1)} %bitcast.34, bf16[8,256,256]{2,1,0:T(8,128)(2,1)} %get-tuple-element.39.ky_ref, ...), custom_call_target="tpu_custom_call" | custom-call | tf_op jit(solution)/shard_map/forward/pallas_call | solution.py:274
  186.5 24.5 %next_adjoint.1 = (f32[2,1024,128]{2,1,0:T(8,128)}, f32[64,16,128]{2,1,0:T(8,128)}, bf16[96,16,128]{2,1,0:T(8,128)(2,1)}, bf16[96,16,128]{2,1,0:T(8,128)(2,1)}) custom-call(f32[8]{0:T(128)} %offset_ref.3, bf16[8192,128]{1,0:T(8,128)(2,1)} %get-tuple-element.44.average_ref, f32[8192,128]{1,0:T(8,128)} %forward.3.blurred_ref, ...), custom_call_target="tpu_custom_call" | custom-call | tf_op jit(solution)/shard_map/next_adjoint/pallas_call | solution.py:387
  211.0 2.7 collective-permute-start.6
  213.7 1.9 collective-permute-start.7
  215.6 3.1 %collective-permute-done.6.from_left_ref = bf16[96,16,128]{2,1,0:T(8,128)(2,1)S(1)} collective-permute-done((bf16[96,16,128]{2,1,0:T(8,128)(2,1)}, bf16[96,16,128]{2,1,0:T(8,128)(2,1)S(1)}, u32[]{:S(2)}, u32[]{:S(2)}) %collective-permute-start.6) | collective-permute-done | bytes 393248 | tf_op jit(solution)/shard_map/ppermute | solution.py:543
  218.7 4.3 %collective-permute-done.7.from_right_ref = bf16[96,16,128]{2,1,0:T(8,128)(2,1)S(1)} collective-permute-done((bf16[96,16,128]{2,1,0:T(8,128)(2,1)}, bf16[96,16,128]{2,1,0:T(8,128)(2,1)S(1)}, u32[]{:S(2)}, u32[]{:S(2)}) %collective-permute-start.7) | collective-permute-done | bytes 393248 | tf_op jit(solution)/shard_map/ppermute | solution.py:544
  223.0 0.7 copy-done.9
  223.7 4.2 %join_columns.3 = (f32[2,1024,128]{2,1,0:T(8,128)}, f32[64,16,128]{2,1,0:T(8,128)}, bf16[64,16,128]{2,1,0:T(8,128)(2,1)}, bf16[64,16,128]{2,1,0:T(8,128)(2,1)}) custom-call(f32[2,1024,128]{2,1,0:T(8,128)} %get-tuple-element.57.main_ref, f32[64,16,128]{2,1,0:T(8,128)} %get-tuple-element.58.tail_ref, bf16[96,16,128]{2,1,0:T(8,128)(2,1)} %copy-done.8, ...), custom_call_target="tpu_custom_call" | custom-call | tf_op jit(solution)/shard_map/join_columns/pallas_call | solution.py:429
  227.9 2.3 collective-permute-start.8
  230.3 2.9 %collective-permute-start.9 = (bf16[64,16,128]{2,1,0:T(8,128)(2,1)}, bf16[64,16,128]{2,1,0:T(8,128)(2,1)S(1)}, u32[]{:S(2)}, u32[]{:S(2)}) collective-permute-start(bf16[64,16,128]{2,1,0:T(8,128)(2,1)} %get-tuple-element.64), channel_id=1, source_target_pairs={{1,0},{2,1},{3,2},{4,3},{5,4},{6,5},{7,6},{8,7},{9,8},{10,9},{11,1... | collective-permute-start | bytes 786440 | tf_op jit(solution)/shard_map/ppermute | solution.py:544
  233.2 5.1 %collective-permute-done.8.from_low_ref = bf16[64,16,128]{2,1,0:T(8,128)(2,1)S(1)} collective-permute-done((bf16[64,16,128]{2,1,0:T(8,128)(2,1)}, bf16[64,16,128]{2,1,0:T(8,128)(2,1)S(1)}, u32[]{:S(2)}, u32[]{:S(2)}) %collective-permute-start.8) | collective-permute-done | bytes 262176 | tf_op jit(solution)/shard_map/ppermute | solution.py:543
  238.3 4.4 %collective-permute-done.9.from_high_ref = bf16[64,16,128]{2,1,0:T(8,128)(2,1)S(1)} collective-permute-done((bf16[64,16,128]{2,1,0:T(8,128)(2,1)}, bf16[64,16,128]{2,1,0:T(8,128)(2,1)S(1)}, u32[]{:S(2)}, u32[]{:S(2)}) %collective-permute-start.9) | collective-permute-done | bytes 262176 | tf_op jit(solution)/shard_map/ppermute | solution.py:544
  242.8 0.7 copy-done.13
  243.5 5.7 %finish.1.refs_0_ = f32[1024,128]{1,0:T(8,128)} custom-call(f32[2,1024,128]{2,1,0:T(8,128)} %get-tuple-element.61.main_ref, f32[64,16,128]{2,1,0:T(8,128)} %get-tuple-element.62.tail_ref, bf16[64,16,128]{2,1,0:T(8,128)(2,1)} %copy-done.12, bf16[64,16,128]{2,1,0:T(8,128)(2,1)} %copy-done.13, f32[2,1024,128]{2,1,0:T(8,128)} %get-tuple-element.55.main_ref.estimate_ref, ...), custom_call_target="tpu_custom_call" | custom-call | tf_op jit(solution)/shard_map/finish/pallas_call | solution.py:499
  249.2 1.7 collective-permute-start.11
  250.9 0.9 collective-permute-start.13
  251.8 10.6 %collective-permute-done.10.refs_1_ = f32[1024,128]{1,0:T(8,128)S(1)} collective-permute-done((f32[1024,128]{1,0:T(8,128)}, f32[1024,128]{1,0:T(8,128)S(1)}, u32[]{:S(2)}, u32[]{:S(2)}) %collective-permute-start.10) | collective-permute-done | bytes 524320 | tf_op jit(solution)/shard_map/ppermute | solution.py:550
  262.4 1.9 collective-permute-start.14
  264.3 9.7 %collective-permute-done.11.refs_2_ = f32[1024,128]{1,0:T(8,128)S(1)} collective-permute-done((f32[1024,128]{1,0:T(8,128)}, f32[1024,128]{1,0:T(8,128)S(1)}, u32[]{:S(2)}, u32[]{:S(2)}) %collective-permute-start.11) | collective-permute-done | bytes 524320 | tf_op jit(solution)/shard_map/ppermute | solution.py:550
  274.0 1.2 collective-permute-start.15
  275.3 1.5 collective-permute-start.16
  276.8 1.6 collective-permute-done.16.refs_7_
  278.5 9.4 %assemble.1 = f32[64,64,256]{2,1,0:T(8,128)} custom-call(s32[1]{0:T(128)} %bitcast.index_ref, f32[1024,128]{1,0:T(8,128)} %finish.1.refs_0_, f32[1024,128]{1,0:T(8,128)} %copy-done, f32[1024,128]{1,0:T(8,128)} %copy-done.1, f32[1024,128]{1,0:T(8,128)} %copy-done.2, f32[1024,128]{1,0:T(8,128)} %copy-done.3, f32[1024,128]{1,0:T(8,128)} %copy-done.4, ...), custom_call_target="tpu_custom_call" | custom-call | tf_op jit(solution)/shard_map/assemble/pallas_call | solution.py:531
  (88 shorter events, 3.4 us)
Async XLA Ops:
  0.0 17.0 %copy-start.18 = (s32[8,256,1]{1,2,0:T(1,128)S(1)}, s32[8,256,1]{1,2,0:T(1,128)}, u32[]{:S(2)}) copy-start(s32[8,256,1]{1,2,0:T(1,128)} %param.9) | copy-start | bytes 24580
  11.6 42.3 %collective-permute-start = (bf16[64,16,128]{2,1,0:T(8,128)(2,1)}, bf16[64,16,128]{2,1,0:T(8,128)(2,1)S(1)}, u32[]{:S(2)}, u32[]{:S(2)}) collective-permute-start(bf16[64,16,128]{2,1,0:T(8,128)(2,1)} %get-tuple-element.36), channel_id=1, source_target_pairs={{0,1},{1,2},{2,3},{3,4},{4,5},{5,6},{6,7},{7,8},{8,9},{9,10},{10,1... | collective-permute-start | bytes 786440 | tf_op jit(solution)/shard_map/ppermute | solution.py:543
  15.1 38.9 %collective-permute-start.1 = (bf16[64,16,128]{2,1,0:T(8,128)(2,1)}, bf16[64,16,128]{2,1,0:T(8,128)(2,1)S(1)}, u32[]{:S(2)}, u32[]{:S(2)}) collective-permute-start(bf16[64,16,128]{2,1,0:T(8,128)(2,1)} %get-tuple-element.37), channel_id=1, source_target_pairs={{1,0},{2,1},{3,2},{4,3},{5,4},{6,5},{7,6},{8,7},{9,8},{10,9},{11,1... | collective-permute-start | bytes 786440 | tf_op jit(solution)/shard_map/ppermute | solution.py:544
  26.2 11.6 %copy-start.16 = (f32[8,3,21]{2,0,1:T(8,128)S(1)}, f32[8,3,21]{2,0,1:T(8,128)}, u32[]{:S(2)}) copy-start(f32[8,3,21]{2,0,1:T(8,128)} %param.12) | copy-start | bytes 6052
  26.2 12.5 %copy-start.19 = (s32[8,3]{0,1:T(4,128)S(1)}, s32[8,3]{0,1:T(4,128)}, u32[]{:S(2)}) copy-start(s32[8,3]{0,1:T(4,128)} %param.11) | copy-start | bytes 292
  26.2 13.2 %copy-start.17 = (s32[8,256]{1,0:T(8,128)S(1)}, s32[8,256]{1,0:T(8,128)}, u32[]{:S(2)}) copy-start(s32[8,256]{1,0:T(8,128)} %param.10) | copy-start | bytes 24580
  26.2 60.7 %all-to-all-start = ((bf16[128,2,64,128]{3,2,1,0:T(8,128)(2,1)}), bf16[128,2,64,128]{3,2,1,0:T(8,128)(2,1)}, u32[]{:S(2)}, u32[]{:S(2)}) async-start(bf16[128,2,64,128]{3,2,1,0:T(8,128)(2,1)} %bitcast.30), calls=%async_computation | async-start | bytes 8388608 | tf_op jit(solution)/shard_map/all_to_all | solution.py:573
  53.9 0.7 copy-start.14
  54.6 0.7 copy-start.15
  125.5 8.2 %collective-permute-start.2 = (bf16[96,16,128]{2,1,0:T(8,128)(2,1)}, bf16[96,16,128]{2,1,0:T(8,128)(2,1)S(1)}, u32[]{:S(2)}, u32[]{:S(2)}) collective-permute-start(bf16[96,16,128]{2,1,0:T(8,128)(2,1)} %get-tuple-element.47), channel_id=1, source_target_pairs={{0,16},{16,32},{32,48},{48,64},{64,80},{80,96},{96,112},{1,17},{17... | collective-permute-start | bytes 1179656 | tf_op jit(solution)/shard_map/ppermute | solution.py:543
  128.6 9.3 %collective-permute-start.3 = (bf16[96,16,128]{2,1,0:T(8,128)(2,1)}, bf16[96,16,128]{2,1,0:T(8,128)(2,1)S(1)}, u32[]{:S(2)}, u32[]{:S(2)}) collective-permute-start(bf16[96,16,128]{2,1,0:T(8,128)(2,1)} %get-tuple-element.48), channel_id=1, source_target_pairs={{16,0},{32,16},{48,32},{64,48},{80,64},{96,80},{112,96},{17,1},{33... | collective-permute-start | bytes 1179656 | tf_op jit(solution)/shard_map/ppermute | solution.py:544
  133.7 4.3 %copy-start.6 = (bf16[96,16,128]{2,1,0:T(8,128)(2,1)}, bf16[96,16,128]{2,1,0:T(8,128)(2,1)S(1)}, u32[]{:S(2)}) copy-start(bf16[96,16,128]{2,1,0:T(8,128)(2,1)S(1)} %collective-permute-done.2.from_left_ref) | copy-start | bytes 1179652
  137.9 0.7 copy-start.7
  142.9 13.6 %collective-permute-start.4 = (bf16[64,16,128]{2,1,0:T(8,128)(2,1)}, bf16[64,16,128]{2,1,0:T(8,128)(2,1)S(1)}, u32[]{:S(2)}, u32[]{:S(2)}) collective-permute-start(bf16[64,16,128]{2,1,0:T(8,128)(2,1)} %get-tuple-element.51), channel_id=1, source_target_pairs={{0,1},{1,2},{2,3},{3,4},{4,5},{5,6},{6,7},{7,8},{8,9},{9,10},{10,1... | collective-permute-start | bytes 786440 | tf_op jit(solution)/shard_map/ppermute | solution.py:543
  146.9 12.5 %collective-permute-start.5 = (bf16[64,16,128]{2,1,0:T(8,128)(2,1)}, bf16[64,16,128]{2,1,0:T(8,128)(2,1)S(1)}, u32[]{:S(2)}, u32[]{:S(2)}) collective-permute-start(bf16[64,16,128]{2,1,0:T(8,128)(2,1)} %get-tuple-element.52), channel_id=1, source_target_pairs={{1,0},{2,1},{3,2},{4,3},{5,4},{6,5},{7,6},{8,7},{9,8},{10,9},{11,1... | collective-permute-start | bytes 786440 | tf_op jit(solution)/shard_map/ppermute | solution.py:544
  156.5 2.9 %copy-start.10 = (bf16[64,16,128]{2,1,0:T(8,128)(2,1)}, bf16[64,16,128]{2,1,0:T(8,128)(2,1)S(1)}, u32[]{:S(2)}) copy-start(bf16[64,16,128]{2,1,0:T(8,128)(2,1)S(1)} %collective-permute-done.4.from_low_ref) | copy-start | bytes 786436
  159.4 0.7 copy-start.11
  211.0 7.7 %collective-permute-start.6 = (bf16[96,16,128]{2,1,0:T(8,128)(2,1)}, bf16[96,16,128]{2,1,0:T(8,128)(2,1)S(1)}, u32[]{:S(2)}, u32[]{:S(2)}) collective-permute-start(bf16[96,16,128]{2,1,0:T(8,128)(2,1)} %get-tuple-element.59), channel_id=1, source_target_pairs={{0,16},{16,32},{32,48},{48,64},{64,80},{80,96},{96,112},{1,17},{17... | collective-permute-start | bytes 1179656 | tf_op jit(solution)/shard_map/ppermute | solution.py:543
  213.7 9.3 %collective-permute-start.7 = (bf16[96,16,128]{2,1,0:T(8,128)(2,1)}, bf16[96,16,128]{2,1,0:T(8,128)(2,1)S(1)}, u32[]{:S(2)}, u32[]{:S(2)}) collective-permute-start(bf16[96,16,128]{2,1,0:T(8,128)(2,1)} %get-tuple-element.60), channel_id=1, source_target_pairs={{16,0},{32,16},{48,32},{64,48},{80,64},{96,80},{112,96},{17,1},{33... | collective-permute-start | bytes 1179656 | tf_op jit(solution)/shard_map/ppermute | solution.py:544
  218.7 4.3 %copy-start.8 = (bf16[96,16,128]{2,1,0:T(8,128)(2,1)}, bf16[96,16,128]{2,1,0:T(8,128)(2,1)S(1)}, u32[]{:S(2)}) copy-start(bf16[96,16,128]{2,1,0:T(8,128)(2,1)S(1)} %collective-permute-done.6.from_left_ref) | copy-start | bytes 1179652
  223.0 0.7 copy-start.9
  227.9 10.4 %collective-permute-start.8 = (bf16[64,16,128]{2,1,0:T(8,128)(2,1)}, bf16[64,16,128]{2,1,0:T(8,128)(2,1)S(1)}, u32[]{:S(2)}, u32[]{:S(2)}) collective-permute-start(bf16[64,16,128]{2,1,0:T(8,128)(2,1)} %get-tuple-element.63), channel_id=1, source_target_pairs={{0,1},{1,2},{2,3},{3,4},{4,5},{5,6},{6,7},{7,8},{8,9},{9,10},{10,1... | collective-permute-start | bytes 786440 | tf_op jit(solution)/shard_map/ppermute | solution.py:543
  230.3 12.5 %collective-permute-start.9 = (bf16[64,16,128]{2,1,0:T(8,128)(2,1)}, bf16[64,16,128]{2,1,0:T(8,128)(2,1)S(1)}, u32[]{:S(2)}, u32[]{:S(2)}) collective-permute-start(bf16[64,16,128]{2,1,0:T(8,128)(2,1)} %get-tuple-element.64), channel_id=1, source_target_pairs={{1,0},{2,1},{3,2},{4,3},{5,4},{6,5},{7,6},{8,7},{9,8},{10,9},{11,1... | collective-permute-start | bytes 786440 | tf_op jit(solution)/shard_map/ppermute | solution.py:544
  238.3 4.4 %copy-start.12 = (bf16[64,16,128]{2,1,0:T(8,128)(2,1)}, bf16[64,16,128]{2,1,0:T(8,128)(2,1)S(1)}, u32[]{:S(2)}) copy-start(bf16[64,16,128]{2,1,0:T(8,128)(2,1)S(1)} %collective-permute-done.8.from_low_ref) | copy-start | bytes 786436
  242.8 0.7 copy-start.13
  249.2 13.3 %collective-permute-start.10 = (f32[1024,128]{1,0:T(8,128)}, f32[1024,128]{1,0:T(8,128)S(1)}, u32[]{:S(2)}, u32[]{:S(2)}) collective-permute-start(f32[1024,128]{1,0:T(8,128)} %finish.1.refs_0_), channel_id=1, source_target_pairs={{32,0},{48,16},{64,32},{80,48},{96,64},{112,80},{0,96},{16,112},{3... | collective-permute-start | bytes 1572872 | tf_op jit(solution)/shard_map/ppermute | solution.py:550
  249.2 24.8 %collective-permute-start.11 = (f32[1024,128]{1,0:T(8,128)}, f32[1024,128]{1,0:T(8,128)S(1)}, u32[]{:S(2)}, u32[]{:S(2)}) collective-permute-start(f32[1024,128]{1,0:T(8,128)} %finish.1.refs_0_), channel_id=1, source_target_pairs={{64,0},{80,16},{96,32},{112,48},{0,64},{16,80},{32,96},{48,112},{6... | collective-permute-start | bytes 1572872 | tf_op jit(solution)/shard_map/ppermute | solution.py:550
  250.9 24.4 %collective-permute-start.12 = (f32[1024,128]{1,0:T(8,128)}, f32[1024,128]{1,0:T(8,128)S(1)}, u32[]{:S(2)}, u32[]{:S(2)}) collective-permute-start(f32[1024,128]{1,0:T(8,128)} %finish.1.refs_0_), channel_id=1, source_target_pairs={{96,0},{112,16},{0,32},{16,48},{32,64},{48,80},{64,96},{80,112},{9... | collective-permute-start | bytes 1572872 | tf_op jit(solution)/shard_map/ppermute | solution.py:550
  250.9 25.9 %collective-permute-start.13 = (f32[1024,128]{1,0:T(8,128)}, f32[1024,128]{1,0:T(8,128)S(1)}, u32[]{:S(2)}, u32[]{:S(2)}) collective-permute-start(f32[1024,128]{1,0:T(8,128)} %finish.1.refs_0_), channel_id=1, source_target_pairs={{0,16},{16,0},{32,48},{48,32},{64,80},{80,64},{96,112},{112,96},{1... | collective-permute-start | bytes 1572872 | tf_op jit(solution)/shard_map/ppermute | solution.py:553
  262.4 16.0 %copy-start = (f32[1024,128]{1,0:T(8,128)}, f32[1024,128]{1,0:T(8,128)S(1)}, u32[]{:S(2)}) copy-start(f32[1024,128]{1,0:T(8,128)S(1)} %collective-permute-done.10.refs_1_) | copy-start | bytes 1572868
  262.4 14.4 %collective-permute-start.14 = (f32[1024,128]{1,0:T(8,128)S(1)}, f32[1024,128]{1,0:T(8,128)S(1)}, u32[]{:S(2)}, u32[]{:S(2)}) collective-permute-start(f32[1024,128]{1,0:T(8,128)S(1)} %collective-permute-done.10.refs_1_), channel_id=1, source_target_pairs={{0,16},{16,0},{32,48},{48,32},{64,80},{80,64},{96,112},{112,96},{1... | collective-permute-start | bytes 1572872 | tf_op jit(solution)/shard_map/ppermute | solution.py:553
  274.0 4.5 %copy-start.1 = (f32[1024,128]{1,0:T(8,128)}, f32[1024,128]{1,0:T(8,128)S(1)}, u32[]{:S(2)}) copy-start(f32[1024,128]{1,0:T(8,128)S(1)} %collective-permute-done.11.refs_2_) | copy-start | bytes 1572868
  274.0 2.8 collective-permute-start.15
  275.3 3.2 %copy-start.2 = (f32[1024,128]{1,0:T(8,128)}, f32[1024,128]{1,0:T(8,128)S(1)}, u32[]{:S(2)}) copy-start(f32[1024,128]{1,0:T(8,128)S(1)} %collective-permute-done.12.refs_3_) | copy-start | bytes 1572868
  275.3 3.2 %collective-permute-start.16 = (f32[1024,128]{1,0:T(8,128)S(1)}, f32[1024,128]{1,0:T(8,128)}, u32[]{:S(2)}, u32[]{:S(2)}) collective-permute-start(f32[1024,128]{1,0:T(8,128)S(1)} %collective-permute-done.12.refs_3_), channel_id=1, source_target_pairs={{0,16},{16,0},{32,48},{48,32},{64,80},{80,64},{96,112},{112,96},{1... | collective-permute-start | bytes 1572872 | tf_op jit(solution)/shard_map/ppermute | solution.py:553
  276.8 1.7 copy-start.3
  276.8 1.7 copy-start.4
  276.8 1.7 copy-start.5

commit v2 on v1

v2 whole, which is shorter than its diff:
```python
import jax
import jax.numpy as jnp
from jax import lax
from jax.experimental import pallas as pl
from jax.experimental.pallas import tpu as pltpu
from jax.sharding import PartitionSpec as P


CAP = 2
TAPS = 21
HALO = 16
VIEWS = 8
SLOTS = 16
NY = 64
PART = 32
ROWS = 256
QUADS = 16

F32 = jnp.float32
BF16 = jnp.bfloat16
I32 = jnp.int32
I16 = jnp.int16


def lane_block(shape):
    return lax.broadcasted_iota(I32, shape, len(shape) - 1) // PART


def rotate(value, amount):
    return pltpu.roll(value, amount % 128, value.ndim - 1)


def digit_swap(shape):
    row = lax.broadcasted_iota(I32, shape, 0)
    column = lax.broadcasted_iota(I32, shape, 1)
    target = ((row // PART) % 4) * 128 + (row // 128) * PART + row % PART
    return jnp.where(column == target, 1.0, 0.0).astype(BF16)


def swap_fours(first, second):
    upper = lax.broadcasted_iota(I32, first.shape, 0) < 4
    return (jnp.where(upper, first, pltpu.roll(second, 4, 0)),
            jnp.where(upper, pltpu.roll(first, 4, 0), second))


def vmem(count):
    return [pl.BlockSpec(memory_space=pltpu.VMEM)] * count


def smem(count):
    return [pl.BlockSpec(memory_space=pltpu.SMEM)] * count


def to_fixed(value, scale):
    return (value * scale + 0.5).astype(I32).astype(I16)


def from_fixed(value, step):
    return value.astype(I32).astype(F32) * step


def partial_bound(offset_ref):
    total = 0.0
    for view in range(VIEWS):
        total = total + 2.0 / jnp.full((8, 128), offset_ref[view], F32)
    return total * 1.05


def band_kernel(taps_ref, shift_ref, ky_ref, kyt_ref, kx_ref, kxt_ref, bzf_ref, bza_ref):
    radius = (TAPS - 1) // 2

    def fill(difference, view, axis):
        result = jnp.zeros(difference.shape, F32)
        for tap in range(TAPS):
            result = jnp.where(difference == tap, taps_ref[(view * 3 + axis) * TAPS + tap], result)
        return result

    def one_view(view, carry):
        shift_z = shift_ref[view * 3]
        shift_y = shift_ref[view * 3 + 1]
        shift_x = shift_ref[view * 3 + 2]
        row = lax.broadcasted_iota(I32, (16, 2 * ROWS), 0)
        lane = lax.broadcasted_iota(I32, (16, 2 * ROWS), 1)
        offset = (lane // 16 - 16) * 4 + lane % 4 - row % 4
        same = (lane // 4) % 4 == row // 4
        for strip, target_ref in ((jnp.where(same, offset - shift_y + radius, -1), ky_ref),
                                  (jnp.where(same, -offset - shift_y + radius, -1), kyt_ref)):
            values = fill(strip, view, 1)
            for quad in range(QUADS):
                target_ref[view, quad * 16:(quad + 1) * 16, :] = values[
                    :, ROWS - quad * 16:2 * ROWS - quad * 16].astype(BF16)
        row = lax.broadcasted_iota(I32, (PART, 128), 0)
        lane = lax.broadcasted_iota(I32, (PART, 128), 1)
        for half in range(2):
            base = fill(half * PART + row - (lane % PART + HALO) - shift_x + radius, view, 2)
            for block in range(4):
                first = half * 128 + block * PART
                kx_ref[view, first:first + PART, :] = jnp.where(lane // PART == block, base, 0.0).astype(BF16)
            base = fill(half * PART + lane % PART - (row + HALO) - shift_x + radius, view, 2)
            for block in range(4):
                kxt_ref[view, block * PART:(block + 1) * PART, half * 128:(half + 1) * 128] = jnp.where(
                    lane // PART == block, base, 0.0).astype(BF16)
        row = lax.broadcasted_iota(I32, (64, 192), 0)
        lane = lax.broadcasted_iota(I32, (64, 192), 1)
        difference = jnp.where(lane % 4 == row % 4, lane // 4 - 16 - row // 4 - shift_z + radius, -1)
        bzf_ref[pl.ds(pl.multiple_of(view * 64, 64), 64), :] = fill(difference, view, 0).astype(BF16)
        return carry

    lax.fori_loop(0, VIEWS, one_view, 0)
    row = lax.broadcasted_iota(I32, (192, 128), 0)
    lane = lax.broadcasted_iota(I32, (192, 128), 1)
    left = lane < 64
    for pair in range(VIEWS // 2):
        shift = jnp.where(left, shift_ref[pair * 6], shift_ref[pair * 6 + 3])
        difference = jnp.where(lane % 4 == row % 4, row // 4 - 16 - (lane // 4) % 16 - shift + radius, -1)
        total = jnp.zeros((192, 128), F32)
        for tap in range(TAPS):
            value = jnp.where(left, taps_ref[pair * 6 * TAPS + tap], taps_ref[(pair * 6 + 3) * TAPS + tap])
            total = jnp.where(difference == tap, value, total)
        bza_ref[:, pair * 128:(pair + 1) * 128] = total.astype(BF16)


def build_bands(taps, shifts):
    return pl.pallas_call(
        band_kernel,
        out_shape=(
            jax.ShapeDtypeStruct((VIEWS, ROWS, ROWS), BF16),
            jax.ShapeDtypeStruct((VIEWS, ROWS, ROWS), BF16),
            jax.ShapeDtypeStruct((VIEWS, ROWS, 128), BF16),
            jax.ShapeDtypeStruct((VIEWS, 128, ROWS), BF16),
            jax.ShapeDtypeStruct((VIEWS * 64, 192), BF16),
            jax.ShapeDtypeStruct((192, VIEWS * 64), BF16),
        ),
        in_specs=smem(2),
        out_specs=tuple(vmem(6)),
        name="bands",
    )(taps, shifts)


def pack_kernel(target_ref, pieces_ref, out_ref, swap_ref):
    swap_ref[...] = digit_swap((512, 512))
    count = pieces_ref.shape[0]

    def four_pieces(group, carry):
        rows = []
        for k in range(4):
            for half in range(2):
                rows.append(jnp.concatenate(
                    [pieces_ref[group * 4 + k, q, :, half * 128:(half + 1) * 128] for q in range(4)], axis=1))
        mixed = jnp.dot(jnp.concatenate(rows, axis=0), swap_ref[...], preferred_element_type=F32).astype(BF16)
        for k in range(4):
            piece = group * 4 + k
            target = target_ref[piece]
            rank = jnp.int32(0)
            for other in range(count):
                rank = rank + jnp.where((target_ref[other] == target) & (other < piece), 1, 0)
            slot = target * CAP + rank
            for half in range(2):
                first = (k * 2 + half) * NY
                for part in range(4):
                    out_ref[half * 4 + part, slot] = mixed[first:first + NY, part * 128:(part + 1) * 128]
        return carry

    lax.fori_loop(0, count // 4, four_pieces, 0)


def pack_pieces(targets, pieces, block_count):
    return pl.pallas_call(
        pack_kernel,
        out_shape=jax.ShapeDtypeStruct((VIEWS, block_count * CAP, NY, 128), BF16),
        in_specs=smem(1) + vmem(1),
        out_specs=vmem(1)[0],
        scratch_shapes=[pltpu.VMEM((512, 512), BF16)],
        name="pack",
    )(targets, pieces)


def window_kernel(index_ref, estimate_ref, main_ref):
    part = index_ref[0]
    block = lane_block((NY, 128))
    lane = lax.broadcasted_iota(I32, (NY, 128), 1) % PART

    def two_planes(step, carry):
        for half in range(2):
            column = (part + half) * PART - HALO + lane
            inside = (column >= 0) & (column < 256)
            planes = []
            for odd in range(2):
                result = jnp.zeros((NY, 128), F32)
                for h in range(4):
                    plane = estimate_ref[h * 16 + step * 2 + odd]
                    amount = (16 - PART * part - PART * half + PART * h + 512) % 256
                    result = jnp.where(block == h, pltpu.roll(plane, amount, 1)[:, :128], result)
                planes.append(jnp.where(inside, result, 0.0))
            for m in range(8):
                low, high = swap_fours(planes[0][m * 8:m * 8 + 8], planes[1][m * 8:m * 8 + 8])
                main_ref[half, pl.ds(pl.multiple_of(m * 128 + step * 8, 8), 8), :] = low
                main_ref[half, pl.ds(pl.multiple_of(m * 128 + 64 + step * 8, 8), 8), :] = high
        return carry

    lax.fori_loop(0, 8, two_planes, 0)


def window_estimate(index, estimate):
    return pl.pallas_call(
        window_kernel,
        out_shape=jax.ShapeDtypeStruct((2, 1024, 128), F32),
        in_specs=smem(1) + vmem(1),
        out_specs=vmem(1)[0],
        name="window",
    )(index, estimate)


def ends_kernel(index_ref, first_ref, last_ref, low_ref, high_ref):
    part = index_ref[0]
    amount = (16 - PART * part + 256) % 256
    lane = lax.broadcasted_iota(I32, (32, 128), 1)
    column = part * PART - HALO + lane % 64
    inside = (column >= 0) & (column < 256)

    def four_planes(step, carry):
        for source_ref, target_ref in ((first_ref, low_ref), (last_ref, high_ref)):
            planes = []
            for k in range(4):
                plane = source_ref[step * 4 + k]
                top = pltpu.roll(plane[:32], amount, 1)[:, :128]
                bottom = pltpu.roll(plane[32:], (amount + 64) % 256, 1)[:, :128]
                planes.append(jnp.where(inside, jnp.where(lane < 64, top, bottom), 0.0))
            for m in range(4):
                rows = slice(m * 8, m * 8 + 8)
                front = swap_fours(planes[0][rows], planes[1][rows])
                back = swap_fours(planes[2][rows], planes[3][rows])
                for odd in range(2):
                    target_ref[m * 2 + odd, pl.ds(pl.multiple_of(step * 16, 16), 16), :] = jnp.concatenate(
                        [front[odd], back[odd]], axis=0).astype(BF16)
        return carry

    lax.fori_loop(0, 4, four_planes, 0)


def window_ends(index, estimate):
    return pl.pallas_call(
        ends_kernel,
        grid=(1,),
        out_shape=(jax.ShapeDtypeStruct((8, 64, 128), BF16),) * 2,
        in_specs=smem(1) + [pl.BlockSpec((16, NY, 256), lambda step: (0, 0, 0)),
                            pl.BlockSpec((16, NY, 256), lambda step: (3, 0, 0))],
        out_specs=tuple(vmem(2)),
        name="ends",
    )(index, estimate, estimate)


def build_tail(edge_ref, from_low_ref, from_high_ref, tail_ref):
    block = lane_block((64, 128))

    def two_quads(quad, carry):
        low = from_low_ref[quad].astype(F32) * edge_ref[2]
        high = from_high_ref[quad].astype(F32) * edge_ref[3]
        for member in range(2):
            base = member * 64
            result = jnp.where(block == 0, rotate(low, -base), rotate(low, 32 - base))
            result = jnp.where(block == 1, rotate(high, 32 - base), result)
            tail_ref[quad + member * 8] = jnp.where(block == 3, rotate(high, 64 - base), result)
        return carry

    lax.fori_loop(0, QUADS // 2, two_quads, 0)


def weight_kernel(rows_ref, main_ref, tail_ref, out_main_ref, out_tail_ref):
    quarter = lax.broadcasted_iota(I32, (64, 128), 0) % 4

    def one_quad(quad, carry):
        rows = pl.ds(pl.multiple_of(quad * 64, 64), 64)
        totals = [jnp.zeros((64, 128), F32) for _ in range(3)]
        for view in range(VIEWS):
            factor = jnp.full((64, 128), rows_ref[view * NY + quad * 4], F32)
            for k in range(1, 4):
                factor = jnp.where(quarter == k, rows_ref[view * NY + quad * 4 + k], factor)
            totals[0] = totals[0] + factor * main_ref[view, 0]
            totals[1] = totals[1] + factor * main_ref[view, 1]
            totals[2] = totals[2] + factor * tail_ref[view]
        out_main_ref[0, rows, :] = 1.0 / jnp.maximum(totals[0], 1.0)
        out_main_ref[1, rows, :] = 1.0 / jnp.maximum(totals[1], 1.0)
        out_tail_ref[quad] = 1.0 / jnp.maximum(totals[2], 1.0)
        return carry

    lax.fori_loop(0, QUADS, one_quad, 0)


def build_weights(rows, main, tail):
    return pl.pallas_call(
        weight_kernel,
        out_shape=(
            jax.ShapeDtypeStruct((2, 1024, 128), F32),
            jax.ShapeDtypeStruct((QUADS, 64, 128), F32),
        ),
        in_specs=smem(1) + vmem(2),
        out_specs=tuple(vmem(2)),
        name="weights",
    )(rows, main, tail)


def forward_depth(main_ref, tail_ref, bzf_ref, planes_ref):
    block = lane_block((64, 128))

    def stacked(quad):
        rows = pl.ds(pl.multiple_of(quad * 64, 64), 64)
        left = main_ref[0, rows, :]
        right = main_ref[1, rows, :]
        tail = tail_ref[quad]
        turned = rotate(tail, 64)
        lower = jnp.concatenate([jnp.where(block == 0, tail, rotate(left, 32)),
                                 jnp.where(block == 0, turned, rotate(right, 32))], axis=1)
        upper = jnp.concatenate([jnp.where(block == 3, turned, rotate(left, 96)),
                                 jnp.where(block == 3, tail, rotate(right, 96))], axis=1)
        return jnp.concatenate([lower, jnp.concatenate([left, right], axis=1), upper], axis=0).astype(BF16)

    def two_quads(step, carry):
        both = jnp.concatenate([stacked(step * 2), stacked(step * 2 + 1)], axis=1)
        blurred = jnp.dot(bzf_ref[...], both, preferred_element_type=F32).astype(BF16)
        for member in range(2):
            first = pl.multiple_of(step * 32 + member * 16, 16)
            for group in range(VIEWS * 4):
                planes_ref[group, pl.ds(first, 16), :] = blurred[
                    group * 16:(group + 1) * 16, member * ROWS:(member + 1) * ROWS]
        return carry

    lax.fori_loop(0, QUADS // 2, two_quads, 0, unroll=2)


def forward_plane(view, planes_ref, ky, kx):
    volume = planes_ref[pl.ds(view * 4, 4)].reshape(4 * ROWS, ROWS)
    along_x = jnp.concatenate([jnp.dot(volume[r * 512:(r + 1) * 512], kx, preferred_element_type=F32)
                               for r in range(2)], axis=0).astype(BF16)
    side = jnp.concatenate([along_x[r * ROWS:(r + 1) * ROWS] for r in range(4)], axis=1)
    return jnp.dot(ky, side, preferred_element_type=F32)


def adjoint_plane(view, quotient, kyt, kxt, depth_ref):
    along_y = jnp.dot(kyt, quotient.astype(BF16), preferred_element_type=F32).astype(BF16)
    stacked = jnp.concatenate([along_y[:, r * 128:(r + 1) * 128] for r in range(4)], axis=0)
    along_x = jnp.concatenate([jnp.dot(stacked[r * 512:(r + 1) * 512], kxt, preferred_element_type=F32)
                               for r in range(2)], axis=0).astype(BF16)
    for r in range(4):
        first = pl.multiple_of(view * 64 + r * 16, 16)
        for quad in range(QUADS):
            depth_ref[quad, pl.ds(first, 16), :] = along_x[r * ROWS + quad * 16:r * ROWS + quad * 16 + 16]


def adjoint_depth(scale, bza_ref, depth_ref, main_ref, tail_ref, to_left_ref, to_right_ref):
    block = lane_block((64, 128))
    low_half = block < 2

    def pair(quad, carry):
        tails = []
        members = (quad, quad + QUADS // 2)
        both = jnp.concatenate([depth_ref[member] for member in members], axis=1)
        summed_both = jnp.dot(bza_ref[...], both, preferred_element_type=F32)
        for index, member in enumerate(members):
            summed = summed_both[:, index * ROWS:(index + 1) * ROWS]
            mains = []
            for half in range(2):
                lanes = slice(half * 128, (half + 1) * 128)
                lower = jnp.where(block < 3, rotate(summed[:64, lanes], 96), 0.0)
                upper = jnp.where(block > 0, rotate(summed[128:, lanes], 32), 0.0)
                mains.append(summed[64:128, lanes] + lower + upper)
            tail = jnp.where(block == 0, summed[:64, :128], summed[128:, 128:])
            tail = jnp.where(block == 1, rotate(summed[128:, :128], 64), tail)
            tail = jnp.where(block == 2, rotate(summed[:64, 128:], 64), tail)
            rows = pl.ds(pl.multiple_of(member * 64, 64), 64)
            main_ref[0, rows, :] = mains[0]
            main_ref[1, rows, :] = mains[1]
            tail_ref[member] = tail
            to_left_ref[member] = to_fixed(mains[0], scale)
            to_right_ref[member] = to_fixed(mains[1], scale)
            tails.append(tail)
        to_left_ref[QUADS + quad] = to_fixed(jnp.where(low_half, tails[0], rotate(tails[1], 64)), scale)
        to_right_ref[QUADS + quad] = to_fixed(jnp.where(low_half, rotate(tails[0], 64), tails[1]), scale)
        return carry

    lax.fori_loop(0, QUADS // 2, pair, 0, unroll=2)


def tall(value):
    return jnp.concatenate([value] * 8, axis=0)


def forward_kernel(edge_ref, main_ref, from_low_ref, from_high_ref, bzf_ref, ky_ref, kx_ref, out_ref, tail_ref,
                   planes_ref):
    build_tail(edge_ref, from_low_ref, from_high_ref, tail_ref)
    forward_depth(main_ref, tail_ref, bzf_ref, planes_ref)

    def one_view(view, carry):
        out_ref[view] = forward_plane(view, planes_ref, ky_ref[view], kx_ref[view]).astype(BF16)
        return carry

    lax.fori_loop(0, VIEWS, one_view, 0)


def forward(edges, main, from_low, from_high, bzf, ky, kx):
    return pl.pallas_call(
        forward_kernel,
        out_shape=(
            jax.ShapeDtypeStruct((VIEWS, ROWS, 2 * ROWS), BF16),
            jax.ShapeDtypeStruct((QUADS, 64, 128), F32),
        ),
        in_specs=smem(1) + vmem(6),
        out_specs=tuple(vmem(2)),
        scratch_shapes=[pltpu.VMEM((VIEWS * 4, ROWS, ROWS), BF16)],
        name="forward",
    )(edges, main, from_low, from_high, bzf, ky, kx)


def per_view(*shape):
    return pl.BlockSpec((1,) + shape, lambda view: (view,) + (0,) * len(shape))


PARTIAL_SHAPES = (
    jax.ShapeDtypeStruct((2, 1024, 128), F32),
    jax.ShapeDtypeStruct((QUADS, 64, 128), F32),
    jax.ShapeDtypeStruct((QUADS + QUADS // 2, 64, 128), I16),
    jax.ShapeDtypeStruct((QUADS + QUADS // 2, 64, 128), I16),
)


def first_adjoint_kernel(start_ref, source_ref, place_ref, inverse_ref, offset_ref, incoming_ref, blurred_ref, kyt_ref,
                         kxt_ref, bza_ref, main_ref, tail_ref, to_left_ref, to_right_ref, average_ref, total_ref,
                         depth_ref, swap_ref):
    view = pl.program_id(0)

    @pl.when(view == 0)
    def _():
        swap_ref[...] = digit_swap((512, 512))

    for slot in range(SLOTS):
        total_ref[slot] = jnp.zeros((NY, 128), F32)

    def add(entry, carry):
        place = place_ref[entry]
        piece = incoming_ref[source_ref[entry] - view * incoming_ref.shape[0]].astype(F32)
        slot = place - view * SLOTS
        total_ref[slot] = total_ref[slot] + piece * inverse_ref[place]
        return carry

    lax.fori_loop(start_ref[view], start_ref[view + 1], add, 0)
    rows = []
    for r in range(4):
        rows.append(jnp.concatenate([total_ref[h * 4 + r].astype(BF16) for h in range(4)], axis=1))
    mixed = jnp.dot(jnp.concatenate(rows, axis=0), swap_ref[...], preferred_element_type=F32)
    for r in range(4):
        lanes = slice(r * 128, r * 128 + 128)
        for m in range(8):
            first = r * NY + m * 8
            ends = []
            for q in (0, 2):
                ends.append(swap_fours(mixed[first:first + 8, q * 128:(q + 1) * 128],
                                       mixed[first:first + 8, (q + 1) * 128:(q + 2) * 128]))
            for odd in range(2):
                quad = 2 * m + odd
                average_ref[0, quad * 16:quad * 16 + 16, lanes] = jnp.concatenate(
                    [ends[0][odd], ends[1][odd]], axis=0).astype(BF16)
    quotient = average_ref[0].astype(F32) / (blurred_ref[0].astype(F32) + offset_ref[view])
    adjoint_plane(view, quotient, kyt_ref[0], kxt_ref[0], depth_ref)

    @pl.when(view == VIEWS - 1)
    def _():
        scale = tall(32767.0 / partial_bound(offset_ref))
        adjoint_depth(scale, bza_ref, depth_ref, main_ref, tail_ref, to_left_ref, to_right_ref)


def first_adjoint(start, source, place, inverse, offset, incoming, blurred, kyt, kxt, bza):
    held = incoming.shape[0] // VIEWS
    return pl.pallas_call(
        first_adjoint_kernel,
        grid=(VIEWS,),
        out_shape=PARTIAL_SHAPES + (jax.ShapeDtypeStruct((VIEWS, ROWS, 2 * ROWS), BF16),),
        in_specs=smem(5) + [pl.BlockSpec((held, NY, 128), lambda view: (view, 0, 0)), per_view(ROWS, 2 * ROWS),
                            per_view(ROWS, ROWS), per_view(128, ROWS)] + vmem(1),
        out_specs=tuple(vmem(4)) + (per_view(ROWS, 2 * ROWS),),
        scratch_shapes=[pltpu.VMEM((SLOTS, NY, 128), F32), pltpu.VMEM((QUADS, VIEWS * 64, ROWS), BF16),
                        pltpu.VMEM((512, 512), BF16)],
        name="first_adjoint",
    )(start, source, place, inverse, offset, incoming, blurred, kyt, kxt, bza)


def join_columns_kernel(offset_ref, edge_ref, main_ref, tail_ref, from_left_ref, from_right_ref, out_main_ref, out_tail_ref,
                        low_ref, high_ref):
    block = lane_block((64, 128))
    low_half = block < 2
    bound = partial_bound(offset_ref)
    scale = tall(32767.0 / bound)
    left_step = tall(bound * (edge_ref[0] / 32767.0))
    right_step = tall(bound * (edge_ref[1] / 32767.0))

    def pair(quad, carry):
        packed_left = from_fixed(from_left_ref[QUADS + quad], left_step)
        packed_right = from_fixed(from_right_ref[QUADS + quad], right_step)
        for second, member in enumerate((quad, quad + QUADS // 2)):
            rows = pl.ds(pl.multiple_of(member * 64, 64), 64)
            left = main_ref[0, rows, :] + from_fixed(from_left_ref[member], left_step)
            right = main_ref[1, rows, :] + from_fixed(from_right_ref[member], right_step)
            if second:
                extra = jnp.where(low_half, rotate(packed_left, 64), packed_right)
            else:
                extra = jnp.where(low_half, packed_left, rotate(packed_right, 64))
            tail = tail_ref[member] + extra
            out_main_ref[0, rows, :] = left
            out_main_ref[1, rows, :] = right
            out_tail_ref[member] = tail
            low = jnp.where(block == 1, rotate(left, 32), tail)
            low = jnp.where(block == 3, rotate(right, 96), low)
            high = jnp.where(block == 0, rotate(left, 32), tail)
            high = jnp.where(block == 2, rotate(right, 96), high)
            low_ref[member] = to_fixed(low, scale)
            high_ref[member] = to_fixed(high, scale)
        return carry

    lax.fori_loop(0, QUADS // 2, pair, 0)


def join_columns(offset, edges, main, tail, from_left, from_right):
    return pl.pallas_call(
        join_columns_kernel,
        out_shape=(
            jax.ShapeDtypeStruct((2, 1024, 128), F32),
            jax.ShapeDtypeStruct((QUADS, 64, 128), F32),
            jax.ShapeDtypeStruct((QUADS, 64, 128), I16),
            jax.ShapeDtypeStruct((QUADS, 64, 128), I16),
        ),
        in_specs=smem(2) + vmem(4),
        out_specs=tuple(vmem(4)),
        name="join_columns",
    )(offset, edges, main, tail, from_left, from_right)


def joined_planes(quad, steps, block, main_ref, tail_ref, from_low_ref, from_high_ref):
    rows = pl.ds(pl.multiple_of(quad * 64, 64), 64)
    low = from_fixed(from_low_ref[quad], steps[0])
    high = from_fixed(from_high_ref[quad], steps[1])
    left = main_ref[0, rows, :]
    left = left + jnp.where(block == 0, rotate(low, 96), 0.0) + jnp.where(block == 3, rotate(high, 96), 0.0)
    right = main_ref[1, rows, :]
    right = right + jnp.where(block == 0, rotate(low, 32), 0.0) + jnp.where(block == 3, rotate(high, 32), 0.0)
    if tail_ref is None:
        return rows, left, right
    tail = tail_ref[quad] + jnp.where(block % 2 == 0, low, high)
    return rows, left, right, tail


def depth_steps(bound, edge_ref):
    return tall(bound * (edge_ref[2] / 32767.0)), tall(bound * (edge_ref[3] / 32767.0))


def second_kernel(offset_ref, edge_ref, part_main_ref, part_tail_ref, from_low_ref, from_high_ref, estimate_main_ref,
                  estimate_tail_ref, scale_main_ref, scale_tail_ref, bzf_ref, bza_ref, average_ref, ky_ref, kx_ref,
                  kyt_ref, kxt_ref, out_estimate_ref, main_ref, tail_ref, to_left_ref, to_right_ref, tail_estimate_ref,
                  planes_ref, depth_ref):
    view = pl.program_id(0)

    @pl.when(view == 0)
    def _():
        block = lane_block((64, 128))
        steps = depth_steps(partial_bound(offset_ref), edge_ref)

        def renew(quad, carry):
            rows, left, right, tail = joined_planes(
                quad, steps, block, part_main_ref, part_tail_ref, from_low_ref, from_high_ref)
            out_estimate_ref[0, rows, :] = estimate_main_ref[0, rows, :] * left * scale_main_ref[0, rows, :]
            out_estimate_ref[1, rows, :] = estimate_main_ref[1, rows, :] * right * scale_main_ref[1, rows, :]
            tail_estimate_ref[quad] = estimate_tail_ref[quad] * tail * scale_tail_ref[quad]
            return carry

        lax.fori_loop(0, QUADS, renew, 0)
        forward_depth(out_estimate_ref, tail_estimate_ref, bzf_ref, planes_ref)

    blurred = forward_plane(view, planes_ref, ky_ref[0], kx_ref[0]) + offset_ref[view]
    adjoint_plane(view, average_ref[0].astype(F32) / blurred, kyt_ref[0], kxt_ref[0], depth_ref)

    @pl.when(view == VIEWS - 1)
    def _():
        scale = tall(32767.0 / partial_bound(offset_ref))
        adjoint_depth(scale, bza_ref, depth_ref, main_ref, tail_ref, to_left_ref, to_right_ref)


def second(offset, edges, *operands):
    return pl.pallas_call(
        second_kernel,
        grid=(VIEWS,),
        out_shape=(jax.ShapeDtypeStruct((2, 1024, 128), F32),) + PARTIAL_SHAPES,
        in_specs=smem(2) + vmem(10) + [per_view(ROWS, 2 * ROWS), per_view(ROWS, ROWS), per_view(ROWS, 128),
                                       per_view(ROWS, ROWS), per_view(128, ROWS)],
        out_specs=tuple(vmem(5)),
        scratch_shapes=[pltpu.VMEM((QUADS, 64, 128), F32), pltpu.VMEM((VIEWS * 4, ROWS, ROWS), BF16),
                        pltpu.VMEM((QUADS, VIEWS * 64, ROWS), BF16)],
        name="second",
    )(offset, edges, *operands)


def finish_kernel(offset_ref, edge_ref, main_ref, from_low_ref, from_high_ref, estimate_ref, scale_ref, out_ref,
                  value_ref):
    block = lane_block((64, 128))
    lane = lax.broadcasted_iota(I32, (64, 128), 1) % PART
    steps = depth_steps(partial_bound(offset_ref), edge_ref)

    def one_quad(quad, largest):
        rows, left, right = joined_planes(quad, steps, block, main_ref, None, from_low_ref, from_high_ref)
        left = estimate_ref[0, rows, :] * left * scale_ref[0, rows, :]
        right = estimate_ref[1, rows, :] * right * scale_ref[1, rows, :]
        value = jnp.where(lane < HALO, rotate(left, 112), rotate(right, 16))
        value_ref[rows, :] = value
        return jnp.maximum(largest, value)

    largest = lax.fori_loop(0, QUADS, one_quad, jnp.zeros((64, 128), F32))
    unit = (jnp.max(largest) * 64.0).astype(I32) + 1
    vector = jnp.full((16, 128), unit, I32)
    out_ref[1024:1040, :] = (vector >> 15).astype(I16)
    out_ref[1040:1056, :] = (vector & 32767).astype(I16)
    factor = (32767.0 * 64.0) / tall(vector[:8].astype(F32))

    def round_quad(quad, carry):
        rows = pl.ds(pl.multiple_of(quad * 64, 64), 64)
        out_ref[rows, :] = to_fixed(value_ref[rows, :], factor)
        return carry

    lax.fori_loop(0, QUADS, round_quad, 0)


def finish(offset, edges, main, from_low, from_high, estimate, scale):
    return pl.pallas_call(
        finish_kernel,
        out_shape=jax.ShapeDtypeStruct((1056, 128), I16),
        in_specs=smem(2) + vmem(5),
        out_specs=vmem(1)[0],
        scratch_shapes=[pltpu.VMEM((1024, 128), F32)],
        name="finish",
    )(offset, edges, main, from_low, from_high, estimate, scale)


def assemble_kernel(index_ref, *refs):
    chunk_refs, out_ref, buffer_ref = refs[:8], refs[8], refs[9]
    part = index_ref[0]

    @pl.when(pl.program_id(0) == 0)
    def _():
        for place in range(8):
            owner = ((part // 2 + place % 4) % 4) * 2 + (part % 2 if place < 4 else 1 - part % 2)
            buffer_ref[owner] = chunk_refs[place][...]

    units = []
    for k in range(8):
        digits = buffer_ref[k, 1024:1040, :].astype(I32) * 32768 + buffer_ref[k, 1040:1056, :].astype(I32)
        units.append(digits.astype(F32) * (1.0 / (64.0 * 32767.0)))
    block = lane_block((8, 128))
    even = block % 2 == 0
    first = pl.multiple_of(pl.program_id(0) * 16, 16)

    def eight_rows(m, carry):
        low = pl.ds(pl.multiple_of(m * 128 + first, 16), 16)
        high = pl.ds(pl.multiple_of(m * 128 + 64 + first, 16), 16)
        for half in range(2):
            values = []
            for k in range(4):
                place = half * 4 + k
                below = from_fixed(buffer_ref[place, low, :], units[place])
                above = from_fixed(buffer_ref[place, high, :], units[place])
                values.append(swap_fours(below[:8], above[:8]) + swap_fours(below[8:], above[8:]))
            for j in range(4):
                c0, c1, c2, c3 = (values[k][j] for k in range(4))
                a0 = jnp.where(block < 2, c0, rotate(c2, 64))
                a1 = jnp.where(block < 2, c1, rotate(c3, 64))
                a2 = jnp.where(block < 2, rotate(c0, 64), c2)
                a3 = jnp.where(block < 2, rotate(c1, 64), c3)
                results = (jnp.where(even, a0, rotate(a1, 32)), jnp.where(even, rotate(a0, 96), a1),
                           jnp.where(even, a2, rotate(a3, 32)), jnp.where(even, rotate(a2, 96), a3))
                for h in range(4):
                    out_ref[h, 0, j, pl.ds(pl.multiple_of(m * 8, 8), 8), half * 128:(half + 1) * 128] = results[h]
        return carry

    lax.fori_loop(0, 8, eight_rows, 0)


def assemble(index, chunks):
    return pl.pallas_call(
        assemble_kernel,
        grid=(4,),
        out_shape=jax.ShapeDtypeStruct((4, 4, 4, NY, 256), F32),
        in_specs=smem(1) + vmem(8),
        out_specs=pl.BlockSpec((4, 1, 4, NY, 256), lambda step: (0, step, 0, 0, 0)),
        scratch_shapes=[pltpu.VMEM((VIEWS, 1056, 128), I16)],
        name="assemble",
    )(index, *chunks).reshape(64, NY, 256)


def to_neighbours(upward, downward, axis):
    count = lax.axis_size(axis)
    from_low = lax.ppermute(upward, axis, [(i, (i + 1) % count) for i in range(count)])
    from_high = lax.ppermute(downward, axis, [((i + 1) % count, i) for i in range(count)])
    return from_low, from_high


def gather_parts(own):
    parts = [own] + [
        lax.ppermute(own, "view", [((i + 2 * step) % VIEWS, i) for i in range(VIEWS)]) for step in (1, 3, 2)
    ]
    parts = [parts[0], parts[1], parts[3], parts[2]]
    return parts, [lax.ppermute(part, "view", [(i, i ^ 1) for i in range(VIEWS)]) for part in parts]


def column_sums(kernel, shift, positions, length):
    radius = (TAPS - 1) // 2
    source = (positions[None, :, None] - shift[:, None, None]
              - jnp.arange(TAPS, dtype=I32)[None, None, :] + radius)
    inside = (source >= 0) & (source < length)
    return jnp.sum(jnp.where(inside, kernel[:, None, :], 0.0), axis=2)


def program(estimate0, pieces, dest_block, slot_index, psf_shift, psf_taps, background):
    block_count = lax.axis_size("block")
    my_view = lax.axis_index("view")
    my_block = lax.axis_index("block")
    edges = jnp.stack([my_view > 0, my_view < VIEWS - 1, my_block > 0, my_block < block_count - 1]).astype(F32)
    targets = dest_block[:, :, 0].reshape(VIEWS, block_count, SLOTS)
    slots = slot_index.reshape(VIEWS, block_count, SLOTS)

    index = my_view.reshape(1).astype(I32)
    low, high = window_ends(index, estimate0)
    from_low, from_high = to_neighbours(high, low, "block")

    own_targets = lax.dynamic_slice(targets, (my_view, my_block, 0), (1, 1, SLOTS)).reshape(SLOTS)
    own_targets, low, high = lax.optimization_barrier((own_targets, low, high))
    outgoing = pack_pieces(own_targets, pieces[0], block_count)
    incoming = lax.all_to_all(outgoing.reshape(VIEWS * block_count, CAP, NY, 128), ("view", "block"), 0, 0, tiled=True)
    incoming = incoming.reshape(VIEWS * block_count * CAP, NY, 128)

    main = window_estimate(index, estimate0)
    kernel = psf_taps / jnp.sum(psf_taps, axis=2, keepdims=True)
    ky, kyt, kx, kxt, bzf, bza = build_bands(kernel.reshape(-1), psf_shift.reshape(-1))
    blurred, tail = forward(edges, main, from_low, from_high, bzf, ky, kx)

    earlier = jnp.tril(jnp.ones((SLOTS, SLOTS), jnp.bool_), -1)
    same = (targets[:, :, :, None] == targets[:, :, None, :]) & earlier[None, None]
    ranks = jnp.sum(same.astype(I32), axis=3)
    mine = targets == my_block
    received = jnp.arange(CAP, dtype=I32)
    slot_of = jnp.sum(
        jnp.where(mine[..., None] & (ranks[..., None] == received), slots[..., None] + 1, 0), axis=2
    ).reshape(VIEWS, block_count * CAP) - 1
    hits = slot_of[:, :, None] == jnp.arange(SLOTS, dtype=I32)
    counts = jnp.sum(hits.astype(I32), axis=1)
    inverse = 1.0 / jnp.maximum(counts, 1).astype(F32)
    entries = VIEWS * block_count * CAP
    number = jnp.arange(entries, dtype=I32)
    place_of = jnp.where(slot_of >= 0, slot_of + jnp.arange(VIEWS, dtype=I32)[:, None] * SLOTS, -1).reshape(entries)
    before = (place_of[None, :] >= 0) & (number[None, :] < number[:, None])
    position = jnp.where(place_of >= 0, jnp.sum(before.astype(I32), axis=1), -1)
    chosen = position[:, None] == number[None, :]
    source = jnp.sum(jnp.where(chosen, number[:, None], 0), axis=0)
    place = jnp.sum(jnp.where(chosen, place_of[:, None], 0), axis=0)
    start = jnp.sum(((place_of >= 0)[:, None]
                     & (number[:, None] // (block_count * CAP) < jnp.arange(VIEWS + 1))).astype(I32), axis=0)

    global_slot = (targets * SLOTS + slots).reshape(VIEWS, block_count * SLOTS)
    all_slots = jnp.arange(block_count * SLOTS, dtype=I32)
    occupied = jnp.any(global_slot[:, :, None] == all_slots, axis=1)
    mask = jnp.repeat(occupied.astype(F32), 4, axis=1)
    padded = jnp.pad(mask, ((0, 0), (2 * HALO, 2 * HALO)))
    window = lax.dynamic_slice_in_dim(padded, my_block * 64, 128, 1)
    depth = lax.broadcasted_iota(I32, (96, 128), 0) + HALO - lax.broadcasted_iota(I32, (96, 128), 1)
    tap = depth[None] - psf_shift[:, 0, None, None] + (TAPS - 1) // 2
    weight_depth = jnp.zeros((VIEWS, 96), F32)
    band = jnp.zeros((VIEWS, 96, 128), F32)
    for j in range(TAPS):
        band = jnp.where(tap == j, kernel[:, 0, j, None, None], band)
    weight_depth = jnp.sum(band * window[:, None, :], axis=2)
    weight_rows = column_sums(kernel[:, 1], psf_shift[:, 1], jnp.arange(NY, dtype=I32), NY)
    columns = my_view * PART - HALO + jnp.arange(2 * PART, dtype=I32)
    weight_columns = column_sums(kernel[:, 2], psf_shift[:, 2], columns, 256).reshape(VIEWS, 2, PART)
    by_group = weight_depth.reshape(VIEWS, 6, 16)
    planes = by_group[:, :, :, None, None] * weight_columns[:, None, None, :, :]
    planes = planes.transpose(0, 3, 2, 1, 4)
    weight_main = planes[:, :, :, 1:5].reshape(VIEWS, 2, 16, 128)
    weight_tail = jnp.stack([planes[:, :, :, 0], planes[:, :, :, 5]], axis=3)
    weight_tail = weight_tail.transpose(0, 2, 1, 3, 4).reshape(VIEWS, 16, 128)
    scale_main, scale_tail = build_weights(
        weight_rows.reshape(-1), jnp.repeat(weight_main, 4, axis=2), jnp.repeat(weight_tail, 4, axis=1))

    part_main, part_tail, to_left, to_right, average = first_adjoint(
        start, source, place, inverse.reshape(-1), background, incoming, blurred, kyt, kxt, bza)
    from_left, from_right = to_neighbours(to_right, to_left, "view")
    part_main, part_tail, low, high = join_columns(background, edges, part_main, part_tail, from_left, from_right)
    from_low, from_high = to_neighbours(high, low, "block")

    main, part_main, part_tail, to_left, to_right = second(
        background, edges, part_main, part_tail, from_low, from_high, main, tail, scale_main, scale_tail,
        bzf, bza, average, ky, kx, kyt, kxt)
    from_left, from_right = to_neighbours(to_right, to_left, "view")
    part_main, part_tail, low, high = join_columns(background, edges, part_main, part_tail, from_left, from_right)
    from_low, from_high = to_neighbours(high, low, "block")
    own = finish(background, edges, part_main, from_low, from_high, main, scale_main)

    mine, partners = gather_parts(own)
    return assemble(index, mine + partners)


def solution(mesh):
    return jax.shard_map(
        program,
        mesh=mesh,
        in_specs=(
            P("block", None, None),
            P("view", "block", None, None, None),
            P(),
            P(),
            P(),
            P(),
            P(),
        ),
        out_specs=P("block", None, None),
        check_vma=False,
    )
```

time: 289 us -> 195 us (0.67)
  the two profiles are of different devices: /device:TPU:15 before, /device:TPU:0 now
where the time goes in v2:
time: 195 us; the launch traced here: 193 us
  Pallas kernels  91.2 us (47%)
  waiting for transfers between devices  43.6 us (22%)
  starting transfers between devices  37 us (19%)
  local copies, waits for them, and re-layouts  12.9 us (7%)
  other arithmetic  7.59 us (4%)
    ppermute x5, starting transfers between devices, to_neighbours(): lax.ppermute(downward, axis, [((i + 1) % count, i) for i in range(count)])  19.4 us
    pallas_call x1, Pallas kernels, second(): pl.pallas_call(second_kernel, grid=(VIEWS,), out_shape=(jax.ShapeDtypeStr...  19.1 us
    all_to_all x1, waiting for transfers between devices, program(): lax.all_to_all(outgoing.reshape(VIEWS * block_count, CAP, NY, 128), ('vie...  16.2 us
    ppermute x5, waiting for transfers between devices, to_neighbours(): lax.ppermute(upward, axis, [(i, (i + 1) % count) for i in range(count)])  15.7 us
    pallas_call x1, Pallas kernels, first_adjoint(): pl.pallas_call(first_adjoint_kernel, grid=(VIEWS,), out_shape=PARTIAL_SHA...  14 us
    pallas_call x1, Pallas kernels, forward(): pl.pallas_call(forward_kernel, out_shape=(jax.ShapeDtypeStruct((VIEWS, RO...  10.3 us
    ppermute x3, waiting for transfers between devices, gather_parts(): lax.ppermute(own, 'view', [((i + 2 * step) % VIEWS, i) for i in range(VIE...  10.2 us
    pallas_call x1, Pallas kernels, assemble(): pl.pallas_call(assemble_kernel, grid=(4,), out_shape=jax.ShapeDtypeStruct...  9.01 us
  transfers between devices with their start and end apart: 18, of which 7 were waited for; matrix products, arithmetic and copies ran while one was open for 8% of the time, Pallas kernels for 17%

profile of v2, /device:TPU:0, one launch (start us, length us, event | category | flops | bytes accessed | tf_op | source)
XLA Modules:
  0.0 192.7 jit_solution(7890824713510931705)
XLA Ops:
  0.0 2.8 %ends.1 = (bf16[8,64,128]{2,1,0:T(8,128)(2,1)}, bf16[8,64,128]{2,1,0:T(8,128)(2,1)}) custom-call(s32[1]{0:T(128)} %bitcast.index_ref, f32[64,64,256]{2,1,0:T(8,128)} %estimate_ref.1, f32[64,64,256]{2,1,0:T(8,128)} %estimate_ref.1), custom_call_target="tpu_custom_call" | custom-call | tf_op jit(solution)/shard_map/ends/pallas_call | solution.py:242
  2.8 1.6 collective-permute-start
  4.4 4.7 %collective-permute-start.1 = (bf16[8,64,128]{2,1,0:T(8,128)(2,1)}, bf16[8,64,128]{2,1,0:T(8,128)(2,1)S(1)}, u32[]{:S(2)}, u32[]{:S(2)}) collective-permute-start(bf16[8,64,128]{2,1,0:T(8,128)(2,1)} %get-tuple-element.35), channel_id=1, source_target_pairs={{1,0},{2,1},{3,2},{4,3},{5,4},{6,5},{7,6},{8,7},{9,8},{10,9},{11,1... | collective-permute-start | bytes 393224 | tf_op jit(solution)/shard_map/ppermute | solution.py:697
  9.3 0.6 dynamic-slice_bitcast_fusion.target_ref
  9.9 5.5 %pack.1 = bf16[8,32,64,128]{3,2,1,0:T(8,128)(2,1)} custom-call(s32[16]{0:T(128)} %dynamic-slice_bitcast_fusion.target_ref, bf16[16,4,64,256]{3,2,1,0:T(8,128)(2,1)} %bitcast.37), custom_call_target="tpu_custom_call" | custom-call | tf_op jit(solution)/shard_map/pack/pallas_call | solution.py:168
  15.4 7.4 %all-to-all-start = ((bf16[128,2,64,128]{3,2,1,0:T(8,128)(2,1)}), bf16[128,2,64,128]{3,2,1,0:T(8,128)(2,1)}, u32[]{:S(2)}, u32[]{:S(2)}) async-start(bf16[128,2,64,128]{3,2,1,0:T(8,128)(2,1)} %bitcast.36), calls=%async_computation | async-start | bytes 8388608 | tf_op jit(solution)/shard_map/all_to_all | solution.py:732
  22.9 2.5 %convert_reduce_fusion = s32[8,16,16]{2,1,0:T(8,128)S(1)} fusion(s32[8,16,16]{2,1,0:T(8,128)S(1)} %reshape_squeeze.3, pred[16,16]{1,0:T(8,128)(4,1)S(1)} %iota_compare_fusion.6), kind=kLoop, calls=%fused_computation.2 | loop fusion | flops 129024 | bytes 16640 | tf_op jit(solution)/shard_map/reduce_sum | solution.py:742
  25.6 0.4 select_reduce_fusion.2
  25.9 0.1 copy.32
  26.1 0.1 sub.102
  26.5 0.4 fusion
  27.4 0.2 slice_reduce_fusion.19
  27.6 0.6 convert_reduce_fusion.3.start_ref
  28.3 0.2 convert_reduce_fusion.2
  28.5 0.5 slice_reduce_fusion.20
  29.3 0.8 multiply_reduce_fusion
  30.1 0.7 add_convert_fusion.edge_ref
  30.7 6.0 %window.1.main_ref.estimate_main_ref = f32[2,1024,128]{2,1,0:T(8,128)} custom-call(s32[1]{0:T(128)} %bitcast.index_ref, f32[64,64,256]{2,1,0:T(8,128)} %estimate_ref.1), custom_call_target="tpu_custom_call" | custom-call | tf_op jit(solution)/shard_map/window/pallas_call | solution.py:205
  36.8 0.7 reshape.270.taps_ref
  37.5 0.6 reshape.271.shift_ref
  38.1 0.6 div.30.inverse_ref
  38.7 6.8 %bands.1 = (bf16[8,256,256]{2,1,0:T(8,128)(2,1)}, bf16[8,256,256]{2,1,0:T(8,128)(2,1)}, bf16[8,256,128]{2,1,0:T(8,128)(2,1)}, bf16[8,128,256]{2,1,0:T(8,128)(2,1...) custom-call(f32[504]{0:T(512)} %reshape.270.taps_ref, s32[24]{0:T(128)} %reshape.271.shift_ref), custom_call_target="tpu_custom_call" | custom-call | tf_op jit(solution)/shard_map/bands/pallas_call | solution.py:124
  45.5 0.7 select_reduce_fusion
  46.2 0.6 copy-done.15
  46.9 10.3 %forward.1 = (bf16[8,256,512]{2,1,0:T(8,128)(2,1)}, f32[16,64,128]{2,1,0:T(8,128)}) custom-call(f32[4]{0:T(128)} %add_convert_fusion.edge_ref, f32[2,1024,128]{2,1,0:T(8,128)} %window.1.main_ref.estimate_main_ref, bf16[8,64,128]{2,1,0:T(8,128)(2,1)} %copy-done.15, bf16[8,64,128]{2,1,0:T(8,128)(2,1)} %copy-done.16, ...), custom_call_target="tpu_custom_call" | custom-call | tf_op jit(solution)/shard_map/forward/pallas_call | solution.py:401
  57.3 16.2 %all-to-all-done = bf16[128,2,64,128]{3,2,1,0:T(8,128)(2,1)} async-done(((bf16[128,2,64,128]{3,2,1,0:T(8,128)(2,1)}), bf16[128,2,64,128]{3,2,1,0:T(8,128)(2,1)}, u32[]{:S(2)}, u32[]{:S(2)}) %all-to-all-start) | async-done | bytes 4194336 | tf_op jit(solution)/shard_map/all_to_all | solution.py:732
  73.5 14.0 %first_adjoint.1 = (f32[2,1024,128]{2,1,0:T(8,128)}, f32[16,64,128]{2,1,0:T(8,128)}, s16[24,64,128]{2,1,0:T(8,128)(2,1)}, s16[24,64,128]{2,1,0:T(8,128)(2,1)}, bf16[8,256,512]{2,1,0:T(8,128)(2,1)}) custom-call(s32[9]{0:T(128)} %convert_reduce_fusion.3.start_ref, s32[256]{0:T(256)} %get-tuple-element.87.source_ref, s32[256]{0:T(256)} %get-tuple-element.86.place_ref, ...), custom_call_target="tpu_custom_call" | custom-call | tf_op jit(solution)/shard_map/first_adjoint/pallas_call | solution.py:473
  87.6 2.9 %collective-permute-start.3 = (s16[24,64,128]{2,1,0:T(8,128)(2,1)}, s16[24,64,128]{2,1,0:T(8,128)(2,1)S(1)}, u32[]{:S(2)}, u32[]{:S(2)}) collective-permute-start(s16[24,64,128]{2,1,0:T(8,128)(2,1)} %get-tuple-element.48), channel_id=1, source_target_pairs={{16,0},{32,16},{48,32},{64,48},{80,64},{96,80},{112,96},{0,112},{1... | collective-permute-start | bytes 1179656 | tf_op jit(solution)/shard_map/ppermute | solution.py:697
  90.7 0.1 copy.41
  91.1 0.2 broadcast_multiply_fusion
  91.3 4.9 %collective-permute-done.2.from_left_ref = s16[24,64,128]{2,1,0:T(8,128)(2,1)S(1)} collective-permute-done((s16[24,64,128]{2,1,0:T(8,128)(2,1)}, s16[24,64,128]{2,1,0:T(8,128)(2,1)S(1)}, u32[]{:S(2)}, u32[]{:S(2)}) %collective-permute-start.2) | collective-permute-done | bytes 393248 | tf_op jit(solution)/shard_map/ppermute | solution.py:696
  96.2 0.7 copy-done
  96.9 0.1 copy-done.1
  97.1 3.9 %join_columns.2 = (f32[2,1024,128]{2,1,0:T(8,128)}, f32[16,64,128]{2,1,0:T(8,128)}, s16[16,64,128]{2,1,0:T(8,128)(2,1)}, s16[16,64,128]{2,1,0:T(8,128)(2,1)}) custom-call(f32[8]{0:T(128)} %offset_ref.9, f32[4]{0:T(128)} %add_convert_fusion.edge_ref, f32[2,1024,128]{2,1,0:T(8,128)} %get-tuple-element.45.main_ref, f32[16,64,128]{2,1,0:T(8,128)} %get-tuple-element.46.tail_ref, ...), custom_call_target="tpu_custom_call" | custom-call | tf_op jit(solution)/shard_map/join_columns/pallas_call | solution.py:522
  101.0 1.9 collective-permute-start.4
  102.9 3.4 %collective-permute-start.5 = (s16[16,64,128]{2,1,0:T(8,128)(2,1)}, s16[16,64,128]{2,1,0:T(8,128)(2,1)S(1)}, u32[]{:S(2)}, u32[]{:S(2)}) collective-permute-start(s16[16,64,128]{2,1,0:T(8,128)(2,1)} %get-tuple-element.52), channel_id=1, source_target_pairs={{1,0},{2,1},{3,2},{4,3},{5,4},{6,5},{7,6},{8,7},{9,8},{10,9},{11,1... | collective-permute-start | bytes 786440 | tf_op jit(solution)/shard_map/ppermute | solution.py:697
  106.4 0.2 fusion.32
  106.6 0.1 slice.145
  106.8 0.3 maximum_bitcast_fusion
  107.1 0.2 reshape.277
  107.3 0.3 reshape.280
  107.8 0.7 reshape.272.rows_ref
  108.5 0.7 broadcast_in_dim.296
  109.3 0.9 broadcast_in_dim.295
  110.2 3.8 %weights.1 = (f32[2,1024,128]{2,1,0:T(8,128)}, f32[16,64,128]{2,1,0:T(8,128)}) custom-call(f32[512]{0:T(512)} %reshape.272.rows_ref, f32[8,2,64,128]{3,2,1,0:T(8,128)} %bitcast.38, f32[8,64,128]{2,1,0:T(8,128)} %bitcast.40), custom_call_target="tpu_custom_call" | custom-call | tf_op jit(solution)/shard_map/weights/pallas_call | solution.py:291
  114.0 0.7 copy-done.11
  114.8 19.1 %second.1 = (f32[2,1024,128]{2,1,0:T(8,128)}, f32[2,1024,128]{2,1,0:T(8,128)}, f32[16,64,128]{2,1,0:T(8,128)}, s16[24,64,128]{2,1,0:T(8,128)(2,1)}, s16[24,64,128]{2,1,0:T(8,128)(2,1)}) custom-call(f32[8]{0:T(128)} %offset_ref.9, f32[4]{0:T(128)} %add_convert_fusion.edge_ref, f32[2,1024,128]{2,1,0:T(8,128)} %get-tuple-element.49.part_main_ref, ...), custom_call_target="tpu_custom_call" | custom-call | tf_op jit(solution)/shard_map/second/pallas_call | solution.py:586
  133.9 2.9 %collective-permute-start.7 = (s16[24,64,128]{2,1,0:T(8,128)(2,1)}, s16[24,64,128]{2,1,0:T(8,128)(2,1)S(1)}, u32[]{:S(2)}, u32[]{:S(2)}) collective-permute-start(s16[24,64,128]{2,1,0:T(8,128)(2,1)} %get-tuple-element.60), channel_id=1, source_target_pairs={{16,0},{32,16},{48,32},{64,48},{80,64},{96,80},{112,96},{0,112},{1... | collective-permute-start | bytes 1179656 | tf_op jit(solution)/shard_map/ppermute | solution.py:697
  136.9 5.7 %collective-permute-done.6.from_left_ref = s16[24,64,128]{2,1,0:T(8,128)(2,1)S(1)} collective-permute-done((s16[24,64,128]{2,1,0:T(8,128)(2,1)}, s16[24,64,128]{2,1,0:T(8,128)(2,1)S(1)}, u32[]{:S(2)}, u32[]{:S(2)}) %collective-permute-start.6) | collective-permute-done | bytes 393248 | tf_op jit(solution)/shard_map/ppermute | solution.py:696
  142.6 0.7 copy-done.2
  143.3 0.2 copy-done.3
  143.5 3.9 %join_columns.3 = (f32[2,1024,128]{2,1,0:T(8,128)}, f32[16,64,128]{2,1,0:T(8,128)}, s16[16,64,128]{2,1,0:T(8,128)(2,1)}, s16[16,64,128]{2,1,0:T(8,128)(2,1)}) custom-call(f32[8]{0:T(128)} %offset_ref.9, f32[4]{0:T(128)} %add_convert_fusion.edge_ref, f32[2,1024,128]{2,1,0:T(8,128)} %get-tuple-element.57.main_ref, f32[16,64,128]{2,1,0:T(8,128)} %get-tuple-element.58.tail_ref, ...), custom_call_target="tpu_custom_call" | custom-call | tf_op jit(solution)/shard_map/join_columns/pallas_call | solution.py:522
  147.4 5.3 %collective-permute-start.9 = (s16[16,64,128]{2,1,0:T(8,128)(2,1)}, s16[16,64,128]{2,1,0:T(8,128)(2,1)S(1)}, u32[]{:S(2)}, u32[]{:S(2)}) collective-permute-start(s16[16,64,128]{2,1,0:T(8,128)(2,1)} %get-tuple-element.63), channel_id=1, source_target_pairs={{1,0},{2,1},{3,2},{4,3},{5,4},{6,5},{7,6},{8,7},{9,8},{10,9},{11,1... | collective-permute-start | bytes 786440 | tf_op jit(solution)/shard_map/ppermute | solution.py:697
  152.8 5.1 %collective-permute-done.8.from_low_ref = s16[16,64,128]{2,1,0:T(8,128)(2,1)S(1)} collective-permute-done((s16[16,64,128]{2,1,0:T(8,128)(2,1)}, s16[16,64,128]{2,1,0:T(8,128)(2,1)S(1)}, u32[]{:S(2)}, u32[]{:S(2)}) %collective-permute-start.8) | collective-permute-done | bytes 262176 | tf_op jit(solution)/shard_map/ppermute | solution.py:696
  157.9 0.7 copy-done.13
  158.7 5.9 %finish.1.refs_0_ = s16[1056,128]{1,0:T(8,128)(2,1)} custom-call(f32[8]{0:T(128)} %offset_ref.9, f32[4]{0:T(128)} %add_convert_fusion.edge_ref, f32[2,1024,128]{2,1,0:T(8,128)} %get-tuple-element.61.main_ref, s16[16,64,128]{2,1,0:T(8,128)(2,1)} %copy-done.13, s16[16,64,128]{2,1,0:T(8,128)(2,1)} %copy-done.14, ...), custom_call_target="tpu_custom_call" | custom-call | tf_op jit(solution)/shard_map/finish/pallas_call | solution.py:629
  164.6 2.6 %collective-permute-start.11 = (s16[1056,128]{1,0:T(8,128)(2,1)}, s16[1056,128]{1,0:T(8,128)(2,1)S(1)}, u32[]{:S(2)}, u32[]{:S(2)}) collective-permute-start(s16[1056,128]{1,0:T(8,128)(2,1)} %finish.1.refs_0_), channel_id=1, source_target_pairs={{64,0},{80,16},{96,32},{112,48},{0,64},{16,80},{32,96},{48,112},{6... | collective-permute-start | bytes 811016 | tf_op jit(solution)/shard_map/ppermute | solution.py:703
  167.2 0.4 collective-permute-start.12
  167.6 6.6 %collective-permute-done.10.refs_1_ = s16[1056,128]{1,0:T(8,128)(2,1)S(1)} collective-permute-done((s16[1056,128]{1,0:T(8,128)(2,1)}, s16[1056,128]{1,0:T(8,128)(2,1)S(1)}, u32[]{:S(2)}, u32[]{:S(2)}) %collective-permute-start.10) | collective-permute-done | bytes 270368 | tf_op jit(solution)/shard_map/ppermute | solution.py:703
  174.1 3.6 %collective-permute-start.14 = (s16[1056,128]{1,0:T(8,128)(2,1)S(1)}, s16[1056,128]{1,0:T(8,128)(2,1)S(1)}, u32[]{:S(2)}, u32[]{:S(2)}) collective-permute-start(s16[1056,128]{1,0:T(8,128)(2,1)S(1)} %collective-permute-done.10.refs_1_), channel_id=1, source_target_pairs={{0,16},{16,0},{32,48},{48,32},{64,80},{80,64},{96,112},{112,96},{1... | collective-permute-start | bytes 811016 | tf_op jit(solution)/shard_map/ppermute | solution.py:706
  177.8 3.6 %collective-permute-done.12.refs_3_ = s16[1056,128]{1,0:T(8,128)(2,1)S(1)} collective-permute-done((s16[1056,128]{1,0:T(8,128)(2,1)}, s16[1056,128]{1,0:T(8,128)(2,1)S(1)}, u32[]{:S(2)}, u32[]{:S(2)}) %collective-permute-start.12) | collective-permute-done | bytes 270368 | tf_op jit(solution)/shard_map/ppermute | solution.py:703
  181.5 1.5 collective-permute-done.16.refs_7_
  183.0 0.7 copy-done.10
  183.7 9.0 %assemble.1 = f32[4,4,4,64,256]{4,3,2,1,0:T(8,128)} custom-call(s32[1]{0:T(128)} %bitcast.index_ref, s16[1056,128]{1,0:T(8,128)(2,1)} %finish.1.refs_0_, s16[1056,128]{1,0:T(8,128)(2,1)} %copy-done.4, s16[1056,128]{1,0:T(8,128)(2,1)} %copy-done.5, s16[1056,128]{1,0:T(8,128)(2,1)} %copy-done.6, s16[1056,128]{1,0:T(8,128)(2,1)} %copy-done.7, ...), custom_call_target="tpu_custom_call" | custom-call | tf_op jit(solution)/shard_map/assemble/pallas_call | solution.py:683
  (93 shorter events, 2.5 us)
Async XLA Ops:
  0.0 9.2 %copy-start.19 = (s32[8,256,1]{1,2,0:T(1,128)S(1)}, s32[8,256,1]{1,2,0:T(1,128)}, u32[]{:S(2)}) copy-start(s32[8,256,1]{1,2,0:T(1,128)} %param.9) | copy-start | bytes 24580
  2.8 43.4 %collective-permute-start = (bf16[8,64,128]{2,1,0:T(8,128)(2,1)}, bf16[8,64,128]{2,1,0:T(8,128)(2,1)S(1)}, u32[]{:S(2)}, u32[]{:S(2)}) collective-permute-start(bf16[8,64,128]{2,1,0:T(8,128)(2,1)} %get-tuple-element.36), channel_id=1, source_target_pairs={{0,1},{1,2},{2,3},{3,4},{4,5},{5,6},{6,7},{7,8},{8,9},{9,10},{10,1... | collective-permute-start | bytes 393224 | tf_op jit(solution)/shard_map/ppermute | solution.py:696
  4.4 41.8 %collective-permute-start.1 = (bf16[8,64,128]{2,1,0:T(8,128)(2,1)}, bf16[8,64,128]{2,1,0:T(8,128)(2,1)S(1)}, u32[]{:S(2)}, u32[]{:S(2)}) collective-permute-start(bf16[8,64,128]{2,1,0:T(8,128)(2,1)} %get-tuple-element.35), channel_id=1, source_target_pairs={{1,0},{2,1},{3,2},{4,3},{5,4},{6,5},{7,6},{8,7},{9,8},{10,9},{11,1... | collective-permute-start | bytes 393224 | tf_op jit(solution)/shard_map/ppermute | solution.py:697
  15.4 7.5 %copy-start.18 = (s32[8,256]{1,0:T(8,128)S(1)}, s32[8,256]{1,0:T(8,128)}, u32[]{:S(2)}) copy-start(s32[8,256]{1,0:T(8,128)} %param.10) | copy-start | bytes 24580
  15.4 58.1 %all-to-all-start = ((bf16[128,2,64,128]{3,2,1,0:T(8,128)(2,1)}), bf16[128,2,64,128]{3,2,1,0:T(8,128)(2,1)}, u32[]{:S(2)}, u32[]{:S(2)}) async-start(bf16[128,2,64,128]{3,2,1,0:T(8,128)(2,1)} %bitcast.36), calls=%async_computation | async-start | bytes 8388608 | tf_op jit(solution)/shard_map/all_to_all | solution.py:732
  22.8 4.4 %copy-start.17 = (f32[8,3,21]{2,0,1:T(8,128)S(1)}, f32[8,3,21]{2,0,1:T(8,128)}, u32[]{:S(2)}) copy-start(f32[8,3,21]{2,0,1:T(8,128)} %param.12) | copy-start | bytes 6052
  22.8 6.3 %copy-start.20 = (s32[8,3]{0,1:T(4,128)S(1)}, s32[8,3]{0,1:T(4,128)}, u32[]{:S(2)}) copy-start(s32[8,3]{0,1:T(4,128)} %param.11) | copy-start | bytes 292
  46.2 0.6 copy-start.15
  46.2 0.7 copy-start.16
  87.6 8.6 %collective-permute-start.2 = (s16[24,64,128]{2,1,0:T(8,128)(2,1)}, s16[24,64,128]{2,1,0:T(8,128)(2,1)S(1)}, u32[]{:S(2)}, u32[]{:S(2)}) collective-permute-start(s16[24,64,128]{2,1,0:T(8,128)(2,1)} %get-tuple-element.47), channel_id=1, source_target_pairs={{0,16},{16,32},{32,48},{48,64},{64,80},{80,96},{96,112},{112,0},{1... | collective-permute-start | bytes 1179656 | tf_op jit(solution)/shard_map/ppermute | solution.py:696
  87.6 8.6 %collective-permute-start.3 = (s16[24,64,128]{2,1,0:T(8,128)(2,1)}, s16[24,64,128]{2,1,0:T(8,128)(2,1)S(1)}, u32[]{:S(2)}, u32[]{:S(2)}) collective-permute-start(s16[24,64,128]{2,1,0:T(8,128)(2,1)} %get-tuple-element.48), channel_id=1, source_target_pairs={{16,0},{32,16},{48,32},{64,48},{80,64},{96,80},{112,96},{0,112},{1... | collective-permute-start | bytes 1179656 | tf_op jit(solution)/shard_map/ppermute | solution.py:697
  96.2 0.7 copy-start
  96.2 0.9 copy-start.1
  101.0 13.0 %collective-permute-start.4 = (s16[16,64,128]{2,1,0:T(8,128)(2,1)}, s16[16,64,128]{2,1,0:T(8,128)(2,1)S(1)}, u32[]{:S(2)}, u32[]{:S(2)}) collective-permute-start(s16[16,64,128]{2,1,0:T(8,128)(2,1)} %get-tuple-element.51), channel_id=1, source_target_pairs={{0,1},{1,2},{2,3},{3,4},{4,5},{5,6},{6,7},{7,8},{8,9},{9,10},{10,1... | collective-permute-start | bytes 786440 | tf_op jit(solution)/shard_map/ppermute | solution.py:696
  102.9 11.1 %collective-permute-start.5 = (s16[16,64,128]{2,1,0:T(8,128)(2,1)}, s16[16,64,128]{2,1,0:T(8,128)(2,1)S(1)}, u32[]{:S(2)}, u32[]{:S(2)}) collective-permute-start(s16[16,64,128]{2,1,0:T(8,128)(2,1)} %get-tuple-element.52), channel_id=1, source_target_pairs={{1,0},{2,1},{3,2},{4,3},{5,4},{6,5},{7,6},{8,7},{9,8},{10,9},{11,1... | collective-permute-start | bytes 786440 | tf_op jit(solution)/shard_map/ppermute | solution.py:697
  114.0 0.7 copy-start.11
  114.0 0.8 copy-start.12
  133.9 8.6 %collective-permute-start.6 = (s16[24,64,128]{2,1,0:T(8,128)(2,1)}, s16[24,64,128]{2,1,0:T(8,128)(2,1)S(1)}, u32[]{:S(2)}, u32[]{:S(2)}) collective-permute-start(s16[24,64,128]{2,1,0:T(8,128)(2,1)} %get-tuple-element.59), channel_id=1, source_target_pairs={{0,16},{16,32},{32,48},{48,64},{64,80},{80,96},{96,112},{112,0},{1... | collective-permute-start | bytes 1179656 | tf_op jit(solution)/shard_map/ppermute | solution.py:696
  133.9 8.6 %collective-permute-start.7 = (s16[24,64,128]{2,1,0:T(8,128)(2,1)}, s16[24,64,128]{2,1,0:T(8,128)(2,1)S(1)}, u32[]{:S(2)}, u32[]{:S(2)}) collective-permute-start(s16[24,64,128]{2,1,0:T(8,128)(2,1)} %get-tuple-element.60), channel_id=1, source_target_pairs={{16,0},{32,16},{48,32},{64,48},{80,64},{96,80},{112,96},{0,112},{1... | collective-permute-start | bytes 1179656 | tf_op jit(solution)/shard_map/ppermute | solution.py:697
  142.6 0.7 copy-start.2
  142.6 0.9 copy-start.3
  147.4 10.4 %collective-permute-start.8 = (s16[16,64,128]{2,1,0:T(8,128)(2,1)}, s16[16,64,128]{2,1,0:T(8,128)(2,1)S(1)}, u32[]{:S(2)}, u32[]{:S(2)}) collective-permute-start(s16[16,64,128]{2,1,0:T(8,128)(2,1)} %get-tuple-element.62), channel_id=1, source_target_pairs={{0,1},{1,2},{2,3},{3,4},{4,5},{5,6},{6,7},{7,8},{8,9},{9,10},{10,1... | collective-permute-start | bytes 786440 | tf_op jit(solution)/shard_map/ppermute | solution.py:696
  147.4 10.4 %collective-permute-start.9 = (s16[16,64,128]{2,1,0:T(8,128)(2,1)}, s16[16,64,128]{2,1,0:T(8,128)(2,1)S(1)}, u32[]{:S(2)}, u32[]{:S(2)}) collective-permute-start(s16[16,64,128]{2,1,0:T(8,128)(2,1)} %get-tuple-element.63), channel_id=1, source_target_pairs={{1,0},{2,1},{3,2},{4,3},{5,4},{6,5},{7,6},{8,7},{9,8},{10,9},{11,1... | collective-permute-start | bytes 786440 | tf_op jit(solution)/shard_map/ppermute | solution.py:697
  157.9 0.7 copy-start.13
  157.9 0.8 copy-start.14
  164.6 9.6 %collective-permute-start.10 = (s16[1056,128]{1,0:T(8,128)(2,1)}, s16[1056,128]{1,0:T(8,128)(2,1)S(1)}, u32[]{:S(2)}, u32[]{:S(2)}) collective-permute-start(s16[1056,128]{1,0:T(8,128)(2,1)} %finish.1.refs_0_), channel_id=1, source_target_pairs={{32,0},{48,16},{64,32},{80,48},{96,64},{112,80},{0,96},{16,112},{3... | collective-permute-start | bytes 811016 | tf_op jit(solution)/shard_map/ppermute | solution.py:703
  164.6 13.1 %collective-permute-start.11 = (s16[1056,128]{1,0:T(8,128)(2,1)}, s16[1056,128]{1,0:T(8,128)(2,1)S(1)}, u32[]{:S(2)}, u32[]{:S(2)}) collective-permute-start(s16[1056,128]{1,0:T(8,128)(2,1)} %finish.1.refs_0_), channel_id=1, source_target_pairs={{64,0},{80,16},{96,32},{112,48},{0,64},{16,80},{32,96},{48,112},{6... | collective-permute-start | bytes 811016 | tf_op jit(solution)/shard_map/ppermute | solution.py:703
  167.2 14.3 %collective-permute-start.12 = (s16[1056,128]{1,0:T(8,128)(2,1)}, s16[1056,128]{1,0:T(8,128)(2,1)S(1)}, u32[]{:S(2)}, u32[]{:S(2)}) collective-permute-start(s16[1056,128]{1,0:T(8,128)(2,1)} %finish.1.refs_0_), channel_id=1, source_target_pairs={{96,0},{112,16},{0,32},{16,48},{32,64},{48,80},{64,96},{80,112},{9... | collective-permute-start | bytes 811016 | tf_op jit(solution)/shard_map/ppermute | solution.py:703
  167.6 13.9 %collective-permute-start.13 = (s16[1056,128]{1,0:T(8,128)(2,1)}, s16[1056,128]{1,0:T(8,128)(2,1)S(1)}, u32[]{:S(2)}, u32[]{:S(2)}) collective-permute-start(s16[1056,128]{1,0:T(8,128)(2,1)} %finish.1.refs_0_), channel_id=1, source_target_pairs={{0,16},{16,0},{32,48},{48,32},{64,80},{80,64},{96,112},{112,96},{1... | collective-permute-start | bytes 811016 | tf_op jit(solution)/shard_map/ppermute | solution.py:706
  174.1 8.9 %copy-start.4 = (s16[1056,128]{1,0:T(8,128)(2,1)}, s16[1056,128]{1,0:T(8,128)(2,1)S(1)}, u32[]{:S(2)}) copy-start(s16[1056,128]{1,0:T(8,128)(2,1)S(1)} %collective-permute-done.10.refs_1_) | copy-start | bytes 811012
  174.1 7.3 %collective-permute-start.14 = (s16[1056,128]{1,0:T(8,128)(2,1)S(1)}, s16[1056,128]{1,0:T(8,128)(2,1)S(1)}, u32[]{:S(2)}, u32[]{:S(2)}) collective-permute-start(s16[1056,128]{1,0:T(8,128)(2,1)S(1)} %collective-permute-done.10.refs_1_), channel_id=1, source_target_pairs={{0,16},{16,0},{32,48},{48,32},{64,80},{80,64},{96,112},{112,96},{1... | collective-permute-start | bytes 811016 | tf_op jit(solution)/shard_map/ppermute | solution.py:706
  177.7 5.3 %copy-start.5 = (s16[1056,128]{1,0:T(8,128)(2,1)}, s16[1056,128]{1,0:T(8,128)(2,1)S(1)}, u32[]{:S(2)}) copy-start(s16[1056,128]{1,0:T(8,128)(2,1)S(1)} %collective-permute-done.11.refs_2_) | copy-start | bytes 811012
  177.7 3.8 %collective-permute-start.15 = (s16[1056,128]{1,0:T(8,128)(2,1)S(1)}, s16[1056,128]{1,0:T(8,128)(2,1)S(1)}, u32[]{:S(2)}, u32[]{:S(2)}) collective-permute-start(s16[1056,128]{1,0:T(8,128)(2,1)S(1)} %collective-permute-done.11.refs_2_), channel_id=1, source_target_pairs={{0,16},{16,0},{32,48},{48,32},{64,80},{80,64},{96,112},{112,96},{1... | collective-permute-start | bytes 811016 | tf_op jit(solution)/shard_map/ppermute | solution.py:706
  181.4 1.6 copy-start.6
  181.4 1.5 collective-permute-start.16
  181.5 1.5 copy-start.7
  181.5 1.5 copy-start.8
  181.5 1.5 copy-start.9
  183.0 0.7 copy-start.10

commit v3 on v2

--- a/solution.py
+++ b/solution.py
@@ -41,6 +41,18 @@
     upper = lax.broadcasted_iota(I32, first.shape, 0) < 4
     return (jnp.where(upper, first, pltpu.roll(second, 4, 0)),
             jnp.where(upper, pltpu.roll(first, 4, 0), second))
+
+
+def held(shape, dtype):
+    return pltpu.VMEM(shape, dtype)
+
+
+def stay(*arrays):
+    return tuple(pltpu.with_memory_space_constraint(array, pltpu.VMEM) for array in arrays)
+
+
+def room(mebibytes):
+    return pltpu.CompilerParams(vmem_limit_bytes=mebibytes << 20)
 
 
 def vmem(count):
@@ -347,9 +359,15 @@
             depth_ref[quad, pl.ds(first, 16), :] = along_x[r * ROWS + quad * 16:r * ROWS + quad * 16 + 16]
 
 
-def adjoint_depth(scale, bza_ref, depth_ref, main_ref, tail_ref, to_left_ref, to_right_ref):
+def own_lanes(left, right):
+    lane = lax.broadcasted_iota(I32, left.shape, 1) % PART
+    return jnp.where(lane < HALO, rotate(left, 112), rotate(right, 16))
+
+
+def adjoint_depth(scale, bza_ref, depth_ref, main_ref, tail_ref, to_left_ref, to_right_ref, last=False):
     block = lane_block((64, 128))
     low_half = block < 2
+    near = lax.broadcasted_iota(I32, (64, 128), 1) % PART < HALO
 
     def pair(quad, carry):
         tails = []
@@ -367,6 +385,12 @@
             tail = jnp.where(block == 0, summed[:64, :128], summed[128:, 128:])
             tail = jnp.where(block == 1, rotate(summed[128:, :128], 64), tail)
             tail = jnp.where(block == 2, rotate(summed[:64, 128:], 64), tail)
+            if last:
+                main_ref[member] = own_lanes(*mains)
+                tail_ref[member] = jnp.where(near, rotate(tail, 112), rotate(tail, 80))
+                to_left_ref[member] = to_fixed(jnp.where(near, mains[0], rotate(tail, 16)), scale)
+                to_right_ref[member] = to_fixed(jnp.where(near, rotate(tail, 48), mains[1]), scale)
+                continue
             rows = pl.ds(pl.multiple_of(member * 64, 64), 64)
             main_ref[0, rows, :] = mains[0]
             main_ref[1, rows, :] = mains[1]
@@ -374,6 +398,8 @@
             to_left_ref[member] = to_fixed(mains[0], scale)
             to_right_ref[member] = to_fixed(mains[1], scale)
             tails.append(tail)
+        if last:
+            return carry
         to_left_ref[QUADS + quad] = to_fixed(jnp.where(low_half, tails[0], rotate(tails[1], 64)), scale)
         to_right_ref[QUADS + quad] = to_fixed(jnp.where(low_half, rotate(tails[0], 64), tails[1]), scale)
         return carry
@@ -416,10 +442,10 @@
 
 
 PARTIAL_SHAPES = (
-    jax.ShapeDtypeStruct((2, 1024, 128), F32),
-    jax.ShapeDtypeStruct((QUADS, 64, 128), F32),
-    jax.ShapeDtypeStruct((QUADS + QUADS // 2, 64, 128), I16),
-    jax.ShapeDtypeStruct((QUADS + QUADS // 2, 64, 128), I16),
+    held((2, 1024, 128), F32),
+    held((QUADS, 64, 128), F32),
+    held((QUADS + QUADS // 2, 64, 128), I16),
+    held((QUADS + QUADS // 2, 64, 128), I16),
 )
 
 
@@ -480,6 +506,7 @@
         scratch_shapes=[pltpu.VMEM((SLOTS, NY, 128), F32), pltpu.VMEM((QUADS, VIEWS * 64, ROWS), BF16),
                         pltpu.VMEM((512, 512), BF16)],
         name="first_adjoint",
+        compiler_params=room(60),
     )(start, source, place, inverse, offset, incoming, blurred, kyt, kxt, bza)
 
 
@@ -522,15 +549,16 @@
     return pl.pallas_call(
         join_columns_kernel,
         out_shape=(
-            jax.ShapeDtypeStruct((2, 1024, 128), F32),
-            jax.ShapeDtypeStruct((QUADS, 64, 128), F32),
-            jax.ShapeDtypeStruct((QUADS, 64, 128), I16),
-            jax.ShapeDtypeStruct((QUADS, 64, 128), I16),
+            held((2, 1024, 128), F32),
+            held((QUADS, 64, 128), F32),
+            held((QUADS, 64, 128), I16),
+            held((QUADS, 64, 128), I16),
         ),
         in_specs=smem(2) + vmem(4),
         out_specs=tuple(vmem(4)),
         name="join_columns",
-    )(offset, edges, main, tail, from_left, from_right)
+        compiler_params=room(48),
+    )(offset, edges, *stay(main, tail, from_left, from_right))
 
 
 def joined_planes(quad, steps, block, main_ref, tail_ref, from_low_ref, from_high_ref):
@@ -541,8 +569,6 @@
     left = left + jnp.where(block == 0, rotate(low, 96), 0.0) + jnp.where(block == 3, rotate(high, 96), 0.0)
     right = main_ref[1, rows, :]
     right = right + jnp.where(block == 0, rotate(low, 32), 0.0) + jnp.where(block == 3, rotate(high, 32), 0.0)
-    if tail_ref is None:
-        return rows, left, right
     tail = tail_ref[quad] + jnp.where(block % 2 == 0, low, high)
     return rows, left, right, tail
 
@@ -553,8 +579,8 @@
 
 def second_kernel(offset_ref, edge_ref, part_main_ref, part_tail_ref, from_low_ref, from_high_ref, estimate_main_ref,
                   estimate_tail_ref, scale_main_ref, scale_tail_ref, bzf_ref, bza_ref, average_ref, ky_ref, kx_ref,
-                  kyt_ref, kxt_ref, out_estimate_ref, main_ref, tail_ref, to_left_ref, to_right_ref, tail_estimate_ref,
-                  planes_ref, depth_ref):
+                  kyt_ref, kxt_ref, own_estimate_ref, own_ref, own_tail_ref, to_left_ref, to_right_ref, new_main_ref,
+                  tail_estimate_ref, planes_ref, depth_ref):
     view = pl.program_id(0)
 
     @pl.when(view == 0)
@@ -565,13 +591,16 @@
         def renew(quad, carry):
             rows, left, right, tail = joined_planes(
                 quad, steps, block, part_main_ref, part_tail_ref, from_low_ref, from_high_ref)
-            out_estimate_ref[0, rows, :] = estimate_main_ref[0, rows, :] * left * scale_main_ref[0, rows, :]
-            out_estimate_ref[1, rows, :] = estimate_main_ref[1, rows, :] * right * scale_main_ref[1, rows, :]
+            left = estimate_main_ref[0, rows, :] * left * scale_main_ref[0, rows, :]
+            right = estimate_main_ref[1, rows, :] * right * scale_main_ref[1, rows, :]
+            new_main_ref[0, rows, :] = left
+            new_main_ref[1, rows, :] = right
+            own_estimate_ref[quad] = own_lanes(left * scale_main_ref[0, rows, :], right * scale_main_ref[1, rows, :])
             tail_estimate_ref[quad] = estimate_tail_ref[quad] * tail * scale_tail_ref[quad]
             return carry
 
         lax.fori_loop(0, QUADS, renew, 0)
-        forward_depth(out_estimate_ref, tail_estimate_ref, bzf_ref, planes_ref)
+        forward_depth(new_main_ref, tail_estimate_ref, bzf_ref, planes_ref)
 
     blurred = forward_plane(view, planes_ref, ky_ref[0], kx_ref[0]) + offset_ref[view]
     adjoint_plane(view, average_ref[0].astype(F32) / blurred, kyt_ref[0], kxt_ref[0], depth_ref)
@@ -579,61 +608,108 @@
     @pl.when(view == VIEWS - 1)
     def _():
         scale = tall(32767.0 / partial_bound(offset_ref))
-        adjoint_depth(scale, bza_ref, depth_ref, main_ref, tail_ref, to_left_ref, to_right_ref)
+        adjoint_depth(scale, bza_ref, depth_ref, own_ref, own_tail_ref, to_left_ref, to_right_ref, last=True)
 
 
 def second(offset, edges, *operands):
     return pl.pallas_call(
         second_kernel,
         grid=(VIEWS,),
-        out_shape=(jax.ShapeDtypeStruct((2, 1024, 128), F32),) + PARTIAL_SHAPES,
+        out_shape=(held((QUADS, 64, 128), F32),) * 3 + (held((QUADS, 64, 128), I16),) * 2,
         in_specs=smem(2) + vmem(10) + [per_view(ROWS, 2 * ROWS), per_view(ROWS, ROWS), per_view(ROWS, 128),
                                        per_view(ROWS, ROWS), per_view(128, ROWS)],
         out_specs=tuple(vmem(5)),
-        scratch_shapes=[pltpu.VMEM((QUADS, 64, 128), F32), pltpu.VMEM((VIEWS * 4, ROWS, ROWS), BF16),
-                        pltpu.VMEM((QUADS, VIEWS * 64, ROWS), BF16)],
+        scratch_shapes=[pltpu.VMEM((2, 1024, 128), F32), pltpu.VMEM((QUADS, 64, 128), F32),
+                        pltpu.VMEM((VIEWS * 4, ROWS, ROWS), BF16), pltpu.VMEM((QUADS, VIEWS * 64, ROWS), BF16)],
         name="second",
-    )(offset, edges, *operands)
-
-
-def finish_kernel(offset_ref, edge_ref, main_ref, from_low_ref, from_high_ref, estimate_ref, scale_ref, out_ref,
-                  value_ref):
+        compiler_params=room(52),
+    )(offset, edges, *stay(*operands[:4]), *operands[4:])
+
+
+def join_own_kernel(offset_ref, edge_ref, own_ref, tail_ref, from_left_ref, from_right_ref, out_ref, low_ref, high_ref):
     block = lane_block((64, 128))
-    lane = lax.broadcasted_iota(I32, (64, 128), 1) % PART
+    near = lax.broadcasted_iota(I32, (64, 128), 1) % PART < HALO
+    bound = partial_bound(offset_ref)
+    scale = tall(32767.0 / bound)
+    left_step = tall(bound * (edge_ref[0] / 32767.0))
+    right_step = tall(bound * (edge_ref[1] / 32767.0))
+
+    def four_quads(quad, carry):
+        low = jnp.zeros((64, 128), F32)
+        high = jnp.zeros((64, 128), F32)
+        for k in range(4):
+            member = quad + k * 4
+            left = from_fixed(from_left_ref[member], left_step)
+            right = from_fixed(from_right_ref[member], right_step)
+            out_ref[member] = own_ref[member] + own_lanes(left, right)
+            tail = tail_ref[member] + jnp.where(near, left, right)
+            low = jnp.where(block == k, rotate(tail, PART * k), low)
+            high = jnp.where(block == k, rotate(tail, PART * k - PART), high)
+        low_ref[quad] = to_fixed(low, scale)
+        high_ref[quad] = to_fixed(high, scale)
+        return carry
+
+    lax.fori_loop(0, QUADS // 4, four_quads, 0)
+
+
+def join_own(offset, edges, own, tail, from_left, from_right):
+    return pl.pallas_call(
+        join_own_kernel,
+        out_shape=(held((QUADS, 64, 128), F32), held((QUADS // 4, 64, 128), I16), held((QUADS // 4, 64, 128), I16)),
+        in_specs=smem(2) + vmem(4),
+        out_specs=tuple(vmem(3)),
+        name="join_own",
+        compiler_params=room(48),
+    )(offset, edges, *stay(own, tail, from_left, from_right))
+
+
+def finish_kernel(offset_ref, edge_ref, own_ref, from_low_ref, from_high_ref, estimate_ref, out_ref, value_ref):
+    block = lane_block((64, 128))
     steps = depth_steps(partial_bound(offset_ref), edge_ref)
 
-    def one_quad(quad, largest):
-        rows, left, right = joined_planes(quad, steps, block, main_ref, None, from_low_ref, from_high_ref)
-        left = estimate_ref[0, rows, :] * left * scale_ref[0, rows, :]
-        right = estimate_ref[1, rows, :] * right * scale_ref[1, rows, :]
-        value = jnp.where(lane < HALO, rotate(left, 112), rotate(right, 16))
-        value_ref[rows, :] = value
-        return jnp.maximum(largest, value)
-
-    largest = lax.fori_loop(0, QUADS, one_quad, jnp.zeros((64, 128), F32))
+    def four_quads(quad, largest):
+        low = from_fixed(from_low_ref[quad], steps[0])
+        high = from_fixed(from_high_ref[quad], steps[1])
+        for k in range(4):
+            member = quad + k * 4
+            summed = own_ref[member] + jnp.where(block == 0, rotate(low, -PART * k), 0.0)
+            summed = summed + jnp.where(block == 3, rotate(high, 96 - PART * k), 0.0)
+            value = estimate_ref[member] * summed
+            value_ref[member] = value
+            largest = jnp.maximum(largest, value)
+        return largest
+
+    largest = lax.fori_loop(0, QUADS // 4, four_quads, jnp.zeros((64, 128), F32))
     unit = (jnp.max(largest) * 64.0).astype(I32) + 1
     vector = jnp.full((16, 128), unit, I32)
     out_ref[1024:1040, :] = (vector >> 15).astype(I16)
     out_ref[1040:1056, :] = (vector & 32767).astype(I16)
-    factor = (32767.0 * 64.0) / tall(vector[:8].astype(F32))
-
-    def round_quad(quad, carry):
-        rows = pl.ds(pl.multiple_of(quad * 64, 64), 64)
-        out_ref[rows, :] = to_fixed(value_ref[rows, :], factor)
-        return carry
-
-    lax.fori_loop(0, QUADS, round_quad, 0)
-
-
-def finish(offset, edges, main, from_low, from_high, estimate, scale):
+    factor = (32767.0 * 64.0) / vector.astype(F32)
+
+    def sixteen_rows(n, carry):
+        for j in range(0, 16, 2):
+            rows = slice(j * 4, j * 4 + 8)
+            ends = [swap_fours(value_ref[n * 4 + 2 * m, rows, :], value_ref[n * 4 + 2 * m + 1, rows, :])
+                    for m in range(2)]
+            for odd in range(2):
+                first = pl.multiple_of((j + odd) * NY + n * 16, 16)
+                out_ref[pl.ds(first, 16), :] = to_fixed(
+                    jnp.concatenate([ends[0][odd], ends[1][odd]], axis=0), factor)
+        return carry
+
+    lax.fori_loop(0, 4, sixteen_rows, 0)
+
+
+def finish(offset, edges, own, from_low, from_high, estimate):
     return pl.pallas_call(
         finish_kernel,
-        out_shape=jax.ShapeDtypeStruct((1056, 128), I16),
-        in_specs=smem(2) + vmem(5),
+        out_shape=held((1056, 128), I16),
+        in_specs=smem(2) + vmem(4),
         out_specs=vmem(1)[0],
-        scratch_shapes=[pltpu.VMEM((1024, 128), F32)],
+        scratch_shapes=[pltpu.VMEM((QUADS, 64, 128), F32)],
         name="finish",
-    )(offset, edges, main, from_low, from_high, estimate, scale)
+        compiler_params=room(52),
+    )(offset, edges, *stay(own, from_low, from_high, estimate))
 
 
 def assemble_kernel(index_ref, *refs):
@@ -646,26 +722,23 @@
             owner = ((part // 2 + place % 4) % 4) * 2 + (part % 2 if place < 4 else 1 - part % 2)
             buffer_ref[owner] = chunk_refs[place][...]
 
+    block = lane_block((16, 128))
+    even = block % 2 == 0
     units = []
-    for k in range(8):
-        digits = buffer_ref[k, 1024:1040, :].astype(I32) * 32768 + buffer_ref[k, 1040:1056, :].astype(I32)
-        units.append(digits.astype(F32) * (1.0 / (64.0 * 32767.0)))
-    block = lane_block((8, 128))
-    even = block % 2 == 0
-    first = pl.multiple_of(pl.program_id(0) * 16, 16)
-
-    def eight_rows(m, carry):
-        low = pl.ds(pl.multiple_of(m * 128 + first, 16), 16)
-        high = pl.ds(pl.multiple_of(m * 128 + 64 + first, 16), 16)
-        for half in range(2):
-            values = []
-            for k in range(4):
-                place = half * 4 + k
-                below = from_fixed(buffer_ref[place, low, :], units[place])
-                above = from_fixed(buffer_ref[place, high, :], units[place])
-                values.append(swap_fours(below[:8], above[:8]) + swap_fours(below[8:], above[8:]))
-            for j in range(4):
-                c0, c1, c2, c3 = (values[k][j] for k in range(4))
+    for half in range(2):
+        unit = jnp.zeros((16, 128), F32)
+        for k in range(4):
+            digits = (buffer_ref[half * 4 + k, 1024:1040, :].astype(I32) * 32768
+                      + buffer_ref[half * 4 + k, 1040:1056, :].astype(I32))
+            unit = jnp.where(block == k, digits.astype(F32) * (1.0 / (64.0 * 32767.0)), unit)
+        units.append(unit)
+    step = pl.program_id(0)
+
+    def sixteen_rows(n, carry):
+        for j in range(4):
+            rows = pl.ds(pl.multiple_of((step * 4 + j) * NY + n * 16, 16), 16)
+            for half in range(2):
+                c0, c1, c2, c3 = (buffer_ref[half * 4 + k, rows, :].astype(I32).astype(F32) for k in range(4))
                 a0 = jnp.where(block < 2, c0, rotate(c2, 64))
                 a1 = jnp.where(block < 2, c1, rotate(c3, 64))
                 a2 = jnp.where(block < 2, rotate(c0, 64), c2)
@@ -673,10 +746,11 @@
                 results = (jnp.where(even, a0, rotate(a1, 32)), jnp.where(even, rotate(a0, 96), a1),
                            jnp.where(even, a2, rotate(a3, 32)), jnp.where(even, rotate(a2, 96), a3))
                 for h in range(4):
-                    out_ref[h, 0, j, pl.ds(pl.multiple_of(m * 8, 8), 8), half * 128:(half + 1) * 128] = results[h]
-        return carry
-
-    lax.fori_loop(0, 8, eight_rows, 0)
+                    out_ref[h, 0, j, pl.ds(pl.multiple_of(n * 16, 16), 16), half * 128:(half + 1) * 128] = (
+                        results[h] * units[half])
+        return carry
+
+    lax.fori_loop(0, 4, sixteen_rows, 0)
 
 
 def assemble(index, chunks):
@@ -688,7 +762,8 @@
         out_specs=pl.BlockSpec((4, 1, 4, NY, 256), lambda step: (0, step, 0, 0, 0)),
         scratch_shapes=[pltpu.VMEM((VIEWS, 1056, 128), I16)],
         name="assemble",
-    )(index, *chunks).reshape(64, NY, 256)
+        compiler_params=room(58),
+    )(index, *stay(*chunks)).reshape(64, NY, 256)
 
 
 def to_neighbours(upward, downward, axis):
@@ -784,19 +859,20 @@
     scale_main, scale_tail = build_weights(
         weight_rows.reshape(-1), jnp.repeat(weight_main, 4, axis=2), jnp.repeat(weight_tail, 4, axis=1))
 
+    incoming, scale_main, scale_tail = lax.optimization_barrier((incoming, scale_main, scale_tail))
     part_main, part_tail, to_left, to_right, average = first_adjoint(
         start, source, place, inverse.reshape(-1), background, incoming, blurred, kyt, kxt, bza)
     from_left, from_right = to_neighbours(to_right, to_left, "view")
     part_main, part_tail, low, high = join_columns(background, edges, part_main, part_tail, from_left, from_right)
     from_low, from_high = to_neighbours(high, low, "block")
 
-    main, part_main, part_tail, to_left, to_right = second(
+    estimate, own, own_tail, to_left, to_right = second(
         background, edges, part_main, part_tail, from_low, from_high, main, tail, scale_main, scale_tail,
         bzf, bza, average, ky, kx, kyt, kxt)
     from_left, from_right = to_neighbours(to_right, to_left, "view")
-    part_main, part_tail, low, high = join_columns(background, edges, part_main, part_tail, from_left, from_right)
+    own, low, high = join_own(background, edges, own, own_tail, from_left, from_right)
     from_low, from_high = to_neighbours(high, low, "block")
-    own = finish(background, edges, part_main, from_low, from_high, main, scale_main)
+    own = finish(background, edges, own, from_low, from_high, estimate)
 
     mine, partners = gather_parts(own)
     return assemble(index, mine + partners)

time: 195 us -> 172 us (0.88)
  Pallas kernels: 91.2 us -> 76.9 us
  waiting for transfers between devices: 43.6 us -> 39.1 us
  local copies, waits for them, and re-layouts: 12.9 us -> 8.69 us
    pallas_call x4, Pallas kernels: 32.9 us -> 22.8 us  [the longest x1 18.5 us: second(): pl.pallas_call(second_kernel, grid=(VIEWS,), out_shape=(held((QUADS, 64,...]
    all_to_all x1, waiting for transfers between devices: 16.2 us -> 7.9 us  [program(): lax.all_to_all(outgoing.reshape(VIEWS * block_count, CAP, NY, 128), ('vie...]
    unnamed x43 -> x21, local copies, waits for them, and re-layouts: 4.93 us -> 0.82 us
    pallas_call x1, Pallas kernels: 9.01 us -> 5.54 us  [assemble(): pl.pallas_call(assemble_kernel, grid=(4,), out_shape=jax.ShapeDtypeStruct...]
    ppermute x4, starting transfers between devices: 3.67 us -> 0.52 us  [gather_parts(): lax.ppermute(part, 'view', [(i, i ^ 1) for i in range(VIEWS)])]
    all_to_all x1, starting transfers between devices: 7.38 us -> 10.4 us  [program(): lax.all_to_all(outgoing.reshape(VIEWS * block_count, CAP, NY, 128), ('vie...]
    ppermute x5, waiting for transfers between devices: 15.7 us -> 18 us  [to_neighbours(): lax.ppermute(upward, axis, [(i, (i + 1) % count) for i in range(count)])]
  transfers between devices with their start and end apart: 18 -> 18, of which waited for: 7 -> 10; matrix products, arithmetic and copies ran while one was open for 8% -> 9% of each run, Pallas kernels for 17% -> 19%
where the time goes in v3:
time: 172 us; the launch traced here: 170 us
  Pallas kernels  76.9 us (45%)
  waiting for transfers between devices  39.1 us (23%)
  starting transfers between devices  37.4 us (22%)
  local copies, waits for them, and re-layouts  8.69 us (5%)
  other arithmetic  7.57 us (4%)
    ppermute x5, starting transfers between devices, to_neighbours(): lax.ppermute(downward, axis, [((i + 1) % count, i) for i in range(count)])  21 us
    pallas_call x1, Pallas kernels, second(): pl.pallas_call(second_kernel, grid=(VIEWS,), out_shape=(held((QUADS, 64,...  18.5 us
    ppermute x5, waiting for transfers between devices, to_neighbours(): lax.ppermute(upward, axis, [(i, (i + 1) % count) for i in range(count)])  18 us
    pallas_call x1, Pallas kernels, first_adjoint(): pl.pallas_call(first_adjoint_kernel, grid=(VIEWS,), out_shape=PARTIAL_SHA...  13.2 us
    ppermute x3, waiting for transfers between devices, gather_parts(): lax.ppermute(own, 'view', [((i + 2 * step) % VIEWS, i) for i in range(VIE...  11.6 us
    all_to_all x1, starting transfers between devices, program(): lax.all_to_all(outgoing.reshape(VIEWS * block_count, CAP, NY, 128), ('vie...  10.4 us
    pallas_call x1, Pallas kernels, forward(): pl.pallas_call(forward_kernel, out_shape=(jax.ShapeDtypeStruct((VIEWS, RO...  10.4 us
    all_to_all x1, waiting for transfers between devices, program(): lax.all_to_all(outgoing.reshape(VIEWS * block_count, CAP, NY, 128), ('vie...  7.9 us
  transfers between devices with their start and end apart: 18, of which 10 were waited for; matrix products, arithmetic and copies ran while one was open for 9% of the time, Pallas kernels for 19%

profile of v3, /device:TPU:0, one launch (start us, length us, event | category | flops | bytes accessed | tf_op | source)
XLA Modules:
  0.0 170.0 jit_solution(16434821952044900417)
XLA Ops:
  0.0 2.8 %ends.1 = (bf16[8,64,128]{2,1,0:T(8,128)(2,1)}, bf16[8,64,128]{2,1,0:T(8,128)(2,1)}) custom-call(s32[1]{0:T(128)} %bitcast.index_ref, f32[64,64,256]{2,1,0:T(8,128)} %estimate_ref.1, f32[64,64,256]{2,1,0:T(8,128)} %estimate_ref.1), custom_call_target="tpu_custom_call" | custom-call | tf_op jit(solution)/shard_map/ends/pallas_call | solution.py:254
  2.8 6.3 %collective-permute-start.1 = (bf16[8,64,128]{2,1,0:T(8,128)(2,1)}, bf16[8,64,128]{2,1,0:T(8,128)(2,1)S(1)}, u32[]{:S(2)}, u32[]{:S(2)}) collective-permute-start(bf16[8,64,128]{2,1,0:T(8,128)(2,1)} %get-tuple-element.38), channel_id=1, source_target_pairs={{1,0},{2,1},{3,2},{4,3},{5,4},{6,5},{7,6},{8,7},{9,8},{10,9},{11,1... | collective-permute-start | bytes 393224 | tf_op jit(solution)/shard_map/ppermute | solution.py:772
  9.3 0.6 dynamic-slice_bitcast_fusion.target_ref
  9.8 5.5 %pack.1 = bf16[8,32,64,128]{3,2,1,0:T(8,128)(2,1)} custom-call(s32[16]{0:T(128)} %dynamic-slice_bitcast_fusion.target_ref, bf16[16,4,64,256]{3,2,1,0:T(8,128)(2,1)} %bitcast.37), custom_call_target="tpu_custom_call" | custom-call | tf_op jit(solution)/shard_map/pack/pallas_call | solution.py:180
  15.4 10.4 %all-to-all-start = ((bf16[128,2,64,128]{3,2,1,0:T(8,128)(2,1)}), bf16[128,2,64,128]{3,2,1,0:T(8,128)(2,1)}, u32[]{:S(2)}, u32[]{:S(2)}) async-start(bf16[128,2,64,128]{3,2,1,0:T(8,128)(2,1)} %bitcast.36), calls=%async_computation | async-start | bytes 8388608 | tf_op jit(solution)/shard_map/all_to_all | solution.py:807
  26.0 2.5 %convert_reduce_fusion = s32[8,16,16]{2,1,0:T(8,128)S(1)} fusion(s32[8,16,16]{2,1,0:T(8,128)S(1)} %reshape_squeeze.3, pred[16,16]{1,0:T(8,128)(4,1)S(1)} %iota_compare_fusion.6), kind=kLoop, calls=%fused_computation.2 | loop fusion | flops 129024 | bytes 16640 | tf_op jit(solution)/shard_map/reduce_sum | solution.py:817
  28.6 0.4 select_reduce_fusion.2
  29.0 0.1 copy.32
  29.3 0.4 fusion
  30.1 0.1 select_reduce_fusion.3
  30.4 0.1 sub.102
  30.5 0.1 copy.37
  30.7 0.1 broadcast_in_dim.292
  30.8 0.2 slice_reduce_fusion.19
  31.1 0.5 slice_reduce_fusion.20
  31.7 0.8 multiply_reduce_fusion
  32.5 0.1 copy.39
  32.7 0.7 convert_reduce_fusion.3.start_ref
  33.4 0.2 convert_reduce_fusion.2
  33.6 0.1 convert_reduce_fusion.1
  33.7 0.1 select_reduce_fusion.4
  33.8 0.2 broadcast_multiply_fusion
  34.0 0.2 fusion.32
  34.3 0.3 maximum_bitcast_fusion
  34.6 0.7 add_convert_fusion.edge_ref
  35.4 0.1 slice.145
  35.5 6.0 %window.1.main_ref.estimate_main_ref = f32[2,1024,128]{2,1,0:T(8,128)} custom-call(s32[1]{0:T(128)} %bitcast.index_ref, f32[64,64,256]{2,1,0:T(8,128)} %estimate_ref.1), custom_call_target="tpu_custom_call" | custom-call | tf_op jit(solution)/shard_map/window/pallas_call | solution.py:217
  41.5 0.6 reshape.278.shift_ref
  42.1 0.7 reshape.277.taps_ref
  42.8 0.6 reshape.270.rows_ref
  43.4 0.6 div.30.inverse_ref
  44.0 0.3 reshape.280
  44.4 0.2 reshape.275
  44.6 6.8 %bands.1 = (bf16[8,256,256]{2,1,0:T(8,128)(2,1)}, bf16[8,256,256]{2,1,0:T(8,128)(2,1)}, bf16[8,256,128]{2,1,0:T(8,128)(2,1)}, bf16[8,128,256]{2,1,0:T(8,128)(2,1...) custom-call(f32[504]{0:T(512)} %reshape.277.taps_ref, s32[24]{0:T(128)} %reshape.278.shift_ref), custom_call_target="tpu_custom_call" | custom-call | tf_op jit(solution)/shard_map/bands/pallas_call | solution.py:136
  51.4 0.7 broadcast_in_dim.296
  52.1 0.9 broadcast_in_dim.295
  53.0 3.8 %weights.1 = (f32[2,1024,128]{2,1,0:T(8,128)}, f32[16,64,128]{2,1,0:T(8,128)}) custom-call(f32[512]{0:T(512)} %reshape.270.rows_ref, f32[8,2,64,128]{3,2,1,0:T(8,128)} %bitcast.38, f32[8,64,128]{2,1,0:T(8,128)} %bitcast.40), custom_call_target="tpu_custom_call" | custom-call | tf_op jit(solution)/shard_map/weights/pallas_call | solution.py:303
  56.8 0.7 select_reduce_fusion
  57.5 0.6 copy-done.4
  58.3 10.4 %forward.1 = (bf16[8,256,512]{2,1,0:T(8,128)(2,1)}, f32[16,64,128]{2,1,0:T(8,128)}) custom-call(f32[4]{0:T(128)} %add_convert_fusion.edge_ref, f32[2,1024,128]{2,1,0:T(8,128)} %window.1.main_ref.estimate_main_ref, bf16[8,64,128]{2,1,0:T(8,128)(2,1)} %copy-done.5, bf16[8,64,128]{2,1,0:T(8,128)(2,1)} %copy-done.4, bf16[512,192]{1,0:T(8,128)(2,1)} %get-tuple-element.44.bzf_ref, ...), custom_call_target="tpu_custom_call" | custom-call | tf_op jit(solution)/shard_map/forward/pallas_call | solution.py:427
  68.6 7.9 %all-to-all-done = bf16[128,2,64,128]{3,2,1,0:T(8,128)(2,1)} async-done(((bf16[128,2,64,128]{3,2,1,0:T(8,128)(2,1)}), bf16[128,2,64,128]{3,2,1,0:T(8,128)(2,1)}, u32[]{:S(2)}, u32[]{:S(2)}) %all-to-all-start) | async-done | bytes 4194336 | tf_op jit(solution)/shard_map/all_to_all | solution.py:807
  76.5 13.2 %first_adjoint.1 = (f32[2,1024,128]{2,1,0:T(8,128)S(1)}, f32[16,64,128]{2,1,0:T(8,128)S(1)}, s16[24,64,128]{2,1,0:T(8,128)(2,1)S(1)}, s16[24,64,128]{2,1,0:T(8,128)(2,1)S(1)}, bf16[8,256,512]{2,1,0:T(8,128)(2,1)}) custom-call(s32[9]{0:T(128)} %convert_reduce_fusion.3.start_ref, s32[256]{0:T(256)} %get-tuple-element.93.source_ref, ...), custom_call_target="tpu_custom_call" | custom-call | tf_op jit(solution)/shard_map/first_adjoint/pallas_call | solution.py:499
  89.8 3.0 %collective-permute-start.3 = (s16[24,64,128]{2,1,0:T(8,128)(2,1)S(1)}, s16[24,64,128]{2,1,0:T(8,128)(2,1)S(1)}, u32[]{:S(2)}, u32[]{:S(2)}) collective-permute-start(s16[24,64,128]{2,1,0:T(8,128)(2,1)S(1)} %get-tuple-element.54), channel_id=1, source_target_pairs={{16,0},{32,16},{48,32},{64,48},{80,64},{96,80},{112,96},{0,112},{1... | collective-permute-start | bytes 1179656 | tf_op jit(solution)/shard_map/ppermute | solution.py:772
  92.7 5.5 %collective-permute-done.2.from_left_ref = s16[24,64,128]{2,1,0:T(8,128)(2,1)S(1)} collective-permute-done((s16[24,64,128]{2,1,0:T(8,128)(2,1)S(1)}, s16[24,64,128]{2,1,0:T(8,128)(2,1)S(1)}, u32[]{:S(2)}, u32[]{:S(2)}) %collective-permute-start.2) | collective-permute-done | bytes 393248 | tf_op jit(solution)/shard_map/ppermute | solution.py:771
  98.2 1.7 join_columns.1
  99.9 1.9 %collective-permute-start.4 = (s16[16,64,128]{2,1,0:T(8,128)(2,1)S(1)}, s16[16,64,128]{2,1,0:T(8,128)(2,1)S(1)}, u32[]{:S(2)}, u32[]{:S(2)}) collective-permute-start(s16[16,64,128]{2,1,0:T(8,128)(2,1)S(1)} %get-tuple-element.57), channel_id=1, source_target_pairs={{0,1},{1,2},{2,3},{3,4},{4,5},{5,6},{6,7},{7,8},{8,9},{9,10},{10,1... | collective-permute-start | bytes 786440 | tf_op jit(solution)/shard_map/ppermute | solution.py:771
  101.8 3.5 %collective-permute-start.5 = (s16[16,64,128]{2,1,0:T(8,128)(2,1)S(1)}, s16[16,64,128]{2,1,0:T(8,128)(2,1)S(1)}, u32[]{:S(2)}, u32[]{:S(2)}) collective-permute-start(s16[16,64,128]{2,1,0:T(8,128)(2,1)S(1)} %get-tuple-element.58), channel_id=1, source_target_pairs={{1,0},{2,1},{3,2},{4,3},{5,4},{6,5},{7,6},{8,7},{9,8},{10,9},{11,1... | collective-permute-start | bytes 786440 | tf_op jit(solution)/shard_map/ppermute | solution.py:772
  105.3 6.3 %collective-permute-done.4.from_low_ref = s16[16,64,128]{2,1,0:T(8,128)(2,1)S(1)} collective-permute-done((s16[16,64,128]{2,1,0:T(8,128)(2,1)S(1)}, s16[16,64,128]{2,1,0:T(8,128)(2,1)S(1)}, u32[]{:S(2)}, u32[]{:S(2)}) %collective-permute-start.4) | collective-permute-done | bytes 262176 | tf_op jit(solution)/shard_map/ppermute | solution.py:771
  111.5 18.5 %second.1 = (f32[16,64,128]{2,1,0:T(8,128)S(1)}, f32[16,64,128]{2,1,0:T(8,128)S(1)}, f32[16,64,128]{2,1,0:T(8,128)S(1)}, s16[16,64,128]{2,1,0:T(8,128)(2,1)S(1)}, s16[16,64,128]{2,1,0:T(8,128)(2,1)S(1)}) custom-call(f32[8]{0:T(128)} %offset_ref.9, f32[4]{0:T(128)} %add_convert_fusion.edge_ref, f32[2,1024,128]{2,1,0:T(8,128)S(1)} %get-tuple-element.55.part_main_ref, ...), custom_call_target="tpu_custom_call" | custom-call | tf_op jit(solution)/shard_map/second/pallas_call | solution.py:615
  130.1 2.9 %collective-permute-start.7 = (s16[16,64,128]{2,1,0:T(8,128)(2,1)S(1)}, s16[16,64,128]{2,1,0:T(8,128)(2,1)S(1)}, u32[]{:S(2)}, u32[]{:S(2)}) collective-permute-start(s16[16,64,128]{2,1,0:T(8,128)(2,1)S(1)} %get-tuple-element.66), channel_id=1, source_target_pairs={{16,0},{32,16},{48,32},{64,48},{80,64},{96,80},{112,96},{0,112},{1... | collective-permute-start | bytes 786440 | tf_op jit(solution)/shard_map/ppermute | solution.py:772
  133.0 4.1 %collective-permute-done.6.from_left_ref = s16[16,64,128]{2,1,0:T(8,128)(2,1)S(1)} collective-permute-done((s16[16,64,128]{2,1,0:T(8,128)(2,1)S(1)}, s16[16,64,128]{2,1,0:T(8,128)(2,1)S(1)}, u32[]{:S(2)}, u32[]{:S(2)}) %collective-permute-start.6) | collective-permute-done | bytes 262176 | tf_op jit(solution)/shard_map/ppermute | solution.py:771
  137.1 1.3 join_own.1
  138.5 5.3 %collective-permute-start.9 = (s16[4,64,128]{2,1,0:T(8,128)(2,1)S(1)}, s16[4,64,128]{2,1,0:T(8,128)(2,1)S(1)}, u32[]{:S(2)}, u32[]{:S(2)}) collective-permute-start(s16[4,64,128]{2,1,0:T(8,128)(2,1)S(1)} %get-tuple-element.69), channel_id=1, source_target_pairs={{1,0},{2,1},{3,2},{4,3},{5,4},{6,5},{7,6},{8,7},{9,8},{10,9},{11,1... | collective-permute-start | bytes 196616 | tf_op jit(solution)/shard_map/ppermute | solution.py:772
  143.8 2.2 %collective-permute-done.8.from_low_ref = s16[4,64,128]{2,1,0:T(8,128)(2,1)S(1)} collective-permute-done((s16[4,64,128]{2,1,0:T(8,128)(2,1)S(1)}, s16[4,64,128]{2,1,0:T(8,128)(2,1)S(1)}, u32[]{:S(2)}, u32[]{:S(2)}) %collective-permute-start.8) | collective-permute-done | bytes 65568 | tf_op jit(solution)/shard_map/ppermute | solution.py:771
  146.0 1.3 finish.1.refs_0_
  147.5 0.7 collective-permute-start.11
  148.2 2.5 %collective-permute-start.10 = (s16[1056,128]{1,0:T(8,128)(2,1)S(1)}, s16[1056,128]{1,0:T(8,128)(2,1)S(1)}, u32[]{:S(2)}, u32[]{:S(2)}) collective-permute-start(s16[1056,128]{1,0:T(8,128)(2,1)S(1)} %finish.1.refs_0_), channel_id=1, source_target_pairs={{32,0},{48,16},{64,32},{80,48},{96,64},{112,80},{0,96},{16,112},{3... | collective-permute-start | bytes 811016 | tf_op jit(solution)/shard_map/ppermute | solution.py:778
  150.7 11.4 %collective-permute-done.12.refs_3_ = s16[1056,128]{1,0:T(8,128)(2,1)S(1)} collective-permute-done((s16[1056,128]{1,0:T(8,128)(2,1)S(1)}, s16[1056,128]{1,0:T(8,128)(2,1)S(1)}, u32[]{:S(2)}, u32[]{:S(2)}) %collective-permute-start.12) | collective-permute-done | bytes 270368 | tf_op jit(solution)/shard_map/ppermute | solution.py:778
  162.1 0.5 collective-permute-start.15
  162.6 0.2 collective-permute-done.10.refs_1_
  162.8 0.8 collective-permute-done.16.refs_7_
  163.6 0.4 collective-permute-done.15.refs_6_
  164.0 0.4 collective-permute-done.14.refs_5_
  164.4 5.5 %assemble.1 = f32[4,4,4,64,256]{4,3,2,1,0:T(8,128)} custom-call(s32[1]{0:T(128)} %bitcast.index_ref, s16[1056,128]{1,0:T(8,128)(2,1)S(1)} %finish.1.refs_0_, s16[1056,128]{1,0:T(8,128)(2,1)S(1)} %collective-permute-done.10.refs_1_, s16[1056,128]{1,0:T(8,128)(2,1)S(1)} %collective-permute-done.11.refs_2_, ...), custom_call_target="tpu_custom_call" | custom-call | tf_op jit(solution)/shard_map/assemble/pallas_call | solution.py:757
  (71 shorter events, 1.7 us)
Async XLA Ops:
  0.0 9.2 %copy-start.7 = (s32[8,256,1]{1,2,0:T(1,128)S(1)}, s32[8,256,1]{1,2,0:T(1,128)}, u32[]{:S(2)}) copy-start(s32[8,256,1]{1,2,0:T(1,128)} %param.9) | copy-start | bytes 24580
  2.8 54.7 %collective-permute-start.1 = (bf16[8,64,128]{2,1,0:T(8,128)(2,1)}, bf16[8,64,128]{2,1,0:T(8,128)(2,1)S(1)}, u32[]{:S(2)}, u32[]{:S(2)}) collective-permute-start(bf16[8,64,128]{2,1,0:T(8,128)(2,1)} %get-tuple-element.38), channel_id=1, source_target_pairs={{1,0},{2,1},{3,2},{4,3},{5,4},{6,5},{7,6},{8,7},{9,8},{10,9},{11,1... | collective-permute-start | bytes 393224 | tf_op jit(solution)/shard_map/ppermute | solution.py:772
  9.2 48.4 %collective-permute-start = (bf16[8,64,128]{2,1,0:T(8,128)(2,1)}, bf16[8,64,128]{2,1,0:T(8,128)(2,1)S(1)}, u32[]{:S(2)}, u32[]{:S(2)}) collective-permute-start(bf16[8,64,128]{2,1,0:T(8,128)(2,1)} %get-tuple-element.39), channel_id=1, source_target_pairs={{0,1},{1,2},{2,3},{3,4},{4,5},{5,6},{6,7},{7,8},{8,9},{9,10},{10,1... | collective-permute-start | bytes 393224 | tf_op jit(solution)/shard_map/ppermute | solution.py:771
  15.4 10.5 %copy-start.8 = (s32[8,256]{1,0:T(8,128)S(1)}, s32[8,256]{1,0:T(8,128)}, u32[]{:S(2)}) copy-start(s32[8,256]{1,0:T(8,128)} %param.10) | copy-start | bytes 24580
  15.4 14.3 %copy-start.6 = (f32[8,3,21]{2,0,1:T(8,128)S(1)}, f32[8,3,21]{2,0,1:T(8,128)}, u32[]{:S(2)}) copy-start(f32[8,3,21]{2,0,1:T(8,128)} %param.12) | copy-start | bytes 6052
  15.4 14.6 %copy-start.9 = (s32[8,3]{0,1:T(4,128)S(1)}, s32[8,3]{0,1:T(4,128)}, u32[]{:S(2)}) copy-start(s32[8,3]{0,1:T(4,128)} %param.11) | copy-start | bytes 292
  15.4 61.2 %all-to-all-start = ((bf16[128,2,64,128]{3,2,1,0:T(8,128)(2,1)}), bf16[128,2,64,128]{3,2,1,0:T(8,128)(2,1)}, u32[]{:S(2)}, u32[]{:S(2)}) async-start(bf16[128,2,64,128]{3,2,1,0:T(8,128)(2,1)} %bitcast.36), calls=%async_computation | async-start | bytes 8388608 | tf_op jit(solution)/shard_map/all_to_all | solution.py:807
  57.5 0.7 copy-start.4
  57.5 0.7 copy-start.5
  76.5 21.6 %copy-start = (f32[4]{0:T(128)S(1)}, f32[4]{0:T(128)}, u32[]{:S(2)}) copy-start(f32[4]{0:T(128)} %add_convert_fusion.edge_ref) | copy-start | bytes 52
  76.5 21.7 %copy-start.2 = (f32[8]{0:T(128)S(1)}, f32[8]{0:T(128)}, u32[]{:S(2)}) copy-start(f32[8]{0:T(128)} %offset_ref.9) | copy-start | bytes 100
  89.8 8.4 %collective-permute-start.2 = (s16[24,64,128]{2,1,0:T(8,128)(2,1)S(1)}, s16[24,64,128]{2,1,0:T(8,128)(2,1)S(1)}, u32[]{:S(2)}, u32[]{:S(2)}) collective-permute-start(s16[24,64,128]{2,1,0:T(8,128)(2,1)S(1)} %get-tuple-element.53), channel_id=1, source_target_pairs={{0,16},{16,32},{32,48},{48,64},{64,80},{80,96},{96,112},{112,0},{1... | collective-permute-start | bytes 1179656 | tf_op jit(solution)/shard_map/ppermute | solution.py:771
  89.8 8.4 %collective-permute-start.3 = (s16[24,64,128]{2,1,0:T(8,128)(2,1)S(1)}, s16[24,64,128]{2,1,0:T(8,128)(2,1)S(1)}, u32[]{:S(2)}, u32[]{:S(2)}) collective-permute-start(s16[24,64,128]{2,1,0:T(8,128)(2,1)S(1)} %get-tuple-element.54), channel_id=1, source_target_pairs={{16,0},{32,16},{48,32},{64,48},{80,64},{96,80},{112,96},{0,112},{1... | collective-permute-start | bytes 1179656 | tf_op jit(solution)/shard_map/ppermute | solution.py:772
  99.9 11.7 %collective-permute-start.4 = (s16[16,64,128]{2,1,0:T(8,128)(2,1)S(1)}, s16[16,64,128]{2,1,0:T(8,128)(2,1)S(1)}, u32[]{:S(2)}, u32[]{:S(2)}) collective-permute-start(s16[16,64,128]{2,1,0:T(8,128)(2,1)S(1)} %get-tuple-element.57), channel_id=1, source_target_pairs={{0,1},{1,2},{2,3},{3,4},{4,5},{5,6},{6,7},{7,8},{8,9},{9,10},{10,1... | collective-permute-start | bytes 786440 | tf_op jit(solution)/shard_map/ppermute | solution.py:771
  101.8 9.7 %collective-permute-start.5 = (s16[16,64,128]{2,1,0:T(8,128)(2,1)S(1)}, s16[16,64,128]{2,1,0:T(8,128)(2,1)S(1)}, u32[]{:S(2)}, u32[]{:S(2)}) collective-permute-start(s16[16,64,128]{2,1,0:T(8,128)(2,1)S(1)} %get-tuple-element.58), channel_id=1, source_target_pairs={{1,0},{2,1},{3,2},{4,3},{5,4},{6,5},{7,6},{8,7},{9,8},{10,9},{11,1... | collective-permute-start | bytes 786440 | tf_op jit(solution)/shard_map/ppermute | solution.py:772
  111.5 25.5 %copy-start.1 = (f32[4]{0:T(128)S(1)}, f32[4]{0:T(128)}, u32[]{:S(2)}) copy-start(f32[4]{0:T(128)} %add_convert_fusion.edge_ref) | copy-start | bytes 52
  111.5 25.5 %copy-start.3 = (f32[8]{0:T(128)S(1)}, f32[8]{0:T(128)}, u32[]{:S(2)}) copy-start(f32[8]{0:T(128)} %offset_ref.9) | copy-start | bytes 100
  130.0 7.0 %collective-permute-start.6 = (s16[16,64,128]{2,1,0:T(8,128)(2,1)S(1)}, s16[16,64,128]{2,1,0:T(8,128)(2,1)S(1)}, u32[]{:S(2)}, u32[]{:S(2)}) collective-permute-start(s16[16,64,128]{2,1,0:T(8,128)(2,1)S(1)} %get-tuple-element.65), channel_id=1, source_target_pairs={{0,16},{16,32},{32,48},{48,64},{64,80},{80,96},{96,112},{112,0},{1... | collective-permute-start | bytes 786440 | tf_op jit(solution)/shard_map/ppermute | solution.py:771
  130.1 7.0 %collective-permute-start.7 = (s16[16,64,128]{2,1,0:T(8,128)(2,1)S(1)}, s16[16,64,128]{2,1,0:T(8,128)(2,1)S(1)}, u32[]{:S(2)}, u32[]{:S(2)}) collective-permute-start(s16[16,64,128]{2,1,0:T(8,128)(2,1)S(1)} %get-tuple-element.66), channel_id=1, source_target_pairs={{16,0},{32,16},{48,32},{64,48},{80,64},{96,80},{112,96},{0,112},{1... | collective-permute-start | bytes 786440 | tf_op jit(solution)/shard_map/ppermute | solution.py:772
  138.4 7.7 %collective-permute-start.8 = (s16[4,64,128]{2,1,0:T(8,128)(2,1)S(1)}, s16[4,64,128]{2,1,0:T(8,128)(2,1)S(1)}, u32[]{:S(2)}, u32[]{:S(2)}) collective-permute-start(s16[4,64,128]{2,1,0:T(8,128)(2,1)S(1)} %get-tuple-element.68), channel_id=1, source_target_pairs={{0,1},{1,2},{2,3},{3,4},{4,5},{5,6},{6,7},{7,8},{8,9},{9,10},{10,1... | collective-permute-start | bytes 196616 | tf_op jit(solution)/shard_map/ppermute | solution.py:771
  138.5 7.6 %collective-permute-start.9 = (s16[4,64,128]{2,1,0:T(8,128)(2,1)S(1)}, s16[4,64,128]{2,1,0:T(8,128)(2,1)S(1)}, u32[]{:S(2)}, u32[]{:S(2)}) collective-permute-start(s16[4,64,128]{2,1,0:T(8,128)(2,1)S(1)} %get-tuple-element.69), channel_id=1, source_target_pairs={{1,0},{2,1},{3,2},{4,3},{5,4},{6,5},{7,6},{8,7},{9,8},{10,9},{11,1... | collective-permute-start | bytes 196616 | tf_op jit(solution)/shard_map/ppermute | solution.py:772
  147.4 14.7 %collective-permute-start.12 = (s16[1056,128]{1,0:T(8,128)(2,1)S(1)}, s16[1056,128]{1,0:T(8,128)(2,1)S(1)}, u32[]{:S(2)}, u32[]{:S(2)}) collective-permute-start(s16[1056,128]{1,0:T(8,128)(2,1)S(1)} %finish.1.refs_0_), channel_id=1, source_target_pairs={{96,0},{112,16},{0,32},{16,48},{32,64},{48,80},{64,96},{80,112},{9... | collective-permute-start | bytes 811016 | tf_op jit(solution)/shard_map/ppermute | solution.py:778
  147.5 14.6 %collective-permute-start.11 = (s16[1056,128]{1,0:T(8,128)(2,1)S(1)}, s16[1056,128]{1,0:T(8,128)(2,1)S(1)}, u32[]{:S(2)}, u32[]{:S(2)}) collective-permute-start(s16[1056,128]{1,0:T(8,128)(2,1)S(1)} %finish.1.refs_0_), channel_id=1, source_target_pairs={{64,0},{80,16},{96,32},{112,48},{0,64},{16,80},{32,96},{48,112},{6... | collective-permute-start | bytes 811016 | tf_op jit(solution)/shard_map/ppermute | solution.py:778
  148.2 14.6 %collective-permute-start.10 = (s16[1056,128]{1,0:T(8,128)(2,1)S(1)}, s16[1056,128]{1,0:T(8,128)(2,1)S(1)}, u32[]{:S(2)}, u32[]{:S(2)}) collective-permute-start(s16[1056,128]{1,0:T(8,128)(2,1)S(1)} %finish.1.refs_0_), channel_id=1, source_target_pairs={{32,0},{48,16},{64,32},{80,48},{96,64},{112,80},{0,96},{16,112},{3... | collective-permute-start | bytes 811016 | tf_op jit(solution)/shard_map/ppermute | solution.py:778
  150.7 12.1 %collective-permute-start.13 = (s16[1056,128]{1,0:T(8,128)(2,1)S(1)}, s16[1056,128]{1,0:T(8,128)(2,1)S(1)}, u32[]{:S(2)}, u32[]{:S(2)}) collective-permute-start(s16[1056,128]{1,0:T(8,128)(2,1)S(1)} %finish.1.refs_0_), channel_id=1, source_target_pairs={{0,16},{16,0},{32,48},{48,32},{64,80},{80,64},{96,112},{112,96},{1... | collective-permute-start | bytes 811016 | tf_op jit(solution)/shard_map/ppermute | solution.py:781
  162.1 1.5 collective-permute-start.16
  162.1 1.9 %collective-permute-start.15 = (s16[1056,128]{1,0:T(8,128)(2,1)S(1)}, s16[1056,128]{1,0:T(8,128)(2,1)S(1)}, u32[]{:S(2)}, u32[]{:S(2)}) collective-permute-start(s16[1056,128]{1,0:T(8,128)(2,1)S(1)} %collective-permute-done.11.refs_2_), channel_id=1, source_target_pairs={{0,16},{16,0},{32,48},{48,32},{64,80},{80,64},{96,112},{112,96},{1... | collective-permute-start | bytes 811016 | tf_op jit(solution)/shard_map/ppermute | solution.py:781
  162.8 1.6 collective-permute-start.14

commit v4 on v3

--- a/solution.py
+++ b/solution.py
@@ -150,15 +150,19 @@
 
 
 def pack_kernel(target_ref, pieces_ref, out_ref, swap_ref):
-    swap_ref[...] = digit_swap((512, 512))
-    count = pieces_ref.shape[0]
-
-    def four_pieces(group, carry):
+    group = pl.program_id(0)
+    count = target_ref.shape[0]
+
+    @pl.when(group == 0)
+    def _():
+        swap_ref[...] = digit_swap((512, 512))
+
+    def four_pieces():
         rows = []
         for k in range(4):
             for half in range(2):
                 rows.append(jnp.concatenate(
-                    [pieces_ref[group * 4 + k, q, :, half * 128:(half + 1) * 128] for q in range(4)], axis=1))
+                    [pieces_ref[k, q, :, half * 128:(half + 1) * 128] for q in range(4)], axis=1))
         mixed = jnp.dot(jnp.concatenate(rows, axis=0), swap_ref[...], preferred_element_type=F32).astype(BF16)
         for k in range(4):
             piece = group * 4 + k
@@ -171,16 +175,16 @@
                 first = (k * 2 + half) * NY
                 for part in range(4):
                     out_ref[half * 4 + part, slot] = mixed[first:first + NY, part * 128:(part + 1) * 128]
-        return carry
-
-    lax.fori_loop(0, count // 4, four_pieces, 0)
+
+    four_pieces()
 
 
 def pack_pieces(targets, pieces, block_count):
     return pl.pallas_call(
         pack_kernel,
+        grid=(pieces.shape[0] // 4,),
         out_shape=jax.ShapeDtypeStruct((VIEWS, block_count * CAP, NY, 128), BF16),
-        in_specs=smem(1) + vmem(1),
+        in_specs=smem(1) + [pl.BlockSpec((4,) + pieces.shape[1:], lambda group: (group, 0, 0, 0))],
         out_specs=vmem(1)[0],
         scratch_shapes=[pltpu.VMEM((512, 512), BF16)],
         name="pack",
@@ -438,7 +442,7 @@
 
 
 def per_view(*shape):
-    return pl.BlockSpec((1,) + shape, lambda view: (view,) + (0,) * len(shape))
+    return pl.BlockSpec((2,) + shape, lambda step: (step,) + (0,) * len(shape))
 
 
 PARTIAL_SHAPES = (
@@ -452,29 +456,30 @@
 def first_adjoint_kernel(start_ref, source_ref, place_ref, inverse_ref, offset_ref, incoming_ref, blurred_ref, kyt_ref,
                          kxt_ref, bza_ref, main_ref, tail_ref, to_left_ref, to_right_ref, average_ref, total_ref,
                          depth_ref, swap_ref):
-    view = pl.program_id(0)
-
-    @pl.when(view == 0)
+    step = pl.program_id(0)
+
+    @pl.when(step == 0)
     def _():
         swap_ref[...] = digit_swap((512, 512))
 
-    for slot in range(SLOTS):
+    for slot in range(2 * SLOTS):
         total_ref[slot] = jnp.zeros((NY, 128), F32)
 
     def add(entry, carry):
         place = place_ref[entry]
-        piece = incoming_ref[source_ref[entry] - view * incoming_ref.shape[0]].astype(F32)
-        slot = place - view * SLOTS
+        piece = incoming_ref[source_ref[entry] - step * incoming_ref.shape[0]].astype(F32)
+        slot = place - step * (2 * SLOTS)
         total_ref[slot] = total_ref[slot] + piece * inverse_ref[place]
         return carry
 
-    lax.fori_loop(start_ref[view], start_ref[view + 1], add, 0)
+    lax.fori_loop(start_ref[step * 2], start_ref[step * 2 + 2], add, 0)
     rows = []
-    for r in range(4):
-        rows.append(jnp.concatenate([total_ref[h * 4 + r].astype(BF16) for h in range(4)], axis=1))
+    for r in range(8):
+        rows.append(jnp.concatenate(
+            [total_ref[r // 4 * SLOTS + h * 4 + r % 4].astype(BF16) for h in range(4)], axis=1))
     mixed = jnp.dot(jnp.concatenate(rows, axis=0), swap_ref[...], preferred_element_type=F32)
-    for r in range(4):
-        lanes = slice(r * 128, r * 128 + 128)
+    for r in range(8):
+        lanes = slice(r % 4 * 128, r % 4 * 128 + 128)
         for m in range(8):
             first = r * NY + m * 8
             ends = []
@@ -483,27 +488,28 @@
                                        mixed[first:first + 8, (q + 1) * 128:(q + 2) * 128]))
             for odd in range(2):
                 quad = 2 * m + odd
-                average_ref[0, quad * 16:quad * 16 + 16, lanes] = jnp.concatenate(
+                average_ref[r // 4, quad * 16:quad * 16 + 16, lanes] = jnp.concatenate(
                     [ends[0][odd], ends[1][odd]], axis=0).astype(BF16)
-    quotient = average_ref[0].astype(F32) / (blurred_ref[0].astype(F32) + offset_ref[view])
-    adjoint_plane(view, quotient, kyt_ref[0], kxt_ref[0], depth_ref)
-
-    @pl.when(view == VIEWS - 1)
+    quotients = [average_ref[k].astype(F32) / (blurred_ref[k].astype(F32) + offset_ref[step * 2 + k]) for k in range(2)]
+    for k in range(2):
+        adjoint_plane(step * 2 + k, quotients[k], kyt_ref[k], kxt_ref[k], depth_ref)
+
+    @pl.when(step == VIEWS // 2 - 1)
     def _():
         scale = tall(32767.0 / partial_bound(offset_ref))
         adjoint_depth(scale, bza_ref, depth_ref, main_ref, tail_ref, to_left_ref, to_right_ref)
 
 
 def first_adjoint(start, source, place, inverse, offset, incoming, blurred, kyt, kxt, bza):
-    held = incoming.shape[0] // VIEWS
+    share = incoming.shape[0] // (VIEWS // 2)
     return pl.pallas_call(
         first_adjoint_kernel,
-        grid=(VIEWS,),
+        grid=(VIEWS // 2,),
         out_shape=PARTIAL_SHAPES + (jax.ShapeDtypeStruct((VIEWS, ROWS, 2 * ROWS), BF16),),
-        in_specs=smem(5) + [pl.BlockSpec((held, NY, 128), lambda view: (view, 0, 0)), per_view(ROWS, 2 * ROWS),
+        in_specs=smem(5) + [pl.BlockSpec((share, NY, 128), lambda view: (view, 0, 0)), per_view(ROWS, 2 * ROWS),
                             per_view(ROWS, ROWS), per_view(128, ROWS)] + vmem(1),
         out_specs=tuple(vmem(4)) + (per_view(ROWS, 2 * ROWS),),
-        scratch_shapes=[pltpu.VMEM((SLOTS, NY, 128), F32), pltpu.VMEM((QUADS, VIEWS * 64, ROWS), BF16),
+        scratch_shapes=[pltpu.VMEM((2 * SLOTS, NY, 128), F32), pltpu.VMEM((QUADS, VIEWS * 64, ROWS), BF16),
                         pltpu.VMEM((512, 512), BF16)],
         name="first_adjoint",
         compiler_params=room(60),
@@ -581,9 +587,9 @@
                   estimate_tail_ref, scale_main_ref, scale_tail_ref, bzf_ref, bza_ref, average_ref, ky_ref, kx_ref,
                   kyt_ref, kxt_ref, own_estimate_ref, own_ref, own_tail_ref, to_left_ref, to_right_ref, new_main_ref,
                   tail_estimate_ref, planes_ref, depth_ref):
-    view = pl.program_id(0)
-
-    @pl.when(view == 0)
+    step = pl.program_id(0)
+
+    @pl.when(step == 0)
     def _():
         block = lane_block((64, 128))
         steps = depth_steps(partial_bound(offset_ref), edge_ref)
@@ -602,10 +608,13 @@
         lax.fori_loop(0, QUADS, renew, 0)
         forward_depth(new_main_ref, tail_estimate_ref, bzf_ref, planes_ref)
 
-    blurred = forward_plane(view, planes_ref, ky_ref[0], kx_ref[0]) + offset_ref[view]
-    adjoint_plane(view, average_ref[0].astype(F32) / blurred, kyt_ref[0], kxt_ref[0], depth_ref)
-
-    @pl.when(view == VIEWS - 1)
+    views = [step * 2, step * 2 + 1]
+    blurred = [forward_plane(views[k], planes_ref, ky_ref[k], kx_ref[k]) + offset_ref[views[k]] for k in range(2)]
+    quotients = [average_ref[k].astype(F32) / blurred[k] for k in range(2)]
+    for k in range(2):
+        adjoint_plane(views[k], quotients[k], kyt_ref[k], kxt_ref[k], depth_ref)
+
+    @pl.when(step == VIEWS // 2 - 1)
     def _():
         scale = tall(32767.0 / partial_bound(offset_ref))
         adjoint_depth(scale, bza_ref, depth_ref, own_ref, own_tail_ref, to_left_ref, to_right_ref, last=True)
@@ -614,7 +623,7 @@
 def second(offset, edges, *operands):
     return pl.pallas_call(
         second_kernel,
-        grid=(VIEWS,),
+        grid=(VIEWS // 2,),
         out_shape=(held((QUADS, 64, 128), F32),) * 3 + (held((QUADS, 64, 128), I16),) * 2,
         in_specs=smem(2) + vmem(10) + [per_view(ROWS, 2 * ROWS), per_view(ROWS, ROWS), per_view(ROWS, 128),
                                        per_view(ROWS, ROWS), per_view(128, ROWS)],
@@ -799,11 +808,10 @@
 
     index = my_view.reshape(1).astype(I32)
     low, high = window_ends(index, estimate0)
+    own_targets = lax.dynamic_slice(targets, (my_view, my_block, 0), (1, 1, SLOTS)).reshape(SLOTS)
+    outgoing = pack_pieces(own_targets, pieces[0], block_count)
+    low, high, outgoing = lax.optimization_barrier((low, high, outgoing))
     from_low, from_high = to_neighbours(high, low, "block")
-
-    own_targets = lax.dynamic_slice(targets, (my_view, my_block, 0), (1, 1, SLOTS)).reshape(SLOTS)
-    own_targets, low, high = lax.optimization_barrier((own_targets, low, high))
-    outgoing = pack_pieces(own_targets, pieces[0], block_count)
     incoming = lax.all_to_all(outgoing.reshape(VIEWS * block_count, CAP, NY, 128), ("view", "block"), 0, 0, tiled=True)
     incoming = incoming.reshape(VIEWS * block_count * CAP, NY, 128)
 

time: 172 us -> 177 us (1.029)
  waiting for transfers between devices: 39.1 us -> 45.6 us
  Pallas kernels: 76.9 us -> 73 us
    ppermute x5, waiting for transfers between devices: 18 us -> 33.8 us  [to_neighbours(): lax.ppermute(upward, axis, [(i, (i + 1) % count) for i in range(count)])]
    all_to_all x1, waiting for transfers between devices: 7.9 us -> 0.01 us  [program(): lax.all_to_all(outgoing.reshape(VIEWS * block_count, CAP, NY, 128), ('vie...]
    pallas_call x3, Pallas kernels: 37.2 us -> 33.4 us  [the longest x1 16.5 us: second(): pl.pallas_call(second_kernel, grid=(VIEWS // 2,), out_shape=(held((QUADS,...]
  transfers between devices with their start and end apart: 18 -> 18, of which waited for: 10 -> 10; matrix products, arithmetic and copies ran while one was open for 9% -> 9% of each run, Pallas kernels for 19% -> 15%
where the time goes in v4:
time: 177 us; the launch traced here: 175 us
  Pallas kernels  73 us (41%)
  waiting for transfers between devices  45.6 us (26%)
  starting transfers between devices  39.1 us (22%)
  local copies, waits for them, and re-layouts  8.79 us (5%)
  other arithmetic  8.27 us (5%)
    ppermute x5, waiting for transfers between devices, to_neighbours(): lax.ppermute(upward, axis, [(i, (i + 1) % count) for i in range(count)])  33.8 us
    ppermute x5, starting transfers between devices, to_neighbours(): lax.ppermute(downward, axis, [((i + 1) % count, i) for i in range(count)])  21 us
    pallas_call x1, Pallas kernels, second(): pl.pallas_call(second_kernel, grid=(VIEWS // 2,), out_shape=(held((QUADS,...  16.5 us
    all_to_all x1, starting transfers between devices, program(): lax.all_to_all(outgoing.reshape(VIEWS * block_count, CAP, NY, 128), ('vie...  11.7 us
    pallas_call x1, Pallas kernels, first_adjoint(): pl.pallas_call(first_adjoint_kernel, grid=(VIEWS // 2,), out_shape=PARTIA...  11.2 us
    pallas_call x1, Pallas kernels, forward(): pl.pallas_call(forward_kernel, out_shape=(jax.ShapeDtypeStruct((VIEWS, RO...  10.3 us
    ppermute x3, waiting for transfers between devices, gather_parts(): lax.ppermute(own, 'view', [((i + 2 * step) % VIEWS, i) for i in range(VIE...  10.2 us
    pallas_call x1, Pallas kernels, build_bands(): pl.pallas_call(band_kernel, out_shape=(jax.ShapeDtypeStruct((VIEWS, ROWS,...  6.78 us
  transfers between devices with their start and end apart: 18, of which 10 were waited for; matrix products, arithmetic and copies ran while one was open for 9% of the time, Pallas kernels for 15%

profile of v4, /device:TPU:0, one launch (start us, length us, event | category | flops | bytes accessed | tf_op | source)
XLA Modules:
  0.0 175.1 jit_solution(14409275142335604333)
XLA Ops:
  0.0 0.7 reduce
  0.8 2.8 %ends.1 = (bf16[8,64,128]{2,1,0:T(8,128)(2,1)}, bf16[8,64,128]{2,1,0:T(8,128)(2,1)}) custom-call(s32[1]{0:T(128)} %bitcast.index_ref, f32[64,64,256]{2,1,0:T(8,128)} %estimate_ref.1, f32[64,64,256]{2,1,0:T(8,128)} %estimate_ref.1), custom_call_target="tpu_custom_call" | custom-call | tf_op jit(solution)/shard_map/ends/pallas_call | solution.py:258
  3.6 0.6 dynamic-slice_bitcast_fusion.target_ref
  4.2 5.7 %pack.1 = bf16[8,32,64,128]{3,2,1,0:T(8,128)(2,1)} custom-call(s32[16]{0:T(128)} %dynamic-slice_bitcast_fusion.target_ref, bf16[16,4,64,256]{3,2,1,0:T(8,128)(2,1)} %bitcast.37), custom_call_target="tpu_custom_call" | custom-call | tf_op jit(solution)/shard_map/pack/pallas_call | solution.py:183
  9.9 11.7 %all-to-all-start = ((bf16[128,2,64,128]{3,2,1,0:T(8,128)(2,1)}), bf16[128,2,64,128]{3,2,1,0:T(8,128)(2,1)}, u32[]{:S(2)}, u32[]{:S(2)}) async-start(bf16[128,2,64,128]{3,2,1,0:T(8,128)(2,1)} %bitcast.36), calls=%async_computation | async-start | bytes 8388608 | tf_op jit(solution)/shard_map/all_to_all | solution.py:815
  21.6 1.0 collective-permute-start
  22.6 4.5 %collective-permute-start.1 = (bf16[8,64,128]{2,1,0:T(8,128)(2,1)S(1)}, bf16[8,64,128]{2,1,0:T(8,128)(2,1)S(1)}, u32[]{:S(2)}, u32[]{:S(2)}) collective-permute-start(bf16[8,64,128]{2,1,0:T(8,128)(2,1)S(1)} %copy-done.10), channel_id=1, source_target_pairs={{1,0},{2,1},{3,2},{4,3},{5,4},{6,5},{7,6},{8,7},{9,8},{10,9},{11,1... | collective-permute-start | bytes 393224 | tf_op jit(solution)/shard_map/ppermute | solution.py:781
  27.2 2.5 %convert_reduce_fusion = s32[8,16,16]{2,1,0:T(8,128)S(1)} fusion(s32[8,16,16]{2,1,0:T(8,128)S(1)} %reshape_squeeze.3, pred[16,16]{1,0:T(8,128)(4,1)S(1)} %iota_compare_fusion.6), kind=kLoop, calls=%fused_computation.2 | loop fusion | flops 129024 | bytes 16640 | tf_op jit(solution)/shard_map/reduce_sum | solution.py:825
  29.8 0.4 select_reduce_fusion.2
  30.2 0.1 copy.32
  30.5 0.4 fusion
  31.6 0.1 sub.102
  31.7 0.1 copy.37
  31.9 0.1 broadcast_in_dim.292
  32.1 0.2 slice_reduce_fusion.19
  32.3 0.5 slice_reduce_fusion.20
  32.9 0.8 multiply_reduce_fusion
  33.8 0.1 copy.39
  33.9 0.7 convert_reduce_fusion.3.start_ref
  34.6 0.2 convert_reduce_fusion.2
  34.8 0.1 convert_reduce_fusion.1
  34.9 0.1 select_reduce_fusion.4
  35.0 0.2 broadcast_multiply_fusion
  35.2 0.2 fusion.32
  35.5 0.3 maximum_bitcast_fusion
  35.8 0.7 add_convert_fusion.edge_ref
  36.6 0.1 slice.145
  36.7 6.0 %window.1.main_ref.estimate_main_ref = f32[2,1024,128]{2,1,0:T(8,128)} custom-call(s32[1]{0:T(128)} %bitcast.index_ref, f32[64,64,256]{2,1,0:T(8,128)} %estimate_ref.1), custom_call_target="tpu_custom_call" | custom-call | tf_op jit(solution)/shard_map/window/pallas_call | solution.py:221
  42.7 0.6 reshape.278.shift_ref
  43.3 0.7 reshape.277.taps_ref
  44.0 0.7 reshape.270.rows_ref
  44.7 0.6 div.30.inverse_ref
  45.2 0.3 reshape.280
  45.6 0.2 reshape.275
  45.8 6.8 %bands.1 = (bf16[8,256,256]{2,1,0:T(8,128)(2,1)}, bf16[8,256,256]{2,1,0:T(8,128)(2,1)}, bf16[8,256,128]{2,1,0:T(8,128)(2,1)}, bf16[8,128,256]{2,1,0:T(8,128)(2,1...) custom-call(f32[504]{0:T(512)} %reshape.277.taps_ref, s32[24]{0:T(128)} %reshape.278.shift_ref), custom_call_target="tpu_custom_call" | custom-call | tf_op jit(solution)/shard_map/bands/pallas_call | solution.py:136
  52.6 0.7 broadcast_in_dim.296
  53.4 0.9 broadcast_in_dim.295
  54.3 3.8 %weights.1 = (f32[2,1024,128]{2,1,0:T(8,128)}, f32[16,64,128]{2,1,0:T(8,128)}) custom-call(f32[512]{0:T(512)} %reshape.270.rows_ref, f32[8,2,64,128]{3,2,1,0:T(8,128)} %bitcast.38, f32[8,64,128]{2,1,0:T(8,128)} %bitcast.40), custom_call_target="tpu_custom_call" | custom-call | tf_op jit(solution)/shard_map/weights/pallas_call | solution.py:307
  58.1 0.7 select_reduce_fusion
  58.8 15.8 %collective-permute-done.from_low_ref = bf16[8,64,128]{2,1,0:T(8,128)(2,1)S(1)} collective-permute-done((bf16[8,64,128]{2,1,0:T(8,128)(2,1)S(1)}, bf16[8,64,128]{2,1,0:T(8,128)(2,1)S(1)}, u32[]{:S(2)}, u32[]{:S(2)}) %collective-permute-start) | collective-permute-done | bytes 131104 | tf_op jit(solution)/shard_map/ppermute | solution.py:780
  74.6 0.6 copy-done.4
  75.3 10.3 %forward.1 = (bf16[8,256,512]{2,1,0:T(8,128)(2,1)}, f32[16,64,128]{2,1,0:T(8,128)}) custom-call(f32[4]{0:T(128)} %add_convert_fusion.edge_ref, f32[2,1024,128]{2,1,0:T(8,128)} %window.1.main_ref.estimate_main_ref, bf16[8,64,128]{2,1,0:T(8,128)(2,1)} %copy-done.4, bf16[8,64,128]{2,1,0:T(8,128)(2,1)} %copy-done.5, bf16[512,192]{1,0:T(8,128)(2,1)} %get-tuple-element.48.bzf_ref, ...), custom_call_target="tpu_custom_call" | custom-call | tf_op jit(solution)/shard_map/forward/pallas_call | solution.py:431
  85.7 11.2 %first_adjoint.1 = (f32[2,1024,128]{2,1,0:T(8,128)S(1)}, f32[16,64,128]{2,1,0:T(8,128)S(1)}, s16[24,64,128]{2,1,0:T(8,128)(2,1)S(1)}, s16[24,64,128]{2,1,0:T(8,128)(2,1)S(1)}, bf16[8,256,512]{2,1,0:T(8,128)(2,1)}) custom-call(s32[9]{0:T(128)} %convert_reduce_fusion.3.start_ref, s32[256]{0:T(256)} %get-tuple-element.97.source_ref, ...), custom_call_target="tpu_custom_call" | custom-call | tf_op jit(solution)/shard_map/first_adjoint/pallas_call | solution.py:505
  96.9 3.0 %collective-permute-start.3 = (s16[24,64,128]{2,1,0:T(8,128)(2,1)S(1)}, s16[24,64,128]{2,1,0:T(8,128)(2,1)S(1)}, u32[]{:S(2)}, u32[]{:S(2)}) collective-permute-start(s16[24,64,128]{2,1,0:T(8,128)(2,1)S(1)} %get-tuple-element.58), channel_id=1, source_target_pairs={{16,0},{32,16},{48,32},{64,48},{80,64},{96,80},{112,96},{0,112},{1... | collective-permute-start | bytes 1179656 | tf_op jit(solution)/shard_map/ppermute | solution.py:781
  99.8 5.5 %collective-permute-done.2.from_left_ref = s16[24,64,128]{2,1,0:T(8,128)(2,1)S(1)} collective-permute-done((s16[24,64,128]{2,1,0:T(8,128)(2,1)S(1)}, s16[24,64,128]{2,1,0:T(8,128)(2,1)S(1)}, u32[]{:S(2)}, u32[]{:S(2)}) %collective-permute-start.2) | collective-permute-done | bytes 393248 | tf_op jit(solution)/shard_map/ppermute | solution.py:780
  105.3 1.7 join_columns.1
  107.1 5.3 %collective-permute-start.5 = (s16[16,64,128]{2,1,0:T(8,128)(2,1)S(1)}, s16[16,64,128]{2,1,0:T(8,128)(2,1)S(1)}, u32[]{:S(2)}, u32[]{:S(2)}) collective-permute-start(s16[16,64,128]{2,1,0:T(8,128)(2,1)S(1)} %get-tuple-element.62), channel_id=1, source_target_pairs={{1,0},{2,1},{3,2},{4,3},{5,4},{6,5},{7,6},{8,7},{9,8},{10,9},{11,1... | collective-permute-start | bytes 786440 | tf_op jit(solution)/shard_map/ppermute | solution.py:781
  112.4 6.3 %collective-permute-done.4.from_low_ref = s16[16,64,128]{2,1,0:T(8,128)(2,1)S(1)} collective-permute-done((s16[16,64,128]{2,1,0:T(8,128)(2,1)S(1)}, s16[16,64,128]{2,1,0:T(8,128)(2,1)S(1)}, u32[]{:S(2)}, u32[]{:S(2)}) %collective-permute-start.4) | collective-permute-done | bytes 262176 | tf_op jit(solution)/shard_map/ppermute | solution.py:780
  118.7 16.5 %second.1 = (f32[16,64,128]{2,1,0:T(8,128)S(1)}, f32[16,64,128]{2,1,0:T(8,128)S(1)}, f32[16,64,128]{2,1,0:T(8,128)S(1)}, s16[16,64,128]{2,1,0:T(8,128)(2,1)S(1)}, s16[16,64,128]{2,1,0:T(8,128)(2,1)S(1)}) custom-call(f32[8]{0:T(128)} %offset_ref.9, f32[4]{0:T(128)} %add_convert_fusion.edge_ref, f32[2,1024,128]{2,1,0:T(8,128)S(1)} %get-tuple-element.59.part_main_ref, ...), custom_call_target="tpu_custom_call" | custom-call | tf_op jit(solution)/shard_map/second/pallas_call | solution.py:624
  135.3 2.9 %collective-permute-start.7 = (s16[16,64,128]{2,1,0:T(8,128)(2,1)S(1)}, s16[16,64,128]{2,1,0:T(8,128)(2,1)S(1)}, u32[]{:S(2)}, u32[]{:S(2)}) collective-permute-start(s16[16,64,128]{2,1,0:T(8,128)(2,1)S(1)} %get-tuple-element.70), channel_id=1, source_target_pairs={{16,0},{32,16},{48,32},{64,48},{80,64},{96,80},{112,96},{0,112},{1... | collective-permute-start | bytes 786440 | tf_op jit(solution)/shard_map/ppermute | solution.py:781
  138.2 4.1 %collective-permute-done.6.from_left_ref = s16[16,64,128]{2,1,0:T(8,128)(2,1)S(1)} collective-permute-done((s16[16,64,128]{2,1,0:T(8,128)(2,1)S(1)}, s16[16,64,128]{2,1,0:T(8,128)(2,1)S(1)}, u32[]{:S(2)}, u32[]{:S(2)}) %collective-permute-start.6) | collective-permute-done | bytes 262176 | tf_op jit(solution)/shard_map/ppermute | solution.py:780
  142.3 1.3 join_own.1
  143.7 5.3 %collective-permute-start.9 = (s16[4,64,128]{2,1,0:T(8,128)(2,1)S(1)}, s16[4,64,128]{2,1,0:T(8,128)(2,1)S(1)}, u32[]{:S(2)}, u32[]{:S(2)}) collective-permute-start(s16[4,64,128]{2,1,0:T(8,128)(2,1)S(1)} %get-tuple-element.73), channel_id=1, source_target_pairs={{1,0},{2,1},{3,2},{4,3},{5,4},{6,5},{7,6},{8,7},{9,8},{10,9},{11,1... | collective-permute-start | bytes 196616 | tf_op jit(solution)/shard_map/ppermute | solution.py:781
  149.0 2.2 %collective-permute-done.8.from_low_ref = s16[4,64,128]{2,1,0:T(8,128)(2,1)S(1)} collective-permute-done((s16[4,64,128]{2,1,0:T(8,128)(2,1)S(1)}, s16[4,64,128]{2,1,0:T(8,128)(2,1)S(1)}, u32[]{:S(2)}, u32[]{:S(2)}) %collective-permute-start.8) | collective-permute-done | bytes 65568 | tf_op jit(solution)/shard_map/ppermute | solution.py:780
  151.3 1.3 finish.1.refs_0_
  152.7 1.7 collective-permute-start.11
  154.4 2.5 %collective-permute-start.10 = (s16[1056,128]{1,0:T(8,128)(2,1)S(1)}, s16[1056,128]{1,0:T(8,128)(2,1)S(1)}, u32[]{:S(2)}, u32[]{:S(2)}) collective-permute-start(s16[1056,128]{1,0:T(8,128)(2,1)S(1)} %finish.1.refs_0_), channel_id=1, source_target_pairs={{32,0},{48,16},{64,32},{80,48},{96,64},{112,80},{0,96},{16,112},{3... | collective-permute-start | bytes 811016 | tf_op jit(solution)/shard_map/ppermute | solution.py:787
  156.9 5.6 %collective-permute-done.12.refs_3_ = s16[1056,128]{1,0:T(8,128)(2,1)S(1)} collective-permute-done((s16[1056,128]{1,0:T(8,128)(2,1)S(1)}, s16[1056,128]{1,0:T(8,128)(2,1)S(1)}, u32[]{:S(2)}, u32[]{:S(2)}) %collective-permute-start.12) | collective-permute-done | bytes 270368 | tf_op jit(solution)/shard_map/ppermute | solution.py:787
  162.5 3.8 %collective-permute-done.11.refs_2_ = s16[1056,128]{1,0:T(8,128)(2,1)S(1)} collective-permute-done((s16[1056,128]{1,0:T(8,128)(2,1)S(1)}, s16[1056,128]{1,0:T(8,128)(2,1)S(1)}, u32[]{:S(2)}, u32[]{:S(2)}) %collective-permute-start.11) | collective-permute-done | bytes 270368 | tf_op jit(solution)/shard_map/ppermute | solution.py:787
  166.3 0.9 collective-permute-start.15
  167.2 0.8 collective-permute-done.10.refs_1_
  168.0 0.4 collective-permute-done.15.refs_6_
  168.4 1.2 collective-permute-done.14.refs_5_
  169.6 5.5 %assemble.1 = f32[4,4,4,64,256]{4,3,2,1,0:T(8,128)} custom-call(s32[1]{0:T(128)} %bitcast.index_ref, s16[1056,128]{1,0:T(8,128)(2,1)S(1)} %finish.1.refs_0_, s16[1056,128]{1,0:T(8,128)(2,1)S(1)} %collective-permute-done.10.refs_1_, s16[1056,128]{1,0:T(8,128)(2,1)S(1)} %collective-permute-done.11.refs_2_, ...), custom_call_target="tpu_custom_call" | custom-call | tf_op jit(solution)/shard_map/assemble/pallas_call | solution.py:766
  (75 shorter events, 1.9 us)
Async XLA Ops:
  9.9 11.8 %copy-start.11 = (bf16[8,64,128]{2,1,0:T(8,128)(2,1)S(1)}, bf16[8,64,128]{2,1,0:T(8,128)(2,1)}, u32[]{:S(2)}) copy-start(bf16[8,64,128]{2,1,0:T(8,128)(2,1)} %get-tuple-element.46) | copy-start | bytes 393220
  9.9 12.7 %copy-start.10 = (bf16[8,64,128]{2,1,0:T(8,128)(2,1)S(1)}, bf16[8,64,128]{2,1,0:T(8,128)(2,1)}, u32[]{:S(2)}) copy-start(bf16[8,64,128]{2,1,0:T(8,128)(2,1)} %get-tuple-element.47) | copy-start | bytes 393220
  9.9 17.2 %copy-start.7 = (s32[8,256,1]{1,2,0:T(1,128)S(1)}, s32[8,256,1]{1,2,0:T(1,128)}, u32[]{:S(2)}) copy-start(s32[8,256,1]{1,2,0:T(1,128)} %param.9) | copy-start | bytes 24580
  9.9 17.2 %copy-start.8 = (s32[8,256]{1,0:T(8,128)S(1)}, s32[8,256]{1,0:T(8,128)}, u32[]{:S(2)}) copy-start(s32[8,256]{1,0:T(8,128)} %param.10) | copy-start | bytes 24580
  9.9 21.0 %copy-start.6 = (f32[8,3,21]{2,0,1:T(8,128)S(1)}, f32[8,3,21]{2,0,1:T(8,128)}, u32[]{:S(2)}) copy-start(f32[8,3,21]{2,0,1:T(8,128)} %param.12) | copy-start | bytes 6052
  9.9 21.3 %copy-start.9 = (s32[8,3]{0,1:T(4,128)S(1)}, s32[8,3]{0,1:T(4,128)}, u32[]{:S(2)}) copy-start(s32[8,3]{0,1:T(4,128)} %param.11) | copy-start | bytes 292
  9.9 75.8 %all-to-all-start = ((bf16[128,2,64,128]{3,2,1,0:T(8,128)(2,1)}), bf16[128,2,64,128]{3,2,1,0:T(8,128)(2,1)}, u32[]{:S(2)}, u32[]{:S(2)}) async-start(bf16[128,2,64,128]{3,2,1,0:T(8,128)(2,1)} %bitcast.36), calls=%async_computation | async-start | bytes 8388608 | tf_op jit(solution)/shard_map/all_to_all | solution.py:815
  21.6 53.0 %collective-permute-start = (bf16[8,64,128]{2,1,0:T(8,128)(2,1)S(1)}, bf16[8,64,128]{2,1,0:T(8,128)(2,1)S(1)}, u32[]{:S(2)}, u32[]{:S(2)}) collective-permute-start(bf16[8,64,128]{2,1,0:T(8,128)(2,1)S(1)} %copy-done.11), channel_id=1, source_target_pairs={{0,1},{1,2},{2,3},{3,4},{4,5},{5,6},{6,7},{7,8},{8,9},{9,10},{10,1... | collective-permute-start | bytes 393224 | tf_op jit(solution)/shard_map/ppermute | solution.py:780
  22.6 52.0 %collective-permute-start.1 = (bf16[8,64,128]{2,1,0:T(8,128)(2,1)S(1)}, bf16[8,64,128]{2,1,0:T(8,128)(2,1)S(1)}, u32[]{:S(2)}, u32[]{:S(2)}) collective-permute-start(bf16[8,64,128]{2,1,0:T(8,128)(2,1)S(1)} %copy-done.10), channel_id=1, source_target_pairs={{1,0},{2,1},{3,2},{4,3},{5,4},{6,5},{7,6},{8,7},{9,8},{10,9},{11,1... | collective-permute-start | bytes 393224 | tf_op jit(solution)/shard_map/ppermute | solution.py:781
  74.6 0.7 copy-start.4
  74.6 0.7 copy-start.5
  85.7 19.6 %copy-start = (f32[4]{0:T(128)S(1)}, f32[4]{0:T(128)}, u32[]{:S(2)}) copy-start(f32[4]{0:T(128)} %add_convert_fusion.edge_ref) | copy-start | bytes 52
  85.7 19.6 %copy-start.2 = (f32[8]{0:T(128)S(1)}, f32[8]{0:T(128)}, u32[]{:S(2)}) copy-start(f32[8]{0:T(128)} %offset_ref.9) | copy-start | bytes 100
  96.9 8.4 %collective-permute-start.2 = (s16[24,64,128]{2,1,0:T(8,128)(2,1)S(1)}, s16[24,64,128]{2,1,0:T(8,128)(2,1)S(1)}, u32[]{:S(2)}, u32[]{:S(2)}) collective-permute-start(s16[24,64,128]{2,1,0:T(8,128)(2,1)S(1)} %get-tuple-element.57), channel_id=1, source_target_pairs={{0,16},{16,32},{32,48},{48,64},{64,80},{80,96},{96,112},{112,0},{1... | collective-permute-start | bytes 1179656 | tf_op jit(solution)/shard_map/ppermute | solution.py:780
  96.9 8.4 %collective-permute-start.3 = (s16[24,64,128]{2,1,0:T(8,128)(2,1)S(1)}, s16[24,64,128]{2,1,0:T(8,128)(2,1)S(1)}, u32[]{:S(2)}, u32[]{:S(2)}) collective-permute-start(s16[24,64,128]{2,1,0:T(8,128)(2,1)S(1)} %get-tuple-element.58), channel_id=1, source_target_pairs={{16,0},{32,16},{48,32},{64,48},{80,64},{96,80},{112,96},{0,112},{1... | collective-permute-start | bytes 1179656 | tf_op jit(solution)/shard_map/ppermute | solution.py:781
  107.0 11.7 %collective-permute-start.4 = (s16[16,64,128]{2,1,0:T(8,128)(2,1)S(1)}, s16[16,64,128]{2,1,0:T(8,128)(2,1)S(1)}, u32[]{:S(2)}, u32[]{:S(2)}) collective-permute-start(s16[16,64,128]{2,1,0:T(8,128)(2,1)S(1)} %get-tuple-element.61), channel_id=1, source_target_pairs={{0,1},{1,2},{2,3},{3,4},{4,5},{5,6},{6,7},{7,8},{8,9},{9,10},{10,1... | collective-permute-start | bytes 786440 | tf_op jit(solution)/shard_map/ppermute | solution.py:780
  107.1 11.6 %collective-permute-start.5 = (s16[16,64,128]{2,1,0:T(8,128)(2,1)S(1)}, s16[16,64,128]{2,1,0:T(8,128)(2,1)S(1)}, u32[]{:S(2)}, u32[]{:S(2)}) collective-permute-start(s16[16,64,128]{2,1,0:T(8,128)(2,1)S(1)} %get-tuple-element.62), channel_id=1, source_target_pairs={{1,0},{2,1},{3,2},{4,3},{5,4},{6,5},{7,6},{8,7},{9,8},{10,9},{11,1... | collective-permute-start | bytes 786440 | tf_op jit(solution)/shard_map/ppermute | solution.py:781
  118.7 23.6 %copy-start.1 = (f32[4]{0:T(128)S(1)}, f32[4]{0:T(128)}, u32[]{:S(2)}) copy-start(f32[4]{0:T(128)} %add_convert_fusion.edge_ref) | copy-start | bytes 52
  118.7 23.6 %copy-start.3 = (f32[8]{0:T(128)S(1)}, f32[8]{0:T(128)}, u32[]{:S(2)}) copy-start(f32[8]{0:T(128)} %offset_ref.9) | copy-start | bytes 100
  135.2 7.0 %collective-permute-start.6 = (s16[16,64,128]{2,1,0:T(8,128)(2,1)S(1)}, s16[16,64,128]{2,1,0:T(8,128)(2,1)S(1)}, u32[]{:S(2)}, u32[]{:S(2)}) collective-permute-start(s16[16,64,128]{2,1,0:T(8,128)(2,1)S(1)} %get-tuple-element.69), channel_id=1, source_target_pairs={{0,16},{16,32},{32,48},{48,64},{64,80},{80,96},{96,112},{112,0},{1... | collective-permute-start | bytes 786440 | tf_op jit(solution)/shard_map/ppermute | solution.py:780
  135.3 7.0 %collective-permute-start.7 = (s16[16,64,128]{2,1,0:T(8,128)(2,1)S(1)}, s16[16,64,128]{2,1,0:T(8,128)(2,1)S(1)}, u32[]{:S(2)}, u32[]{:S(2)}) collective-permute-start(s16[16,64,128]{2,1,0:T(8,128)(2,1)S(1)} %get-tuple-element.70), channel_id=1, source_target_pairs={{16,0},{32,16},{48,32},{64,48},{80,64},{96,80},{112,96},{0,112},{1... | collective-permute-start | bytes 786440 | tf_op jit(solution)/shard_map/ppermute | solution.py:781
  143.6 7.7 %collective-permute-start.8 = (s16[4,64,128]{2,1,0:T(8,128)(2,1)S(1)}, s16[4,64,128]{2,1,0:T(8,128)(2,1)S(1)}, u32[]{:S(2)}, u32[]{:S(2)}) collective-permute-start(s16[4,64,128]{2,1,0:T(8,128)(2,1)S(1)} %get-tuple-element.72), channel_id=1, source_target_pairs={{0,1},{1,2},{2,3},{3,4},{4,5},{5,6},{6,7},{7,8},{8,9},{9,10},{10,1... | collective-permute-start | bytes 196616 | tf_op jit(solution)/shard_map/ppermute | solution.py:780
  143.7 7.6 %collective-permute-start.9 = (s16[4,64,128]{2,1,0:T(8,128)(2,1)S(1)}, s16[4,64,128]{2,1,0:T(8,128)(2,1)S(1)}, u32[]{:S(2)}, u32[]{:S(2)}) collective-permute-start(s16[4,64,128]{2,1,0:T(8,128)(2,1)S(1)} %get-tuple-element.73), channel_id=1, source_target_pairs={{1,0},{2,1},{3,2},{4,3},{5,4},{6,5},{7,6},{8,7},{9,8},{10,9},{11,1... | collective-permute-start | bytes 196616 | tf_op jit(solution)/shard_map/ppermute | solution.py:781
  152.6 9.9 %collective-permute-start.12 = (s16[1056,128]{1,0:T(8,128)(2,1)S(1)}, s16[1056,128]{1,0:T(8,128)(2,1)S(1)}, u32[]{:S(2)}, u32[]{:S(2)}) collective-permute-start(s16[1056,128]{1,0:T(8,128)(2,1)S(1)} %finish.1.refs_0_), channel_id=1, source_target_pairs={{96,0},{112,16},{0,32},{16,48},{32,64},{48,80},{64,96},{80,112},{9... | collective-permute-start | bytes 811016 | tf_op jit(solution)/shard_map/ppermute | solution.py:787
  152.7 13.6 %collective-permute-start.11 = (s16[1056,128]{1,0:T(8,128)(2,1)S(1)}, s16[1056,128]{1,0:T(8,128)(2,1)S(1)}, u32[]{:S(2)}, u32[]{:S(2)}) collective-permute-start(s16[1056,128]{1,0:T(8,128)(2,1)S(1)} %finish.1.refs_0_), channel_id=1, source_target_pairs={{64,0},{80,16},{96,32},{112,48},{0,64},{16,80},{32,96},{48,112},{6... | collective-permute-start | bytes 811016 | tf_op jit(solution)/shard_map/ppermute | solution.py:787
  154.4 13.7 %collective-permute-start.10 = (s16[1056,128]{1,0:T(8,128)(2,1)S(1)}, s16[1056,128]{1,0:T(8,128)(2,1)S(1)}, u32[]{:S(2)}, u32[]{:S(2)}) collective-permute-start(s16[1056,128]{1,0:T(8,128)(2,1)S(1)} %finish.1.refs_0_), channel_id=1, source_target_pairs={{32,0},{48,16},{64,32},{80,48},{96,64},{112,80},{0,96},{16,112},{3... | collective-permute-start | bytes 811016 | tf_op jit(solution)/shard_map/ppermute | solution.py:787
  156.9 11.1 %collective-permute-start.13 = (s16[1056,128]{1,0:T(8,128)(2,1)S(1)}, s16[1056,128]{1,0:T(8,128)(2,1)S(1)}, u32[]{:S(2)}, u32[]{:S(2)}) collective-permute-start(s16[1056,128]{1,0:T(8,128)(2,1)S(1)} %finish.1.refs_0_), channel_id=1, source_target_pairs={{0,16},{16,0},{32,48},{48,32},{64,80},{80,64},{96,112},{112,96},{1... | collective-permute-start | bytes 811016 | tf_op jit(solution)/shard_map/ppermute | solution.py:790
  162.5 5.5 %collective-permute-start.16 = (s16[1056,128]{1,0:T(8,128)(2,1)S(1)}, s16[1056,128]{1,0:T(8,128)(2,1)S(1)}, u32[]{:S(2)}, u32[]{:S(2)}) collective-permute-start(s16[1056,128]{1,0:T(8,128)(2,1)S(1)} %collective-permute-done.12.refs_3_), channel_id=1, source_target_pairs={{0,16},{16,0},{32,48},{48,32},{64,80},{80,64},{96,112},{112,96},{1... | collective-permute-start | bytes 811016 | tf_op jit(solution)/shard_map/ppermute | solution.py:790
  166.3 2.1 %collective-permute-start.15 = (s16[1056,128]{1,0:T(8,128)(2,1)S(1)}, s16[1056,128]{1,0:T(8,128)(2,1)S(1)}, u32[]{:S(2)}, u32[]{:S(2)}) collective-permute-start(s16[1056,128]{1,0:T(8,128)(2,1)S(1)} %collective-permute-done.11.refs_2_), channel_id=1, source_target_pairs={{0,16},{16,0},{32,48},{48,32},{64,80},{80,64},{96,112},{112,96},{1... | collective-permute-start | bytes 811016 | tf_op jit(solution)/shard_map/ppermute | solution.py:790
  168.0 1.5 collective-permute-start.14

commit v5 on v4

--- a/solution.py
+++ b/solution.py
@@ -149,46 +149,78 @@
     )(taps, shifts)
 
 
-def pack_kernel(target_ref, pieces_ref, out_ref, swap_ref):
-    group = pl.program_id(0)
+def pack_kernel(index_ref, target_ref, pieces_ref, first_ref, last_ref, out_ref, low_ref, high_ref, stage_ref, swap_ref,
+                sent_ref):
+    step = pl.program_id(0)
     count = target_ref.shape[0]
 
-    @pl.when(group == 0)
+    @pl.when(step == 0)
     def _():
         swap_ref[...] = digit_swap((512, 512))
 
-    def four_pieces():
-        rows = []
+    rows = []
+    for k in range(4):
+        for half in range(2):
+            rows.append(jnp.concatenate(
+                [pieces_ref[k, q, :, half * 128:(half + 1) * 128] for q in range(4)], axis=1))
+    mixed = jnp.dot(jnp.concatenate(rows, axis=0), swap_ref[...], preferred_element_type=F32).astype(BF16)
+    for k in range(4):
+        piece = step * 4 + k
+        target = target_ref[piece]
+        rank = jnp.int32(0)
+        for other in range(count):
+            rank = rank + jnp.where((target_ref[other] == target) & (other < piece), 1, 0)
+        slot = target * CAP + rank
+        for half in range(2):
+            first = (k * 2 + half) * NY
+            for part in range(4):
+                stage_ref[piece, half * 4 + part] = mixed[first:first + NY, part * 128:(part + 1) * 128]
+        pltpu.make_async_copy(stage_ref.at[piece], out_ref.at[:, slot], sent_ref.at[piece]).start()
+
+    part = index_ref[0]
+    amount = (16 - PART * part + 256) % 256
+    lane = lax.broadcasted_iota(I32, (32, 128), 1)
+    column = part * PART - HALO + lane % 64
+    inside = (column >= 0) & (column < 256)
+    for source_ref, target_ref_out in ((first_ref, low_ref), (last_ref, high_ref)):
+        planes = []
         for k in range(4):
-            for half in range(2):
-                rows.append(jnp.concatenate(
-                    [pieces_ref[k, q, :, half * 128:(half + 1) * 128] for q in range(4)], axis=1))
-        mixed = jnp.dot(jnp.concatenate(rows, axis=0), swap_ref[...], preferred_element_type=F32).astype(BF16)
-        for k in range(4):
-            piece = group * 4 + k
-            target = target_ref[piece]
-            rank = jnp.int32(0)
-            for other in range(count):
-                rank = rank + jnp.where((target_ref[other] == target) & (other < piece), 1, 0)
-            slot = target * CAP + rank
-            for half in range(2):
-                first = (k * 2 + half) * NY
-                for part in range(4):
-                    out_ref[half * 4 + part, slot] = mixed[first:first + NY, part * 128:(part + 1) * 128]
-
-    four_pieces()
-
-
-def pack_pieces(targets, pieces, block_count):
+            plane = source_ref[k]
+            top = pltpu.roll(plane[:32], amount, 1)[:, :128]
+            bottom = pltpu.roll(plane[32:], (amount + 64) % 256, 1)[:, :128]
+            planes.append(jnp.where(inside, jnp.where(lane < 64, top, bottom), 0.0))
+        for m in range(4):
+            rows = slice(m * 8, m * 8 + 8)
+            front = swap_fours(planes[0][rows], planes[1][rows])
+            back = swap_fours(planes[2][rows], planes[3][rows])
+            for odd in range(2):
+                target_ref_out[m * 2 + odd, pl.ds(pl.multiple_of(step * 16, 16), 16), :] = jnp.concatenate(
+                    [front[odd], back[odd]], axis=0).astype(BF16)
+
+    @pl.when(step == 3)
+    def _():
+        for piece in range(count):
+            pltpu.make_async_copy(stage_ref.at[piece], out_ref.at[:, 0], sent_ref.at[piece]).wait()
+
+
+def pack_pieces(index, targets, pieces, estimate, block_count):
+    count = pieces.shape[0]
     return pl.pallas_call(
         pack_kernel,
-        grid=(pieces.shape[0] // 4,),
-        out_shape=jax.ShapeDtypeStruct((VIEWS, block_count * CAP, NY, 128), BF16),
-        in_specs=smem(1) + [pl.BlockSpec((4,) + pieces.shape[1:], lambda group: (group, 0, 0, 0))],
-        out_specs=vmem(1)[0],
-        scratch_shapes=[pltpu.VMEM((512, 512), BF16)],
+        grid=(4,),
+        out_shape=(
+            jax.ShapeDtypeStruct((VIEWS, block_count * CAP, NY, 128), BF16),
+            jax.ShapeDtypeStruct((8, 64, 128), BF16),
+            jax.ShapeDtypeStruct((8, 64, 128), BF16),
+        ),
+        in_specs=smem(2) + [pl.BlockSpec((4,) + pieces.shape[1:], lambda step: (step, 0, 0, 0)),
+                            pl.BlockSpec((4, NY, 256), lambda step: (step, 0, 0)),
+                            pl.BlockSpec((4, NY, 256), lambda step: (12 + step, 0, 0))],
+        out_specs=(pl.BlockSpec(memory_space=pl.ANY),) + tuple(vmem(2)),
+        scratch_shapes=[pltpu.VMEM((count, VIEWS, NY, 128), BF16), pltpu.VMEM((512, 512), BF16),
+                        pltpu.SemaphoreType.DMA((count,))],
         name="pack",
-    )(targets, pieces)
+    )(index, targets, pieces, estimate, estimate)
 
 
 def window_kernel(index_ref, estimate_ref, main_ref):
@@ -225,45 +257,6 @@
         out_specs=vmem(1)[0],
         name="window",
     )(index, estimate)
-
-
-def ends_kernel(index_ref, first_ref, last_ref, low_ref, high_ref):
-    part = index_ref[0]
-    amount = (16 - PART * part + 256) % 256
-    lane = lax.broadcasted_iota(I32, (32, 128), 1)
-    column = part * PART - HALO + lane % 64
-    inside = (column >= 0) & (column < 256)
-
-    def four_planes(step, carry):
-        for source_ref, target_ref in ((first_ref, low_ref), (last_ref, high_ref)):
-            planes = []
-            for k in range(4):
-                plane = source_ref[step * 4 + k]
-                top = pltpu.roll(plane[:32], amount, 1)[:, :128]
-                bottom = pltpu.roll(plane[32:], (amount + 64) % 256, 1)[:, :128]
-                planes.append(jnp.where(inside, jnp.where(lane < 64, top, bottom), 0.0))
-            for m in range(4):
-                rows = slice(m * 8, m * 8 + 8)
-                front = swap_fours(planes[0][rows], planes[1][rows])
-                back = swap_fours(planes[2][rows], planes[3][rows])
-                for odd in range(2):
-                    target_ref[m * 2 + odd, pl.ds(pl.multiple_of(step * 16, 16), 16), :] = jnp.concatenate(
-                        [front[odd], back[odd]], axis=0).astype(BF16)
-        return carry
-
-    lax.fori_loop(0, 4, four_planes, 0)
-
-
-def window_ends(index, estimate):
-    return pl.pallas_call(
-        ends_kernel,
-        grid=(1,),
-        out_shape=(jax.ShapeDtypeStruct((8, 64, 128), BF16),) * 2,
-        in_specs=smem(1) + [pl.BlockSpec((16, NY, 256), lambda step: (0, 0, 0)),
-                            pl.BlockSpec((16, NY, 256), lambda step: (3, 0, 0))],
-        out_specs=tuple(vmem(2)),
-        name="ends",
-    )(index, estimate, estimate)
 
 
 def build_tail(edge_ref, from_low_ref, from_high_ref, tail_ref):
@@ -807,10 +800,8 @@
     slots = slot_index.reshape(VIEWS, block_count, SLOTS)
 
     index = my_view.reshape(1).astype(I32)
-    low, high = window_ends(index, estimate0)
     own_targets = lax.dynamic_slice(targets, (my_view, my_block, 0), (1, 1, SLOTS)).reshape(SLOTS)
-    outgoing = pack_pieces(own_targets, pieces[0], block_count)
-    low, high, outgoing = lax.optimization_barrier((low, high, outgoing))
+    outgoing, low, high = pack_pieces(index, own_targets, pieces[0], estimate0, block_count)
     from_low, from_high = to_neighbours(high, low, "block")
     incoming = lax.all_to_all(outgoing.reshape(VIEWS * block_count, CAP, NY, 128), ("view", "block"), 0, 0, tiled=True)
     incoming = incoming.reshape(VIEWS * block_count * CAP, NY, 128)

time: 177 us -> 174 us (0.983)
  Pallas kernels: 73 us -> 70.2 us
    pallas_call x2 -> x1, Pallas kernels: 8.46 us -> 5.63 us  [pack_pieces(): pl.pallas_call(pack_kernel, grid=(4,), out_shape=(jax.ShapeDtypeStruct((V...]
  transfers between devices with their start and end apart: 18 -> 18, of which waited for: 10 -> 10; matrix products, arithmetic and copies ran while one was open for 9% -> 9% of each run, Pallas kernels for 15% -> 16%
where the time goes in v5:
time: 174 us; the launch traced here: 172 us
  Pallas kernels  70.2 us (40%)
  waiting for transfers between devices  45.6 us (26%)
  starting transfers between devices  39.1 us (22%)
  local copies, waits for them, and re-layouts  8.81 us (5%)
  other arithmetic  8.27 us (5%)
    ppermute x5, waiting for transfers between devices, to_neighbours(): lax.ppermute(upward, axis, [(i, (i + 1) % count) for i in range(count)])  33.8 us
    ppermute x5, starting transfers between devices, to_neighbours(): lax.ppermute(downward, axis, [((i + 1) % count, i) for i in range(count)])  21 us
    pallas_call x1, Pallas kernels, second(): pl.pallas_call(second_kernel, grid=(VIEWS // 2,), out_shape=(held((QUADS,...  16.5 us
    all_to_all x1, starting transfers between devices, program(): lax.all_to_all(outgoing.reshape(VIEWS * block_count, CAP, NY, 128), ('vie...  11.7 us
    pallas_call x1, Pallas kernels, first_adjoint(): pl.pallas_call(first_adjoint_kernel, grid=(VIEWS // 2,), out_shape=PARTIA...  11.2 us
    pallas_call x1, Pallas kernels, forward(): pl.pallas_call(forward_kernel, out_shape=(jax.ShapeDtypeStruct((VIEWS, RO...  10.3 us
    ppermute x3, waiting for transfers between devices, gather_parts(): lax.ppermute(own, 'view', [((i + 2 * step) % VIEWS, i) for i in range(VIE...  10.2 us
    pallas_call x1, Pallas kernels, build_bands(): pl.pallas_call(band_kernel, out_shape=(jax.ShapeDtypeStruct((VIEWS, ROWS,...  6.78 us
  transfers between devices with their start and end apart: 18, of which 10 were waited for; matrix products, arithmetic and copies ran while one was open for 9% of the time, Pallas kernels for 16%

profile of v5, /device:TPU:0, one launch (start us, length us, event | category | flops | bytes accessed | tf_op | source)
XLA Modules:
  0.0 172.3 jit_solution(4363289106370450253)
XLA Ops:
  0.0 0.7 reduce
  0.8 0.6 dynamic-slice_bitcast_fusion.target_ref
  1.4 5.6 %pack.1 = (bf16[8,32,64,128]{3,2,1,0:T(8,128)(2,1)}, bf16[8,64,128]{2,1,0:T(8,128)(2,1)}, bf16[8,64,128]{2,1,0:T(8,128)(2,1)}) custom-call(s32[1]{0:T(128)} %bitcast.index_ref, s32[16]{0:T(128)} %dynamic-slice_bitcast_fusion.target_ref, bf16[16,4,64,256]{3,2,1,0:T(8,128)(2,1)} %bitcast.39, f32[64,64,256]{2,1,0:T(8,128)} %estimate_ref.1, ...), custom_call_target="tpu_custom_call" | custom-call | tf_op jit(solution)/shard_map/pack/pallas_call | solution.py:208
  7.1 11.7 %all-to-all-start = ((bf16[128,2,64,128]{3,2,1,0:T(8,128)(2,1)}), bf16[128,2,64,128]{3,2,1,0:T(8,128)(2,1)}, u32[]{:S(2)}, u32[]{:S(2)}) async-start(bf16[128,2,64,128]{3,2,1,0:T(8,128)(2,1)} %bitcast.36), calls=%async_computation | async-start | bytes 8388608 | tf_op jit(solution)/shard_map/all_to_all | solution.py:806
  18.8 1.0 collective-permute-start
  19.8 4.5 %collective-permute-start.1 = (bf16[8,64,128]{2,1,0:T(8,128)(2,1)S(1)}, bf16[8,64,128]{2,1,0:T(8,128)(2,1)S(1)}, u32[]{:S(2)}, u32[]{:S(2)}) collective-permute-start(bf16[8,64,128]{2,1,0:T(8,128)(2,1)S(1)} %copy-done.10), channel_id=1, source_target_pairs={{1,0},{2,1},{3,2},{4,3},{5,4},{6,5},{7,6},{8,7},{9,8},{10,9},{11,1... | collective-permute-start | bytes 393224 | tf_op jit(solution)/shard_map/ppermute | solution.py:774
  24.4 2.5 %convert_reduce_fusion = s32[8,16,16]{2,1,0:T(8,128)S(1)} fusion(s32[8,16,16]{2,1,0:T(8,128)S(1)} %reshape_squeeze.3, pred[16,16]{1,0:T(8,128)(4,1)S(1)} %iota_compare_fusion.6), kind=kLoop, calls=%fused_computation.2 | loop fusion | flops 129024 | bytes 16640 | tf_op jit(solution)/shard_map/reduce_sum | solution.py:816
  27.0 0.4 select_reduce_fusion.2
  27.5 0.1 copy.32
  27.7 0.4 fusion
  28.5 0.1 select_reduce_fusion.3
  28.8 0.1 sub.102
  29.0 0.1 copy.37
  29.1 0.1 broadcast_in_dim.292
  29.3 0.2 slice_reduce_fusion.19
  29.5 0.5 slice_reduce_fusion.20
  30.1 0.8 multiply_reduce_fusion
  31.0 0.1 copy.39
  31.1 0.7 convert_reduce_fusion.3.start_ref
  31.8 0.2 convert_reduce_fusion.2
  32.0 0.1 convert_reduce_fusion.1
  32.2 0.1 select_reduce_fusion.4
  32.3 0.2 broadcast_multiply_fusion
  32.5 0.2 fusion.32
  32.7 0.3 maximum_bitcast_fusion
  33.0 0.7 add_convert_fusion.edge_ref
  33.8 0.1 slice.145
  33.9 6.0 %window.1.main_ref.estimate_main_ref = f32[2,1024,128]{2,1,0:T(8,128)} custom-call(s32[1]{0:T(128)} %bitcast.index_ref, f32[64,64,256]{2,1,0:T(8,128)} %estimate_ref.1), custom_call_target="tpu_custom_call" | custom-call | tf_op jit(solution)/shard_map/window/pallas_call | solution.py:253
  39.9 0.6 reshape.278.shift_ref
  40.5 0.7 reshape.277.taps_ref
  41.2 0.7 reshape.270.rows_ref
  41.9 0.6 div.30.inverse_ref
  42.5 0.3 reshape.280
  42.8 0.2 reshape.275
  43.1 6.8 %bands.1 = (bf16[8,256,256]{2,1,0:T(8,128)(2,1)}, bf16[8,256,256]{2,1,0:T(8,128)(2,1)}, bf16[8,256,128]{2,1,0:T(8,128)(2,1)}, bf16[8,128,256]{2,1,0:T(8,128)(2,1...) custom-call(f32[504]{0:T(512)} %reshape.277.taps_ref, s32[24]{0:T(128)} %reshape.278.shift_ref), custom_call_target="tpu_custom_call" | custom-call | tf_op jit(solution)/shard_map/bands/pallas_call | solution.py:136
  49.8 0.7 broadcast_in_dim.296
  50.6 0.9 broadcast_in_dim.295
  51.5 3.8 %weights.1 = (f32[2,1024,128]{2,1,0:T(8,128)}, f32[16,64,128]{2,1,0:T(8,128)}) custom-call(f32[512]{0:T(512)} %reshape.270.rows_ref, f32[8,2,64,128]{3,2,1,0:T(8,128)} %bitcast.37, f32[8,64,128]{2,1,0:T(8,128)} %bitcast.40), custom_call_target="tpu_custom_call" | custom-call | tf_op jit(solution)/shard_map/weights/pallas_call | solution.py:300
  55.3 0.7 select_reduce_fusion
  56.0 15.8 %collective-permute-done.from_low_ref = bf16[8,64,128]{2,1,0:T(8,128)(2,1)S(1)} collective-permute-done((bf16[8,64,128]{2,1,0:T(8,128)(2,1)S(1)}, bf16[8,64,128]{2,1,0:T(8,128)(2,1)S(1)}, u32[]{:S(2)}, u32[]{:S(2)}) %collective-permute-start) | collective-permute-done | bytes 131104 | tf_op jit(solution)/shard_map/ppermute | solution.py:773
  71.8 0.6 copy-done.4
  72.5 10.3 %forward.1 = (bf16[8,256,512]{2,1,0:T(8,128)(2,1)}, f32[16,64,128]{2,1,0:T(8,128)}) custom-call(f32[4]{0:T(128)} %add_convert_fusion.edge_ref, f32[2,1024,128]{2,1,0:T(8,128)} %window.1.main_ref.estimate_main_ref, bf16[8,64,128]{2,1,0:T(8,128)(2,1)} %copy-done.4, bf16[8,64,128]{2,1,0:T(8,128)(2,1)} %copy-done.5, bf16[512,192]{1,0:T(8,128)(2,1)} %get-tuple-element.44.bzf_ref, ...), custom_call_target="tpu_custom_call" | custom-call | tf_op jit(solution)/shard_map/forward/pallas_call | solution.py:424
  82.9 11.2 %first_adjoint.1 = (f32[2,1024,128]{2,1,0:T(8,128)S(1)}, f32[16,64,128]{2,1,0:T(8,128)S(1)}, s16[24,64,128]{2,1,0:T(8,128)(2,1)S(1)}, s16[24,64,128]{2,1,0:T(8,128)(2,1)S(1)}, bf16[8,256,512]{2,1,0:T(8,128)(2,1)}) custom-call(s32[9]{0:T(128)} %convert_reduce_fusion.3.start_ref, s32[256]{0:T(256)} %get-tuple-element.93.source_ref, ...), custom_call_target="tpu_custom_call" | custom-call | tf_op jit(solution)/shard_map/first_adjoint/pallas_call | solution.py:498
  94.1 3.0 %collective-permute-start.3 = (s16[24,64,128]{2,1,0:T(8,128)(2,1)S(1)}, s16[24,64,128]{2,1,0:T(8,128)(2,1)S(1)}, u32[]{:S(2)}, u32[]{:S(2)}) collective-permute-start(s16[24,64,128]{2,1,0:T(8,128)(2,1)S(1)} %get-tuple-element.54), channel_id=1, source_target_pairs={{16,0},{32,16},{48,32},{64,48},{80,64},{96,80},{112,96},{0,112},{1... | collective-permute-start | bytes 1179656 | tf_op jit(solution)/shard_map/ppermute | solution.py:774
  97.1 5.5 %collective-permute-done.2.from_left_ref = s16[24,64,128]{2,1,0:T(8,128)(2,1)S(1)} collective-permute-done((s16[24,64,128]{2,1,0:T(8,128)(2,1)S(1)}, s16[24,64,128]{2,1,0:T(8,128)(2,1)S(1)}, u32[]{:S(2)}, u32[]{:S(2)}) %collective-permute-start.2) | collective-permute-done | bytes 393248 | tf_op jit(solution)/shard_map/ppermute | solution.py:773
  102.5 1.7 join_columns.1
  104.3 5.3 %collective-permute-start.5 = (s16[16,64,128]{2,1,0:T(8,128)(2,1)S(1)}, s16[16,64,128]{2,1,0:T(8,128)(2,1)S(1)}, u32[]{:S(2)}, u32[]{:S(2)}) collective-permute-start(s16[16,64,128]{2,1,0:T(8,128)(2,1)S(1)} %get-tuple-element.58), channel_id=1, source_target_pairs={{1,0},{2,1},{3,2},{4,3},{5,4},{6,5},{7,6},{8,7},{9,8},{10,9},{11,1... | collective-permute-start | bytes 786440 | tf_op jit(solution)/shard_map/ppermute | solution.py:774
  109.6 6.3 %collective-permute-done.4.from_low_ref = s16[16,64,128]{2,1,0:T(8,128)(2,1)S(1)} collective-permute-done((s16[16,64,128]{2,1,0:T(8,128)(2,1)S(1)}, s16[16,64,128]{2,1,0:T(8,128)(2,1)S(1)}, u32[]{:S(2)}, u32[]{:S(2)}) %collective-permute-start.4) | collective-permute-done | bytes 262176 | tf_op jit(solution)/shard_map/ppermute | solution.py:773
  115.9 16.5 %second.1 = (f32[16,64,128]{2,1,0:T(8,128)S(1)}, f32[16,64,128]{2,1,0:T(8,128)S(1)}, f32[16,64,128]{2,1,0:T(8,128)S(1)}, s16[16,64,128]{2,1,0:T(8,128)(2,1)S(1)}, s16[16,64,128]{2,1,0:T(8,128)(2,1)S(1)}) custom-call(f32[8]{0:T(128)} %offset_ref.9, f32[4]{0:T(128)} %add_convert_fusion.edge_ref, f32[2,1024,128]{2,1,0:T(8,128)S(1)} %get-tuple-element.55.part_main_ref, ...), custom_call_target="tpu_custom_call" | custom-call | tf_op jit(solution)/shard_map/second/pallas_call | solution.py:617
  132.5 2.9 %collective-permute-start.7 = (s16[16,64,128]{2,1,0:T(8,128)(2,1)S(1)}, s16[16,64,128]{2,1,0:T(8,128)(2,1)S(1)}, u32[]{:S(2)}, u32[]{:S(2)}) collective-permute-start(s16[16,64,128]{2,1,0:T(8,128)(2,1)S(1)} %get-tuple-element.66), channel_id=1, source_target_pairs={{16,0},{32,16},{48,32},{64,48},{80,64},{96,80},{112,96},{0,112},{1... | collective-permute-start | bytes 786440 | tf_op jit(solution)/shard_map/ppermute | solution.py:774
  135.4 4.1 %collective-permute-done.6.from_left_ref = s16[16,64,128]{2,1,0:T(8,128)(2,1)S(1)} collective-permute-done((s16[16,64,128]{2,1,0:T(8,128)(2,1)S(1)}, s16[16,64,128]{2,1,0:T(8,128)(2,1)S(1)}, u32[]{:S(2)}, u32[]{:S(2)}) %collective-permute-start.6) | collective-permute-done | bytes 262176 | tf_op jit(solution)/shard_map/ppermute | solution.py:773
  139.5 1.3 join_own.1
  140.9 5.3 %collective-permute-start.9 = (s16[4,64,128]{2,1,0:T(8,128)(2,1)S(1)}, s16[4,64,128]{2,1,0:T(8,128)(2,1)S(1)}, u32[]{:S(2)}, u32[]{:S(2)}) collective-permute-start(s16[4,64,128]{2,1,0:T(8,128)(2,1)S(1)} %get-tuple-element.69), channel_id=1, source_target_pairs={{1,0},{2,1},{3,2},{4,3},{5,4},{6,5},{7,6},{8,7},{9,8},{10,9},{11,1... | collective-permute-start | bytes 196616 | tf_op jit(solution)/shard_map/ppermute | solution.py:774
  146.2 2.2 %collective-permute-done.8.from_low_ref = s16[4,64,128]{2,1,0:T(8,128)(2,1)S(1)} collective-permute-done((s16[4,64,128]{2,1,0:T(8,128)(2,1)S(1)}, s16[4,64,128]{2,1,0:T(8,128)(2,1)S(1)}, u32[]{:S(2)}, u32[]{:S(2)}) %collective-permute-start.8) | collective-permute-done | bytes 65568 | tf_op jit(solution)/shard_map/ppermute | solution.py:773
  148.5 1.3 finish.1.refs_0_
  149.9 1.6 collective-permute-start.11
  151.5 2.5 %collective-permute-start.10 = (s16[1056,128]{1,0:T(8,128)(2,1)S(1)}, s16[1056,128]{1,0:T(8,128)(2,1)S(1)}, u32[]{:S(2)}, u32[]{:S(2)}) collective-permute-start(s16[1056,128]{1,0:T(8,128)(2,1)S(1)} %finish.1.refs_0_), channel_id=1, source_target_pairs={{32,0},{48,16},{64,32},{80,48},{96,64},{112,80},{0,96},{16,112},{3... | collective-permute-start | bytes 811016 | tf_op jit(solution)/shard_map/ppermute | solution.py:780
  154.1 5.8 %collective-permute-done.12.refs_3_ = s16[1056,128]{1,0:T(8,128)(2,1)S(1)} collective-permute-done((s16[1056,128]{1,0:T(8,128)(2,1)S(1)}, s16[1056,128]{1,0:T(8,128)(2,1)S(1)}, u32[]{:S(2)}, u32[]{:S(2)}) %collective-permute-start.12) | collective-permute-done | bytes 270368 | tf_op jit(solution)/shard_map/ppermute | solution.py:780
  159.8 3.6 %collective-permute-done.11.refs_2_ = s16[1056,128]{1,0:T(8,128)(2,1)S(1)} collective-permute-done((s16[1056,128]{1,0:T(8,128)(2,1)S(1)}, s16[1056,128]{1,0:T(8,128)(2,1)S(1)}, u32[]{:S(2)}, u32[]{:S(2)}) %collective-permute-start.11) | collective-permute-done | bytes 270368 | tf_op jit(solution)/shard_map/ppermute | solution.py:780
  163.4 1.0 collective-permute-start.15
  164.4 0.8 collective-permute-done.10.refs_1_
  165.2 0.3 collective-permute-done.15.refs_6_
  165.6 1.2 collective-permute-done.14.refs_5_
  166.8 5.5 %assemble.1 = f32[4,4,4,64,256]{4,3,2,1,0:T(8,128)} custom-call(s32[1]{0:T(128)} %bitcast.index_ref, s16[1056,128]{1,0:T(8,128)(2,1)S(1)} %finish.1.refs_0_, s16[1056,128]{1,0:T(8,128)(2,1)S(1)} %collective-permute-done.10.refs_1_, s16[1056,128]{1,0:T(8,128)(2,1)S(1)} %collective-permute-done.11.refs_2_, ...), custom_call_target="tpu_custom_call" | custom-call | tf_op jit(solution)/shard_map/assemble/pallas_call | solution.py:759
  (74 shorter events, 1.8 us)
Async XLA Ops:
  7.0 11.8 %copy-start.11 = (bf16[8,64,128]{2,1,0:T(8,128)(2,1)S(1)}, bf16[8,64,128]{2,1,0:T(8,128)(2,1)}, u32[]{:S(2)}) copy-start(bf16[8,64,128]{2,1,0:T(8,128)(2,1)} %get-tuple-element.42) | copy-start | bytes 393220
  7.1 12.7 %copy-start.10 = (bf16[8,64,128]{2,1,0:T(8,128)(2,1)S(1)}, bf16[8,64,128]{2,1,0:T(8,128)(2,1)}, u32[]{:S(2)}) copy-start(bf16[8,64,128]{2,1,0:T(8,128)(2,1)} %get-tuple-element.43) | copy-start | bytes 393220
  7.1 17.2 %copy-start.7 = (s32[8,256,1]{1,2,0:T(1,128)S(1)}, s32[8,256,1]{1,2,0:T(1,128)}, u32[]{:S(2)}) copy-start(s32[8,256,1]{1,2,0:T(1,128)} %param.9) | copy-start | bytes 24580
  7.1 17.2 %copy-start.8 = (s32[8,256]{1,0:T(8,128)S(1)}, s32[8,256]{1,0:T(8,128)}, u32[]{:S(2)}) copy-start(s32[8,256]{1,0:T(8,128)} %param.10) | copy-start | bytes 24580
  7.1 21.0 %copy-start.6 = (f32[8,3,21]{2,0,1:T(8,128)S(1)}, f32[8,3,21]{2,0,1:T(8,128)}, u32[]{:S(2)}) copy-start(f32[8,3,21]{2,0,1:T(8,128)} %param.12) | copy-start | bytes 6052
  7.1 21.3 %copy-start.9 = (s32[8,3]{0,1:T(4,128)S(1)}, s32[8,3]{0,1:T(4,128)}, u32[]{:S(2)}) copy-start(s32[8,3]{0,1:T(4,128)} %param.11) | copy-start | bytes 292
  7.1 75.8 %all-to-all-start = ((bf16[128,2,64,128]{3,2,1,0:T(8,128)(2,1)}), bf16[128,2,64,128]{3,2,1,0:T(8,128)(2,1)}, u32[]{:S(2)}, u32[]{:S(2)}) async-start(bf16[128,2,64,128]{3,2,1,0:T(8,128)(2,1)} %bitcast.36), calls=%async_computation | async-start | bytes 8388608 | tf_op jit(solution)/shard_map/all_to_all | solution.py:806
  18.8 53.0 %collective-permute-start = (bf16[8,64,128]{2,1,0:T(8,128)(2,1)S(1)}, bf16[8,64,128]{2,1,0:T(8,128)(2,1)S(1)}, u32[]{:S(2)}, u32[]{:S(2)}) collective-permute-start(bf16[8,64,128]{2,1,0:T(8,128)(2,1)S(1)} %copy-done.11), channel_id=1, source_target_pairs={{0,1},{1,2},{2,3},{3,4},{4,5},{5,6},{6,7},{7,8},{8,9},{9,10},{10,1... | collective-permute-start | bytes 393224 | tf_op jit(solution)/shard_map/ppermute | solution.py:773
  19.8 52.0 %collective-permute-start.1 = (bf16[8,64,128]{2,1,0:T(8,128)(2,1)S(1)}, bf16[8,64,128]{2,1,0:T(8,128)(2,1)S(1)}, u32[]{:S(2)}, u32[]{:S(2)}) collective-permute-start(bf16[8,64,128]{2,1,0:T(8,128)(2,1)S(1)} %copy-done.10), channel_id=1, source_target_pairs={{1,0},{2,1},{3,2},{4,3},{5,4},{6,5},{7,6},{8,7},{9,8},{10,9},{11,1... | collective-permute-start | bytes 393224 | tf_op jit(solution)/shard_map/ppermute | solution.py:774
  71.8 0.7 copy-start.4
  71.8 0.7 copy-start.5
  82.9 19.6 %copy-start = (f32[4]{0:T(128)S(1)}, f32[4]{0:T(128)}, u32[]{:S(2)}) copy-start(f32[4]{0:T(128)} %add_convert_fusion.edge_ref) | copy-start | bytes 52
  82.9 19.6 %copy-start.2 = (f32[8]{0:T(128)S(1)}, f32[8]{0:T(128)}, u32[]{:S(2)}) copy-start(f32[8]{0:T(128)} %offset_ref.9) | copy-start | bytes 100
  94.1 8.4 %collective-permute-start.2 = (s16[24,64,128]{2,1,0:T(8,128)(2,1)S(1)}, s16[24,64,128]{2,1,0:T(8,128)(2,1)S(1)}, u32[]{:S(2)}, u32[]{:S(2)}) collective-permute-start(s16[24,64,128]{2,1,0:T(8,128)(2,1)S(1)} %get-tuple-element.53), channel_id=1, source_target_pairs={{0,16},{16,32},{32,48},{48,64},{64,80},{80,96},{96,112},{112,0},{1... | collective-permute-start | bytes 1179656 | tf_op jit(solution)/shard_map/ppermute | solution.py:773
  94.1 8.4 %collective-permute-start.3 = (s16[24,64,128]{2,1,0:T(8,128)(2,1)S(1)}, s16[24,64,128]{2,1,0:T(8,128)(2,1)S(1)}, u32[]{:S(2)}, u32[]{:S(2)}) collective-permute-start(s16[24,64,128]{2,1,0:T(8,128)(2,1)S(1)} %get-tuple-element.54), channel_id=1, source_target_pairs={{16,0},{32,16},{48,32},{64,48},{80,64},{96,80},{112,96},{0,112},{1... | collective-permute-start | bytes 1179656 | tf_op jit(solution)/shard_map/ppermute | solution.py:774
  104.2 11.7 %collective-permute-start.4 = (s16[16,64,128]{2,1,0:T(8,128)(2,1)S(1)}, s16[16,64,128]{2,1,0:T(8,128)(2,1)S(1)}, u32[]{:S(2)}, u32[]{:S(2)}) collective-permute-start(s16[16,64,128]{2,1,0:T(8,128)(2,1)S(1)} %get-tuple-element.57), channel_id=1, source_target_pairs={{0,1},{1,2},{2,3},{3,4},{4,5},{5,6},{6,7},{7,8},{8,9},{9,10},{10,1... | collective-permute-start | bytes 786440 | tf_op jit(solution)/shard_map/ppermute | solution.py:773
  104.3 11.6 %collective-permute-start.5 = (s16[16,64,128]{2,1,0:T(8,128)(2,1)S(1)}, s16[16,64,128]{2,1,0:T(8,128)(2,1)S(1)}, u32[]{:S(2)}, u32[]{:S(2)}) collective-permute-start(s16[16,64,128]{2,1,0:T(8,128)(2,1)S(1)} %get-tuple-element.58), channel_id=1, source_target_pairs={{1,0},{2,1},{3,2},{4,3},{5,4},{6,5},{7,6},{8,7},{9,8},{10,9},{11,1... | collective-permute-start | bytes 786440 | tf_op jit(solution)/shard_map/ppermute | solution.py:774
  115.9 23.6 %copy-start.1 = (f32[4]{0:T(128)S(1)}, f32[4]{0:T(128)}, u32[]{:S(2)}) copy-start(f32[4]{0:T(128)} %add_convert_fusion.edge_ref) | copy-start | bytes 52
  115.9 23.6 %copy-start.3 = (f32[8]{0:T(128)S(1)}, f32[8]{0:T(128)}, u32[]{:S(2)}) copy-start(f32[8]{0:T(128)} %offset_ref.9) | copy-start | bytes 100
  132.5 7.0 %collective-permute-start.6 = (s16[16,64,128]{2,1,0:T(8,128)(2,1)S(1)}, s16[16,64,128]{2,1,0:T(8,128)(2,1)S(1)}, u32[]{:S(2)}, u32[]{:S(2)}) collective-permute-start(s16[16,64,128]{2,1,0:T(8,128)(2,1)S(1)} %get-tuple-element.65), channel_id=1, source_target_pairs={{0,16},{16,32},{32,48},{48,64},{64,80},{80,96},{96,112},{112,0},{1... | collective-permute-start | bytes 786440 | tf_op jit(solution)/shard_map/ppermute | solution.py:773
  132.5 7.0 %collective-permute-start.7 = (s16[16,64,128]{2,1,0:T(8,128)(2,1)S(1)}, s16[16,64,128]{2,1,0:T(8,128)(2,1)S(1)}, u32[]{:S(2)}, u32[]{:S(2)}) collective-permute-start(s16[16,64,128]{2,1,0:T(8,128)(2,1)S(1)} %get-tuple-element.66), channel_id=1, source_target_pairs={{16,0},{32,16},{48,32},{64,48},{80,64},{96,80},{112,96},{0,112},{1... | collective-permute-start | bytes 786440 | tf_op jit(solution)/shard_map/ppermute | solution.py:774
  140.8 7.7 %collective-permute-start.8 = (s16[4,64,128]{2,1,0:T(8,128)(2,1)S(1)}, s16[4,64,128]{2,1,0:T(8,128)(2,1)S(1)}, u32[]{:S(2)}, u32[]{:S(2)}) collective-permute-start(s16[4,64,128]{2,1,0:T(8,128)(2,1)S(1)} %get-tuple-element.68), channel_id=1, source_target_pairs={{0,1},{1,2},{2,3},{3,4},{4,5},{5,6},{6,7},{7,8},{8,9},{9,10},{10,1... | collective-permute-start | bytes 196616 | tf_op jit(solution)/shard_map/ppermute | solution.py:773
  140.9 7.6 %collective-permute-start.9 = (s16[4,64,128]{2,1,0:T(8,128)(2,1)S(1)}, s16[4,64,128]{2,1,0:T(8,128)(2,1)S(1)}, u32[]{:S(2)}, u32[]{:S(2)}) collective-permute-start(s16[4,64,128]{2,1,0:T(8,128)(2,1)S(1)} %get-tuple-element.69), channel_id=1, source_target_pairs={{1,0},{2,1},{3,2},{4,3},{5,4},{6,5},{7,6},{8,7},{9,8},{10,9},{11,1... | collective-permute-start | bytes 196616 | tf_op jit(solution)/shard_map/ppermute | solution.py:774
  149.8 10.0 %collective-permute-start.12 = (s16[1056,128]{1,0:T(8,128)(2,1)S(1)}, s16[1056,128]{1,0:T(8,128)(2,1)S(1)}, u32[]{:S(2)}, u32[]{:S(2)}) collective-permute-start(s16[1056,128]{1,0:T(8,128)(2,1)S(1)} %finish.1.refs_0_), channel_id=1, source_target_pairs={{96,0},{112,16},{0,32},{16,48},{32,64},{48,80},{64,96},{80,112},{9... | collective-permute-start | bytes 811016 | tf_op jit(solution)/shard_map/ppermute | solution.py:780
  149.9 13.5 %collective-permute-start.11 = (s16[1056,128]{1,0:T(8,128)(2,1)S(1)}, s16[1056,128]{1,0:T(8,128)(2,1)S(1)}, u32[]{:S(2)}, u32[]{:S(2)}) collective-permute-start(s16[1056,128]{1,0:T(8,128)(2,1)S(1)} %finish.1.refs_0_), channel_id=1, source_target_pairs={{64,0},{80,16},{96,32},{112,48},{0,64},{16,80},{32,96},{48,112},{6... | collective-permute-start | bytes 811016 | tf_op jit(solution)/shard_map/ppermute | solution.py:780
  151.5 13.7 %collective-permute-start.10 = (s16[1056,128]{1,0:T(8,128)(2,1)S(1)}, s16[1056,128]{1,0:T(8,128)(2,1)S(1)}, u32[]{:S(2)}, u32[]{:S(2)}) collective-permute-start(s16[1056,128]{1,0:T(8,128)(2,1)S(1)} %finish.1.refs_0_), channel_id=1, source_target_pairs={{32,0},{48,16},{64,32},{80,48},{96,64},{112,80},{0,96},{16,112},{3... | collective-permute-start | bytes 811016 | tf_op jit(solution)/shard_map/ppermute | solution.py:780
  154.1 11.2 %collective-permute-start.13 = (s16[1056,128]{1,0:T(8,128)(2,1)S(1)}, s16[1056,128]{1,0:T(8,128)(2,1)S(1)}, u32[]{:S(2)}, u32[]{:S(2)}) collective-permute-start(s16[1056,128]{1,0:T(8,128)(2,1)S(1)} %finish.1.refs_0_), channel_id=1, source_target_pairs={{0,16},{16,0},{32,48},{48,32},{64,80},{80,64},{96,112},{112,96},{1... | collective-permute-start | bytes 811016 | tf_op jit(solution)/shard_map/ppermute | solution.py:783
  159.8 5.4 %collective-permute-start.16 = (s16[1056,128]{1,0:T(8,128)(2,1)S(1)}, s16[1056,128]{1,0:T(8,128)(2,1)S(1)}, u32[]{:S(2)}, u32[]{:S(2)}) collective-permute-start(s16[1056,128]{1,0:T(8,128)(2,1)S(1)} %collective-permute-done.12.refs_3_), channel_id=1, source_target_pairs={{0,16},{16,0},{32,48},{48,32},{64,80},{80,64},{96,112},{112,96},{1... | collective-permute-start | bytes 811016 | tf_op jit(solution)/shard_map/ppermute | solution.py:783
  163.4 2.1 %collective-permute-start.15 = (s16[1056,128]{1,0:T(8,128)(2,1)S(1)}, s16[1056,128]{1,0:T(8,128)(2,1)S(1)}, u32[]{:S(2)}, u32[]{:S(2)}) collective-permute-start(s16[1056,128]{1,0:T(8,128)(2,1)S(1)} %collective-permute-done.11.refs_2_), channel_id=1, source_target_pairs={{0,16},{16,0},{32,48},{48,32},{64,80},{80,64},{96,112},{112,96},{1... | collective-permute-start | bytes 811016 | tf_op jit(solution)/shard_map/ppermute | solution.py:783
  165.2 1.5 collective-permute-start.14

commit v6 on v5

--- a/solution.py
+++ b/solution.py
@@ -737,19 +737,23 @@
     step = pl.program_id(0)
 
     def sixteen_rows(n, carry):
-        for j in range(4):
-            rows = pl.ds(pl.multiple_of((step * 4 + j) * NY + n * 16, 16), 16)
+        lines = pl.ds(pl.multiple_of(n * 16, 16), 16)
+        for j in (0, 2):
+            first = pl.multiple_of((step * 4 + j) * NY + n * 16, 16)
             for half in range(2):
-                c0, c1, c2, c3 = (buffer_ref[half * 4 + k, rows, :].astype(I32).astype(F32) for k in range(4))
+                c0, c1, c2, c3 = (
+                    buffer_ref[half * 4 + k, pl.ds(first, 16), :].astype(I32)
+                    | (buffer_ref[half * 4 + k, pl.ds(first + NY, 16), :].astype(I32) << 16) for k in range(4))
                 a0 = jnp.where(block < 2, c0, rotate(c2, 64))
                 a1 = jnp.where(block < 2, c1, rotate(c3, 64))
                 a2 = jnp.where(block < 2, rotate(c0, 64), c2)
                 a3 = jnp.where(block < 2, rotate(c1, 64), c3)
                 results = (jnp.where(even, a0, rotate(a1, 32)), jnp.where(even, rotate(a0, 96), a1),
                            jnp.where(even, a2, rotate(a3, 32)), jnp.where(even, rotate(a2, 96), a3))
+                lanes = slice(half * 128, (half + 1) * 128)
                 for h in range(4):
-                    out_ref[h, 0, j, pl.ds(pl.multiple_of(n * 16, 16), 16), half * 128:(half + 1) * 128] = (
-                        results[h] * units[half])
+                    out_ref[h, 0, j, lines, lanes] = (results[h] & 65535).astype(F32) * units[half]
+                    out_ref[h, 0, j + 1, lines, lanes] = (results[h] >> 16).astype(F32) * units[half]
         return carry
 
     lax.fori_loop(0, 4, sixteen_rows, 0)

time: 174 us -> 173 us (level)
  no operation moved by 1% of the time
where the time goes in v6:
time: 173 us; the launch traced here: 171 us
  Pallas kernels  69 us (40%)
  waiting for transfers between devices  45.6 us (26%)
  starting transfers between devices  39.1 us (23%)
  local copies, waits for them, and re-layouts  8.81 us (5%)
  other arithmetic  8.27 us (5%)
    ppermute x5, waiting for transfers between devices, to_neighbours(): lax.ppermute(upward, axis, [(i, (i + 1) % count) for i in range(count)])  33.8 us
    ppermute x5, starting transfers between devices, to_neighbours(): lax.ppermute(downward, axis, [((i + 1) % count, i) for i in range(count)])  21 us
    pallas_call x1, Pallas kernels, second(): pl.pallas_call(second_kernel, grid=(VIEWS // 2,), out_shape=(held((QUADS,...  16.5 us
    all_to_all x1, starting transfers between devices, program(): lax.all_to_all(outgoing.reshape(VIEWS * block_count, CAP, NY, 128), ('vie...  11.7 us
    pallas_call x1, Pallas kernels, first_adjoint(): pl.pallas_call(first_adjoint_kernel, grid=(VIEWS // 2,), out_shape=PARTIA...  11.2 us
    pallas_call x1, Pallas kernels, forward(): pl.pallas_call(forward_kernel, out_shape=(jax.ShapeDtypeStruct((VIEWS, RO...  10.3 us
    ppermute x3, waiting for transfers between devices, gather_parts(): lax.ppermute(own, 'view', [((i + 2 * step) % VIEWS, i) for i in range(VIE...  10.2 us
    pallas_call x1, Pallas kernels, build_bands(): pl.pallas_call(band_kernel, out_shape=(jax.ShapeDtypeStruct((VIEWS, ROWS,...  6.78 us
  transfers between devices with their start and end apart: 18, of which 10 were waited for; matrix products, arithmetic and copies ran while one was open for 9% of the time, Pallas kernels for 16%

profile of v6, /device:TPU:0, one launch (start us, length us, event | category | flops | bytes accessed | tf_op | source)
XLA Modules:
  0.0 171.1 jit_solution(7499258823887147946)
XLA Ops:
  0.0 0.7 reduce
  0.8 0.6 dynamic-slice_bitcast_fusion.target_ref
  1.4 5.6 %pack.1 = (bf16[8,32,64,128]{3,2,1,0:T(8,128)(2,1)}, bf16[8,64,128]{2,1,0:T(8,128)(2,1)}, bf16[8,64,128]{2,1,0:T(8,128)(2,1)}) custom-call(s32[1]{0:T(128)} %bitcast.index_ref, s32[16]{0:T(128)} %dynamic-slice_bitcast_fusion.target_ref, bf16[16,4,64,256]{3,2,1,0:T(8,128)(2,1)} %bitcast.39, f32[64,64,256]{2,1,0:T(8,128)} %estimate_ref.1, ...), custom_call_target="tpu_custom_call" | custom-call | tf_op jit(solution)/shard_map/pack/pallas_call | solution.py:208
  7.1 11.7 %all-to-all-start = ((bf16[128,2,64,128]{3,2,1,0:T(8,128)(2,1)}), bf16[128,2,64,128]{3,2,1,0:T(8,128)(2,1)}, u32[]{:S(2)}, u32[]{:S(2)}) async-start(bf16[128,2,64,128]{3,2,1,0:T(8,128)(2,1)} %bitcast.36), calls=%async_computation | async-start | bytes 8388608 | tf_op jit(solution)/shard_map/all_to_all | solution.py:810
  18.8 1.0 collective-permute-start
  19.8 4.5 %collective-permute-start.1 = (bf16[8,64,128]{2,1,0:T(8,128)(2,1)S(1)}, bf16[8,64,128]{2,1,0:T(8,128)(2,1)S(1)}, u32[]{:S(2)}, u32[]{:S(2)}) collective-permute-start(bf16[8,64,128]{2,1,0:T(8,128)(2,1)S(1)} %copy-done.10), channel_id=1, source_target_pairs={{1,0},{2,1},{3,2},{4,3},{5,4},{6,5},{7,6},{8,7},{9,8},{10,9},{11,1... | collective-permute-start | bytes 393224 | tf_op jit(solution)/shard_map/ppermute | solution.py:778
  24.4 2.5 %convert_reduce_fusion = s32[8,16,16]{2,1,0:T(8,128)S(1)} fusion(s32[8,16,16]{2,1,0:T(8,128)S(1)} %reshape_squeeze.3, pred[16,16]{1,0:T(8,128)(4,1)S(1)} %iota_compare_fusion.6), kind=kLoop, calls=%fused_computation.2 | loop fusion | flops 129024 | bytes 16640 | tf_op jit(solution)/shard_map/reduce_sum | solution.py:820
  27.0 0.4 select_reduce_fusion.2
  27.5 0.1 copy.32
  27.7 0.4 fusion
  28.5 0.1 select_reduce_fusion.3
  28.8 0.1 sub.102
  29.0 0.1 copy.37
  29.1 0.1 broadcast_in_dim.292
  29.3 0.2 slice_reduce_fusion.19
  29.5 0.5 slice_reduce_fusion.20
  30.1 0.8 multiply_reduce_fusion
  31.0 0.1 copy.39
  31.1 0.7 convert_reduce_fusion.3.start_ref
  31.8 0.2 convert_reduce_fusion.2
  32.0 0.1 convert_reduce_fusion.1
  32.2 0.1 select_reduce_fusion.4
  32.3 0.2 broadcast_multiply_fusion
  32.5 0.2 fusion.32
  32.7 0.3 maximum_bitcast_fusion
  33.0 0.7 add_convert_fusion.edge_ref
  33.8 0.1 slice.145
  33.9 6.0 %window.1.main_ref.estimate_main_ref = f32[2,1024,128]{2,1,0:T(8,128)} custom-call(s32[1]{0:T(128)} %bitcast.index_ref, f32[64,64,256]{2,1,0:T(8,128)} %estimate_ref.1), custom_call_target="tpu_custom_call" | custom-call | tf_op jit(solution)/shard_map/window/pallas_call | solution.py:253
  39.9 0.6 reshape.278.shift_ref
  40.5 0.7 reshape.277.taps_ref
  41.2 0.7 reshape.270.rows_ref
  41.9 0.6 div.30.inverse_ref
  42.5 0.3 reshape.280
  42.8 0.2 reshape.275
  43.1 6.8 %bands.1 = (bf16[8,256,256]{2,1,0:T(8,128)(2,1)}, bf16[8,256,256]{2,1,0:T(8,128)(2,1)}, bf16[8,256,128]{2,1,0:T(8,128)(2,1)}, bf16[8,128,256]{2,1,0:T(8,128)(2,1...) custom-call(f32[504]{0:T(512)} %reshape.277.taps_ref, s32[24]{0:T(128)} %reshape.278.shift_ref), custom_call_target="tpu_custom_call" | custom-call | tf_op jit(solution)/shard_map/bands/pallas_call | solution.py:136
  49.8 0.7 broadcast_in_dim.296
  50.6 0.9 broadcast_in_dim.295
  51.5 3.8 %weights.1 = (f32[2,1024,128]{2,1,0:T(8,128)}, f32[16,64,128]{2,1,0:T(8,128)}) custom-call(f32[512]{0:T(512)} %reshape.270.rows_ref, f32[8,2,64,128]{3,2,1,0:T(8,128)} %bitcast.37, f32[8,64,128]{2,1,0:T(8,128)} %bitcast.40), custom_call_target="tpu_custom_call" | custom-call | tf_op jit(solution)/shard_map/weights/pallas_call | solution.py:300
  55.3 0.7 select_reduce_fusion
  56.0 15.8 %collective-permute-done.from_low_ref = bf16[8,64,128]{2,1,0:T(8,128)(2,1)S(1)} collective-permute-done((bf16[8,64,128]{2,1,0:T(8,128)(2,1)S(1)}, bf16[8,64,128]{2,1,0:T(8,128)(2,1)S(1)}, u32[]{:S(2)}, u32[]{:S(2)}) %collective-permute-start) | collective-permute-done | bytes 131104 | tf_op jit(solution)/shard_map/ppermute | solution.py:777
  71.8 0.6 copy-done.4
  72.5 10.3 %forward.1 = (bf16[8,256,512]{2,1,0:T(8,128)(2,1)}, f32[16,64,128]{2,1,0:T(8,128)}) custom-call(f32[4]{0:T(128)} %add_convert_fusion.edge_ref, f32[2,1024,128]{2,1,0:T(8,128)} %window.1.main_ref.estimate_main_ref, bf16[8,64,128]{2,1,0:T(8,128)(2,1)} %copy-done.4, bf16[8,64,128]{2,1,0:T(8,128)(2,1)} %copy-done.5, bf16[512,192]{1,0:T(8,128)(2,1)} %get-tuple-element.44.bzf_ref, ...), custom_call_target="tpu_custom_call" | custom-call | tf_op jit(solution)/shard_map/forward/pallas_call | solution.py:424
  82.9 11.2 %first_adjoint.1 = (f32[2,1024,128]{2,1,0:T(8,128)S(1)}, f32[16,64,128]{2,1,0:T(8,128)S(1)}, s16[24,64,128]{2,1,0:T(8,128)(2,1)S(1)}, s16[24,64,128]{2,1,0:T(8,128)(2,1)S(1)}, bf16[8,256,512]{2,1,0:T(8,128)(2,1)}) custom-call(s32[9]{0:T(128)} %convert_reduce_fusion.3.start_ref, s32[256]{0:T(256)} %get-tuple-element.93.source_ref, ...), custom_call_target="tpu_custom_call" | custom-call | tf_op jit(solution)/shard_map/first_adjoint/pallas_call | solution.py:498
  94.1 3.0 %collective-permute-start.3 = (s16[24,64,128]{2,1,0:T(8,128)(2,1)S(1)}, s16[24,64,128]{2,1,0:T(8,128)(2,1)S(1)}, u32[]{:S(2)}, u32[]{:S(2)}) collective-permute-start(s16[24,64,128]{2,1,0:T(8,128)(2,1)S(1)} %get-tuple-element.54), channel_id=1, source_target_pairs={{16,0},{32,16},{48,32},{64,48},{80,64},{96,80},{112,96},{0,112},{1... | collective-permute-start | bytes 1179656 | tf_op jit(solution)/shard_map/ppermute | solution.py:778
  97.1 5.5 %collective-permute-done.2.from_left_ref = s16[24,64,128]{2,1,0:T(8,128)(2,1)S(1)} collective-permute-done((s16[24,64,128]{2,1,0:T(8,128)(2,1)S(1)}, s16[24,64,128]{2,1,0:T(8,128)(2,1)S(1)}, u32[]{:S(2)}, u32[]{:S(2)}) %collective-permute-start.2) | collective-permute-done | bytes 393248 | tf_op jit(solution)/shard_map/ppermute | solution.py:777
  102.5 1.7 join_columns.1
  104.3 5.3 %collective-permute-start.5 = (s16[16,64,128]{2,1,0:T(8,128)(2,1)S(1)}, s16[16,64,128]{2,1,0:T(8,128)(2,1)S(1)}, u32[]{:S(2)}, u32[]{:S(2)}) collective-permute-start(s16[16,64,128]{2,1,0:T(8,128)(2,1)S(1)} %get-tuple-element.58), channel_id=1, source_target_pairs={{1,0},{2,1},{3,2},{4,3},{5,4},{6,5},{7,6},{8,7},{9,8},{10,9},{11,1... | collective-permute-start | bytes 786440 | tf_op jit(solution)/shard_map/ppermute | solution.py:778
  109.6 6.3 %collective-permute-done.4.from_low_ref = s16[16,64,128]{2,1,0:T(8,128)(2,1)S(1)} collective-permute-done((s16[16,64,128]{2,1,0:T(8,128)(2,1)S(1)}, s16[16,64,128]{2,1,0:T(8,128)(2,1)S(1)}, u32[]{:S(2)}, u32[]{:S(2)}) %collective-permute-start.4) | collective-permute-done | bytes 262176 | tf_op jit(solution)/shard_map/ppermute | solution.py:777
  115.9 16.5 %second.1 = (f32[16,64,128]{2,1,0:T(8,128)S(1)}, f32[16,64,128]{2,1,0:T(8,128)S(1)}, f32[16,64,128]{2,1,0:T(8,128)S(1)}, s16[16,64,128]{2,1,0:T(8,128)(2,1)S(1)}, s16[16,64,128]{2,1,0:T(8,128)(2,1)S(1)}) custom-call(f32[8]{0:T(128)} %offset_ref.9, f32[4]{0:T(128)} %add_convert_fusion.edge_ref, f32[2,1024,128]{2,1,0:T(8,128)S(1)} %get-tuple-element.55.part_main_ref, ...), custom_call_target="tpu_custom_call" | custom-call | tf_op jit(solution)/shard_map/second/pallas_call | solution.py:617
  132.5 2.9 %collective-permute-start.7 = (s16[16,64,128]{2,1,0:T(8,128)(2,1)S(1)}, s16[16,64,128]{2,1,0:T(8,128)(2,1)S(1)}, u32[]{:S(2)}, u32[]{:S(2)}) collective-permute-start(s16[16,64,128]{2,1,0:T(8,128)(2,1)S(1)} %get-tuple-element.66), channel_id=1, source_target_pairs={{16,0},{32,16},{48,32},{64,48},{80,64},{96,80},{112,96},{0,112},{1... | collective-permute-start | bytes 786440 | tf_op jit(solution)/shard_map/ppermute | solution.py:778
  135.4 4.1 %collective-permute-done.6.from_left_ref = s16[16,64,128]{2,1,0:T(8,128)(2,1)S(1)} collective-permute-done((s16[16,64,128]{2,1,0:T(8,128)(2,1)S(1)}, s16[16,64,128]{2,1,0:T(8,128)(2,1)S(1)}, u32[]{:S(2)}, u32[]{:S(2)}) %collective-permute-start.6) | collective-permute-done | bytes 262176 | tf_op jit(solution)/shard_map/ppermute | solution.py:777
  139.5 1.3 join_own.1
  140.9 5.3 %collective-permute-start.9 = (s16[4,64,128]{2,1,0:T(8,128)(2,1)S(1)}, s16[4,64,128]{2,1,0:T(8,128)(2,1)S(1)}, u32[]{:S(2)}, u32[]{:S(2)}) collective-permute-start(s16[4,64,128]{2,1,0:T(8,128)(2,1)S(1)} %get-tuple-element.69), channel_id=1, source_target_pairs={{1,0},{2,1},{3,2},{4,3},{5,4},{6,5},{7,6},{8,7},{9,8},{10,9},{11,1... | collective-permute-start | bytes 196616 | tf_op jit(solution)/shard_map/ppermute | solution.py:778
  146.2 2.2 %collective-permute-done.8.from_low_ref = s16[4,64,128]{2,1,0:T(8,128)(2,1)S(1)} collective-permute-done((s16[4,64,128]{2,1,0:T(8,128)(2,1)S(1)}, s16[4,64,128]{2,1,0:T(8,128)(2,1)S(1)}, u32[]{:S(2)}, u32[]{:S(2)}) %collective-permute-start.8) | collective-permute-done | bytes 65568 | tf_op jit(solution)/shard_map/ppermute | solution.py:777
  148.5 1.3 finish.1.refs_0_
  149.9 1.6 collective-permute-start.11
  151.5 2.5 %collective-permute-start.10 = (s16[1056,128]{1,0:T(8,128)(2,1)S(1)}, s16[1056,128]{1,0:T(8,128)(2,1)S(1)}, u32[]{:S(2)}, u32[]{:S(2)}) collective-permute-start(s16[1056,128]{1,0:T(8,128)(2,1)S(1)} %finish.1.refs_0_), channel_id=1, source_target_pairs={{32,0},{48,16},{64,32},{80,48},{96,64},{112,80},{0,96},{16,112},{3... | collective-permute-start | bytes 811016 | tf_op jit(solution)/shard_map/ppermute | solution.py:784
  154.1 5.8 %collective-permute-done.12.refs_3_ = s16[1056,128]{1,0:T(8,128)(2,1)S(1)} collective-permute-done((s16[1056,128]{1,0:T(8,128)(2,1)S(1)}, s16[1056,128]{1,0:T(8,128)(2,1)S(1)}, u32[]{:S(2)}, u32[]{:S(2)}) %collective-permute-start.12) | collective-permute-done | bytes 270368 | tf_op jit(solution)/shard_map/ppermute | solution.py:784
  159.8 3.6 %collective-permute-done.11.refs_2_ = s16[1056,128]{1,0:T(8,128)(2,1)S(1)} collective-permute-done((s16[1056,128]{1,0:T(8,128)(2,1)S(1)}, s16[1056,128]{1,0:T(8,128)(2,1)S(1)}, u32[]{:S(2)}, u32[]{:S(2)}) %collective-permute-start.11) | collective-permute-done | bytes 270368 | tf_op jit(solution)/shard_map/ppermute | solution.py:784
  163.4 1.0 collective-permute-start.15
  164.4 0.8 collective-permute-done.10.refs_1_
  165.2 0.3 collective-permute-done.15.refs_6_
  165.6 1.2 collective-permute-done.14.refs_5_
  166.8 4.3 %assemble.1 = f32[4,4,4,64,256]{4,3,2,1,0:T(8,128)} custom-call(s32[1]{0:T(128)} %bitcast.index_ref, s16[1056,128]{1,0:T(8,128)(2,1)S(1)} %finish.1.refs_0_, s16[1056,128]{1,0:T(8,128)(2,1)S(1)} %collective-permute-done.10.refs_1_, s16[1056,128]{1,0:T(8,128)(2,1)S(1)} %collective-permute-done.11.refs_2_, ...), custom_call_target="tpu_custom_call" | custom-call | tf_op jit(solution)/shard_map/assemble/pallas_call | solution.py:763
  (74 shorter events, 1.8 us)
Async XLA Ops:
  7.0 11.8 %copy-start.11 = (bf16[8,64,128]{2,1,0:T(8,128)(2,1)S(1)}, bf16[8,64,128]{2,1,0:T(8,128)(2,1)}, u32[]{:S(2)}) copy-start(bf16[8,64,128]{2,1,0:T(8,128)(2,1)} %get-tuple-element.42) | copy-start | bytes 393220
  7.1 12.7 %copy-start.10 = (bf16[8,64,128]{2,1,0:T(8,128)(2,1)S(1)}, bf16[8,64,128]{2,1,0:T(8,128)(2,1)}, u32[]{:S(2)}) copy-start(bf16[8,64,128]{2,1,0:T(8,128)(2,1)} %get-tuple-element.43) | copy-start | bytes 393220
  7.1 17.2 %copy-start.7 = (s32[8,256,1]{1,2,0:T(1,128)S(1)}, s32[8,256,1]{1,2,0:T(1,128)}, u32[]{:S(2)}) copy-start(s32[8,256,1]{1,2,0:T(1,128)} %param.9) | copy-start | bytes 24580
  7.1 17.2 %copy-start.8 = (s32[8,256]{1,0:T(8,128)S(1)}, s32[8,256]{1,0:T(8,128)}, u32[]{:S(2)}) copy-start(s32[8,256]{1,0:T(8,128)} %param.10) | copy-start | bytes 24580
  7.1 21.0 %copy-start.6 = (f32[8,3,21]{2,0,1:T(8,128)S(1)}, f32[8,3,21]{2,0,1:T(8,128)}, u32[]{:S(2)}) copy-start(f32[8,3,21]{2,0,1:T(8,128)} %param.12) | copy-start | bytes 6052
  7.1 21.3 %copy-start.9 = (s32[8,3]{0,1:T(4,128)S(1)}, s32[8,3]{0,1:T(4,128)}, u32[]{:S(2)}) copy-start(s32[8,3]{0,1:T(4,128)} %param.11) | copy-start | bytes 292
  7.1 75.8 %all-to-all-start = ((bf16[128,2,64,128]{3,2,1,0:T(8,128)(2,1)}), bf16[128,2,64,128]{3,2,1,0:T(8,128)(2,1)}, u32[]{:S(2)}, u32[]{:S(2)}) async-start(bf16[128,2,64,128]{3,2,1,0:T(8,128)(2,1)} %bitcast.36), calls=%async_computation | async-start | bytes 8388608 | tf_op jit(solution)/shard_map/all_to_all | solution.py:810
  18.8 53.0 %collective-permute-start = (bf16[8,64,128]{2,1,0:T(8,128)(2,1)S(1)}, bf16[8,64,128]{2,1,0:T(8,128)(2,1)S(1)}, u32[]{:S(2)}, u32[]{:S(2)}) collective-permute-start(bf16[8,64,128]{2,1,0:T(8,128)(2,1)S(1)} %copy-done.11), channel_id=1, source_target_pairs={{0,1},{1,2},{2,3},{3,4},{4,5},{5,6},{6,7},{7,8},{8,9},{9,10},{10,1... | collective-permute-start | bytes 393224 | tf_op jit(solution)/shard_map/ppermute | solution.py:777
  19.8 52.0 %collective-permute-start.1 = (bf16[8,64,128]{2,1,0:T(8,128)(2,1)S(1)}, bf16[8,64,128]{2,1,0:T(8,128)(2,1)S(1)}, u32[]{:S(2)}, u32[]{:S(2)}) collective-permute-start(bf16[8,64,128]{2,1,0:T(8,128)(2,1)S(1)} %copy-done.10), channel_id=1, source_target_pairs={{1,0},{2,1},{3,2},{4,3},{5,4},{6,5},{7,6},{8,7},{9,8},{10,9},{11,1... | collective-permute-start | bytes 393224 | tf_op jit(solution)/shard_map/ppermute | solution.py:778
  71.8 0.7 copy-start.4
  71.8 0.7 copy-start.5
  82.9 19.6 %copy-start = (f32[4]{0:T(128)S(1)}, f32[4]{0:T(128)}, u32[]{:S(2)}) copy-start(f32[4]{0:T(128)} %add_convert_fusion.edge_ref) | copy-start | bytes 52
  82.9 19.6 %copy-start.2 = (f32[8]{0:T(128)S(1)}, f32[8]{0:T(128)}, u32[]{:S(2)}) copy-start(f32[8]{0:T(128)} %offset_ref.9) | copy-start | bytes 100
  94.1 8.4 %collective-permute-start.2 = (s16[24,64,128]{2,1,0:T(8,128)(2,1)S(1)}, s16[24,64,128]{2,1,0:T(8,128)(2,1)S(1)}, u32[]{:S(2)}, u32[]{:S(2)}) collective-permute-start(s16[24,64,128]{2,1,0:T(8,128)(2,1)S(1)} %get-tuple-element.53), channel_id=1, source_target_pairs={{0,16},{16,32},{32,48},{48,64},{64,80},{80,96},{96,112},{112,0},{1... | collective-permute-start | bytes 1179656 | tf_op jit(solution)/shard_map/ppermute | solution.py:777
  94.1 8.4 %collective-permute-start.3 = (s16[24,64,128]{2,1,0:T(8,128)(2,1)S(1)}, s16[24,64,128]{2,1,0:T(8,128)(2,1)S(1)}, u32[]{:S(2)}, u32[]{:S(2)}) collective-permute-start(s16[24,64,128]{2,1,0:T(8,128)(2,1)S(1)} %get-tuple-element.54), channel_id=1, source_target_pairs={{16,0},{32,16},{48,32},{64,48},{80,64},{96,80},{112,96},{0,112},{1... | collective-permute-start | bytes 1179656 | tf_op jit(solution)/shard_map/ppermute | solution.py:778
  104.2 11.7 %collective-permute-start.4 = (s16[16,64,128]{2,1,0:T(8,128)(2,1)S(1)}, s16[16,64,128]{2,1,0:T(8,128)(2,1)S(1)}, u32[]{:S(2)}, u32[]{:S(2)}) collective-permute-start(s16[16,64,128]{2,1,0:T(8,128)(2,1)S(1)} %get-tuple-element.57), channel_id=1, source_target_pairs={{0,1},{1,2},{2,3},{3,4},{4,5},{5,6},{6,7},{7,8},{8,9},{9,10},{10,1... | collective-permute-start | bytes 786440 | tf_op jit(solution)/shard_map/ppermute | solution.py:777
  104.3 11.6 %collective-permute-start.5 = (s16[16,64,128]{2,1,0:T(8,128)(2,1)S(1)}, s16[16,64,128]{2,1,0:T(8,128)(2,1)S(1)}, u32[]{:S(2)}, u32[]{:S(2)}) collective-permute-start(s16[16,64,128]{2,1,0:T(8,128)(2,1)S(1)} %get-tuple-element.58), channel_id=1, source_target_pairs={{1,0},{2,1},{3,2},{4,3},{5,4},{6,5},{7,6},{8,7},{9,8},{10,9},{11,1... | collective-permute-start | bytes 786440 | tf_op jit(solution)/shard_map/ppermute | solution.py:778
  115.9 23.6 %copy-start.1 = (f32[4]{0:T(128)S(1)}, f32[4]{0:T(128)}, u32[]{:S(2)}) copy-start(f32[4]{0:T(128)} %add_convert_fusion.edge_ref) | copy-start | bytes 52
  115.9 23.6 %copy-start.3 = (f32[8]{0:T(128)S(1)}, f32[8]{0:T(128)}, u32[]{:S(2)}) copy-start(f32[8]{0:T(128)} %offset_ref.9) | copy-start | bytes 100
  132.5 7.0 %collective-permute-start.6 = (s16[16,64,128]{2,1,0:T(8,128)(2,1)S(1)}, s16[16,64,128]{2,1,0:T(8,128)(2,1)S(1)}, u32[]{:S(2)}, u32[]{:S(2)}) collective-permute-start(s16[16,64,128]{2,1,0:T(8,128)(2,1)S(1)} %get-tuple-element.65), channel_id=1, source_target_pairs={{0,16},{16,32},{32,48},{48,64},{64,80},{80,96},{96,112},{112,0},{1... | collective-permute-start | bytes 786440 | tf_op jit(solution)/shard_map/ppermute | solution.py:777
  132.5 7.0 %collective-permute-start.7 = (s16[16,64,128]{2,1,0:T(8,128)(2,1)S(1)}, s16[16,64,128]{2,1,0:T(8,128)(2,1)S(1)}, u32[]{:S(2)}, u32[]{:S(2)}) collective-permute-start(s16[16,64,128]{2,1,0:T(8,128)(2,1)S(1)} %get-tuple-element.66), channel_id=1, source_target_pairs={{16,0},{32,16},{48,32},{64,48},{80,64},{96,80},{112,96},{0,112},{1... | collective-permute-start | bytes 786440 | tf_op jit(solution)/shard_map/ppermute | solution.py:778
  140.8 7.7 %collective-permute-start.8 = (s16[4,64,128]{2,1,0:T(8,128)(2,1)S(1)}, s16[4,64,128]{2,1,0:T(8,128)(2,1)S(1)}, u32[]{:S(2)}, u32[]{:S(2)}) collective-permute-start(s16[4,64,128]{2,1,0:T(8,128)(2,1)S(1)} %get-tuple-element.68), channel_id=1, source_target_pairs={{0,1},{1,2},{2,3},{3,4},{4,5},{5,6},{6,7},{7,8},{8,9},{9,10},{10,1... | collective-permute-start | bytes 196616 | tf_op jit(solution)/shard_map/ppermute | solution.py:777
  140.9 7.6 %collective-permute-start.9 = (s16[4,64,128]{2,1,0:T(8,128)(2,1)S(1)}, s16[4,64,128]{2,1,0:T(8,128)(2,1)S(1)}, u32[]{:S(2)}, u32[]{:S(2)}) collective-permute-start(s16[4,64,128]{2,1,0:T(8,128)(2,1)S(1)} %get-tuple-element.69), channel_id=1, source_target_pairs={{1,0},{2,1},{3,2},{4,3},{5,4},{6,5},{7,6},{8,7},{9,8},{10,9},{11,1... | collective-permute-start | bytes 196616 | tf_op jit(solution)/shard_map/ppermute | solution.py:778
  149.8 10.0 %collective-permute-start.12 = (s16[1056,128]{1,0:T(8,128)(2,1)S(1)}, s16[1056,128]{1,0:T(8,128)(2,1)S(1)}, u32[]{:S(2)}, u32[]{:S(2)}) collective-permute-start(s16[1056,128]{1,0:T(8,128)(2,1)S(1)} %finish.1.refs_0_), channel_id=1, source_target_pairs={{96,0},{112,16},{0,32},{16,48},{32,64},{48,80},{64,96},{80,112},{9... | collective-permute-start | bytes 811016 | tf_op jit(solution)/shard_map/ppermute | solution.py:784
  149.9 13.5 %collective-permute-start.11 = (s16[1056,128]{1,0:T(8,128)(2,1)S(1)}, s16[1056,128]{1,0:T(8,128)(2,1)S(1)}, u32[]{:S(2)}, u32[]{:S(2)}) collective-permute-start(s16[1056,128]{1,0:T(8,128)(2,1)S(1)} %finish.1.refs_0_), channel_id=1, source_target_pairs={{64,0},{80,16},{96,32},{112,48},{0,64},{16,80},{32,96},{48,112},{6... | collective-permute-start | bytes 811016 | tf_op jit(solution)/shard_map/ppermute | solution.py:784
  151.5 13.7 %collective-permute-start.10 = (s16[1056,128]{1,0:T(8,128)(2,1)S(1)}, s16[1056,128]{1,0:T(8,128)(2,1)S(1)}, u32[]{:S(2)}, u32[]{:S(2)}) collective-permute-start(s16[1056,128]{1,0:T(8,128)(2,1)S(1)} %finish.1.refs_0_), channel_id=1, source_target_pairs={{32,0},{48,16},{64,32},{80,48},{96,64},{112,80},{0,96},{16,112},{3... | collective-permute-start | bytes 811016 | tf_op jit(solution)/shard_map/ppermute | solution.py:784
  154.1 11.2 %collective-permute-start.13 = (s16[1056,128]{1,0:T(8,128)(2,1)S(1)}, s16[1056,128]{1,0:T(8,128)(2,1)S(1)}, u32[]{:S(2)}, u32[]{:S(2)}) collective-permute-start(s16[1056,128]{1,0:T(8,128)(2,1)S(1)} %finish.1.refs_0_), channel_id=1, source_target_pairs={{0,16},{16,0},{32,48},{48,32},{64,80},{80,64},{96,112},{112,96},{1... | collective-permute-start | bytes 811016 | tf_op jit(solution)/shard_map/ppermute | solution.py:787
  159.8 5.4 %collective-permute-start.16 = (s16[1056,128]{1,0:T(8,128)(2,1)S(1)}, s16[1056,128]{1,0:T(8,128)(2,1)S(1)}, u32[]{:S(2)}, u32[]{:S(2)}) collective-permute-start(s16[1056,128]{1,0:T(8,128)(2,1)S(1)} %collective-permute-done.12.refs_3_), channel_id=1, source_target_pairs={{0,16},{16,0},{32,48},{48,32},{64,80},{80,64},{96,112},{112,96},{1... | collective-permute-start | bytes 811016 | tf_op jit(solution)/shard_map/ppermute | solution.py:787
  163.4 2.1 %collective-permute-start.15 = (s16[1056,128]{1,0:T(8,128)(2,1)S(1)}, s16[1056,128]{1,0:T(8,128)(2,1)S(1)}, u32[]{:S(2)}, u32[]{:S(2)}) collective-permute-start(s16[1056,128]{1,0:T(8,128)(2,1)S(1)} %collective-permute-done.11.refs_2_), channel_id=1, source_target_pairs={{0,16},{16,0},{32,48},{48,32},{64,80},{80,64},{96,112},{112,96},{1... | collective-permute-start | bytes 811016 | tf_op jit(solution)/shard_map/ppermute | solution.py:787
  165.2 1.5 collective-permute-start.14

commit v7 on v6

--- a/solution.py
+++ b/solution.py
@@ -78,7 +78,8 @@
     return total * 1.05
 
 
-def band_kernel(taps_ref, shift_ref, ky_ref, kyt_ref, kx_ref, kxt_ref, bzf_ref, bza_ref):
+def band_kernel(taps_ref, shift_ref, ky_ref, kyt_ref, kx_ref, kxt_ref, bzf_ref, bza_ref, swap_ref):
+    swap_ref[...] = digit_swap((512, 512))
     radius = (TAPS - 1) // 2
 
     def fill(difference, view, axis):
@@ -142,9 +143,10 @@
             jax.ShapeDtypeStruct((VIEWS, 128, ROWS), BF16),
             jax.ShapeDtypeStruct((VIEWS * 64, 192), BF16),
             jax.ShapeDtypeStruct((192, VIEWS * 64), BF16),
+            jax.ShapeDtypeStruct((512, 512), BF16),
         ),
         in_specs=smem(2),
-        out_specs=tuple(vmem(6)),
+        out_specs=tuple(vmem(7)),
         name="bands",
     )(taps, shifts)
 
@@ -447,13 +449,9 @@
 
 
 def first_adjoint_kernel(start_ref, source_ref, place_ref, inverse_ref, offset_ref, incoming_ref, blurred_ref, kyt_ref,
-                         kxt_ref, bza_ref, main_ref, tail_ref, to_left_ref, to_right_ref, average_ref, total_ref,
-                         depth_ref, swap_ref):
+                         kxt_ref, bza_ref, swap_ref, main_ref, tail_ref, to_left_ref, to_right_ref, average_ref,
+                         total_ref, depth_ref):
     step = pl.program_id(0)
-
-    @pl.when(step == 0)
-    def _():
-        swap_ref[...] = digit_swap((512, 512))
 
     for slot in range(2 * SLOTS):
         total_ref[slot] = jnp.zeros((NY, 128), F32)
@@ -493,20 +491,19 @@
         adjoint_depth(scale, bza_ref, depth_ref, main_ref, tail_ref, to_left_ref, to_right_ref)
 
 
-def first_adjoint(start, source, place, inverse, offset, incoming, blurred, kyt, kxt, bza):
+def first_adjoint(start, source, place, inverse, offset, incoming, blurred, kyt, kxt, bza, swap):
     share = incoming.shape[0] // (VIEWS // 2)
     return pl.pallas_call(
         first_adjoint_kernel,
         grid=(VIEWS // 2,),
         out_shape=PARTIAL_SHAPES + (jax.ShapeDtypeStruct((VIEWS, ROWS, 2 * ROWS), BF16),),
         in_specs=smem(5) + [pl.BlockSpec((share, NY, 128), lambda view: (view, 0, 0)), per_view(ROWS, 2 * ROWS),
-                            per_view(ROWS, ROWS), per_view(128, ROWS)] + vmem(1),
+                            per_view(ROWS, ROWS), per_view(128, ROWS)] + vmem(2),
         out_specs=tuple(vmem(4)) + (per_view(ROWS, 2 * ROWS),),
-        scratch_shapes=[pltpu.VMEM((2 * SLOTS, NY, 128), F32), pltpu.VMEM((QUADS, VIEWS * 64, ROWS), BF16),
-                        pltpu.VMEM((512, 512), BF16)],
+        scratch_shapes=[pltpu.VMEM((2 * SLOTS, NY, 128), F32), pltpu.VMEM((QUADS, VIEWS * 64, ROWS), BF16)],
         name="first_adjoint",
         compiler_params=room(60),
-    )(start, source, place, inverse, offset, incoming, blurred, kyt, kxt, bza)
+    )(start, source, place, inverse, offset, incoming, blurred, kyt, kxt, bza, swap)
 
 
 def join_columns_kernel(offset_ref, edge_ref, main_ref, tail_ref, from_left_ref, from_right_ref, out_main_ref, out_tail_ref,
@@ -756,7 +753,7 @@
                     out_ref[h, 0, j + 1, lines, lanes] = (results[h] >> 16).astype(F32) * units[half]
         return carry
 
-    lax.fori_loop(0, 4, sixteen_rows, 0)
+    lax.fori_loop(0, 4, sixteen_rows, 0, unroll=2)
 
 
 def assemble(index, chunks):
@@ -812,7 +809,7 @@
 
     main = window_estimate(index, estimate0)
     kernel = psf_taps / jnp.sum(psf_taps, axis=2, keepdims=True)
-    ky, kyt, kx, kxt, bzf, bza = build_bands(kernel.reshape(-1), psf_shift.reshape(-1))
+    ky, kyt, kx, kxt, bzf, bza, swap = build_bands(kernel.reshape(-1), psf_shift.reshape(-1))
     blurred, tail = forward(edges, main, from_low, from_high, bzf, ky, kx)
 
     earlier = jnp.tril(jnp.ones((SLOTS, SLOTS), jnp.bool_), -1)
@@ -864,7 +861,7 @@
 
     incoming, scale_main, scale_tail = lax.optimization_barrier((incoming, scale_main, scale_tail))
     part_main, part_tail, to_left, to_right, average = first_adjoint(
-        start, source, place, inverse.reshape(-1), background, incoming, blurred, kyt, kxt, bza)
+        start, source, place, inverse.reshape(-1), background, incoming, blurred, kyt, kxt, bza, swap)
     from_left, from_right = to_neighbours(to_right, to_left, "view")
     part_main, part_tail, low, high = join_columns(background, edges, part_main, part_tail, from_left, from_right)
     from_low, from_high = to_neighbours(high, low, "block")

time: 173 us -> 172 us (level)
  no operation moved by 1% of the time
where the time goes in v7:
time: 172 us; the launch traced here: 171 us
  Pallas kernels  68.8 us (40%)
  waiting for transfers between devices  45.1 us (26%)
  starting transfers between devices  39.1 us (23%)
  local copies, waits for them, and re-layouts  8.85 us (5%)
  other arithmetic  8.27 us (5%)
    ppermute x5, waiting for transfers between devices, to_neighbours(): lax.ppermute(upward, axis, [(i, (i + 1) % count) for i in range(count)])  33.4 us
    ppermute x5, starting transfers between devices, to_neighbours(): lax.ppermute(downward, axis, [((i + 1) % count, i) for i in range(count)])  21 us
    pallas_call x1, Pallas kernels, second(): pl.pallas_call(second_kernel, grid=(VIEWS // 2,), out_shape=(held((QUADS,...  16.5 us
    all_to_all x1, starting transfers between devices, program(): lax.all_to_all(outgoing.reshape(VIEWS * block_count, CAP, NY, 128), ('vie...  11.7 us
    pallas_call x1, Pallas kernels, first_adjoint(): pl.pallas_call(first_adjoint_kernel, grid=(VIEWS // 2,), out_shape=PARTIA...  11.2 us
    pallas_call x1, Pallas kernels, forward(): pl.pallas_call(forward_kernel, out_shape=(jax.ShapeDtypeStruct((VIEWS, RO...  10.4 us
    ppermute x3, waiting for transfers between devices, gather_parts(): lax.ppermute(own, 'view', [((i + 2 * step) % VIEWS, i) for i in range(VIE...  10.2 us
    pallas_call x1, Pallas kernels, build_bands(): pl.pallas_call(band_kernel, out_shape=(jax.ShapeDtypeStruct((VIEWS, ROWS,...  7.12 us
  transfers between devices with their start and end apart: 18, of which 10 were waited for; matrix products, arithmetic and copies ran while one was open for 9% of the time, Pallas kernels for 16%

profile of v7, /device:TPU:0, one launch (start us, length us, event | category | flops | bytes accessed | tf_op | source)
XLA Modules:
  0.0 170.5 jit_solution(6176459910518316115)
XLA Ops:
  0.0 0.7 reduce
  0.8 0.6 dynamic-slice_bitcast_fusion.target_ref
  1.4 5.6 %pack.1 = (bf16[8,32,64,128]{3,2,1,0:T(8,128)(2,1)}, bf16[8,64,128]{2,1,0:T(8,128)(2,1)}, bf16[8,64,128]{2,1,0:T(8,128)(2,1)}) custom-call(s32[1]{0:T(128)} %bitcast.index_ref, s32[16]{0:T(128)} %dynamic-slice_bitcast_fusion.target_ref, bf16[16,4,64,256]{3,2,1,0:T(8,128)(2,1)} %bitcast.39, f32[64,64,256]{2,1,0:T(8,128)} %estimate_ref.1, ...), custom_call_target="tpu_custom_call" | custom-call | tf_op jit(solution)/shard_map/pack/pallas_call | solution.py:210
  7.1 11.7 %all-to-all-start = ((bf16[128,2,64,128]{3,2,1,0:T(8,128)(2,1)}), bf16[128,2,64,128]{3,2,1,0:T(8,128)(2,1)}, u32[]{:S(2)}, u32[]{:S(2)}) async-start(bf16[128,2,64,128]{3,2,1,0:T(8,128)(2,1)} %bitcast.36), calls=%async_computation | async-start | bytes 8388608 | tf_op jit(solution)/shard_map/all_to_all | solution.py:807
  18.8 1.0 collective-permute-start
  19.8 4.5 %collective-permute-start.1 = (bf16[8,64,128]{2,1,0:T(8,128)(2,1)S(1)}, bf16[8,64,128]{2,1,0:T(8,128)(2,1)S(1)}, u32[]{:S(2)}, u32[]{:S(2)}) collective-permute-start(bf16[8,64,128]{2,1,0:T(8,128)(2,1)S(1)} %copy-done.10), channel_id=1, source_target_pairs={{1,0},{2,1},{3,2},{4,3},{5,4},{6,5},{7,6},{8,7},{9,8},{10,9},{11,1... | collective-permute-start | bytes 393224 | tf_op jit(solution)/shard_map/ppermute | solution.py:775
  24.4 2.5 %convert_reduce_fusion = s32[8,16,16]{2,1,0:T(8,128)S(1)} fusion(s32[8,16,16]{2,1,0:T(8,128)S(1)} %reshape_squeeze.3, pred[16,16]{1,0:T(8,128)(4,1)S(1)} %iota_compare_fusion.6), kind=kLoop, calls=%fused_computation.2 | loop fusion | flops 129024 | bytes 16640 | tf_op jit(solution)/shard_map/reduce_sum | solution.py:817
  27.0 0.4 select_reduce_fusion.2
  27.5 0.1 copy.32
  27.7 0.4 fusion
  28.5 0.1 select_reduce_fusion.3
  28.8 0.1 sub.102
  29.0 0.1 copy.37
  29.1 0.1 broadcast_in_dim.292
  29.3 0.2 slice_reduce_fusion.19
  29.5 0.5 slice_reduce_fusion.20
  30.1 0.8 multiply_reduce_fusion
  31.0 0.1 copy.39
  31.1 0.6 convert_reduce_fusion.3.start_ref
  31.8 0.2 convert_reduce_fusion.2
  32.0 0.1 convert_reduce_fusion.1
  32.1 0.1 select_reduce_fusion.4
  32.2 0.2 broadcast_multiply_fusion
  32.4 0.2 fusion.32
  32.7 0.3 maximum_bitcast_fusion
  33.0 0.7 add_convert_fusion.edge_ref
  33.7 0.1 slice.145
  33.9 6.0 %window.1.main_ref.estimate_main_ref = f32[2,1024,128]{2,1,0:T(8,128)} custom-call(s32[1]{0:T(128)} %bitcast.index_ref, f32[64,64,256]{2,1,0:T(8,128)} %estimate_ref.1), custom_call_target="tpu_custom_call" | custom-call | tf_op jit(solution)/shard_map/window/pallas_call | solution.py:255
  39.9 0.7 reshape.278.shift_ref
  40.5 0.7 reshape.277.taps_ref
  41.2 0.7 reshape.270.rows_ref
  41.9 0.6 div.30.inverse_ref
  42.5 0.3 reshape.280
  42.8 0.2 reshape.275
  43.1 7.1 %bands.1 = (bf16[8,256,256]{2,1,0:T(8,128)(2,1)}, bf16[8,256,256]{2,1,0:T(8,128)(2,1)}, bf16[8,256,128]{2,1,0:T(8,128)(2,1)}, bf16[8,128,256]{2,1,0:T(8,128)(2,1...) custom-call(f32[504]{0:T(512)} %reshape.277.taps_ref, s32[24]{0:T(128)} %reshape.278.shift_ref), custom_call_target="tpu_custom_call" | custom-call | tf_op jit(solution)/shard_map/bands/pallas_call | solution.py:137
  50.2 0.8 broadcast_in_dim.296
  50.9 0.9 broadcast_in_dim.295
  51.8 3.9 %weights.1 = (f32[2,1024,128]{2,1,0:T(8,128)}, f32[16,64,128]{2,1,0:T(8,128)}) custom-call(f32[512]{0:T(512)} %reshape.270.rows_ref, f32[8,2,64,128]{3,2,1,0:T(8,128)} %bitcast.37, f32[8,64,128]{2,1,0:T(8,128)} %bitcast.40), custom_call_target="tpu_custom_call" | custom-call | tf_op jit(solution)/shard_map/weights/pallas_call | solution.py:302
  55.7 0.7 select_reduce_fusion
  56.5 15.3 %collective-permute-done.from_low_ref = bf16[8,64,128]{2,1,0:T(8,128)(2,1)S(1)} collective-permute-done((bf16[8,64,128]{2,1,0:T(8,128)(2,1)S(1)}, bf16[8,64,128]{2,1,0:T(8,128)(2,1)S(1)}, u32[]{:S(2)}, u32[]{:S(2)}) %collective-permute-start) | collective-permute-done | bytes 131104 | tf_op jit(solution)/shard_map/ppermute | solution.py:774
  71.8 0.6 copy-done.4
  72.5 10.4 %forward.1 = (bf16[8,256,512]{2,1,0:T(8,128)(2,1)}, f32[16,64,128]{2,1,0:T(8,128)}) custom-call(f32[4]{0:T(128)} %add_convert_fusion.edge_ref, f32[2,1024,128]{2,1,0:T(8,128)} %window.1.main_ref.estimate_main_ref, bf16[8,64,128]{2,1,0:T(8,128)(2,1)} %copy-done.4, bf16[8,64,128]{2,1,0:T(8,128)(2,1)} %copy-done.5, bf16[512,192]{1,0:T(8,128)(2,1)} %get-tuple-element.45.bzf_ref, ...), custom_call_target="tpu_custom_call" | custom-call | tf_op jit(solution)/shard_map/forward/pallas_call | solution.py:426
  82.9 11.2 %first_adjoint.1 = (f32[2,1024,128]{2,1,0:T(8,128)S(1)}, f32[16,64,128]{2,1,0:T(8,128)S(1)}, s16[24,64,128]{2,1,0:T(8,128)(2,1)S(1)}, s16[24,64,128]{2,1,0:T(8,128)(2,1)S(1)}, bf16[8,256,512]{2,1,0:T(8,128)(2,1)}) custom-call(s32[9]{0:T(128)} %convert_reduce_fusion.3.start_ref, s32[256]{0:T(256)} %get-tuple-element.95.source_ref, ...), custom_call_target="tpu_custom_call" | custom-call | tf_op jit(solution)/shard_map/first_adjoint/pallas_call | solution.py:496
  94.1 2.9 %collective-permute-start.3 = (s16[24,64,128]{2,1,0:T(8,128)(2,1)S(1)}, s16[24,64,128]{2,1,0:T(8,128)(2,1)S(1)}, u32[]{:S(2)}, u32[]{:S(2)}) collective-permute-start(s16[24,64,128]{2,1,0:T(8,128)(2,1)S(1)} %get-tuple-element.56), channel_id=1, source_target_pairs={{16,0},{32,16},{48,32},{64,48},{80,64},{96,80},{112,96},{0,112},{1... | collective-permute-start | bytes 1179656 | tf_op jit(solution)/shard_map/ppermute | solution.py:775
  97.0 5.5 %collective-permute-done.2.from_left_ref = s16[24,64,128]{2,1,0:T(8,128)(2,1)S(1)} collective-permute-done((s16[24,64,128]{2,1,0:T(8,128)(2,1)S(1)}, s16[24,64,128]{2,1,0:T(8,128)(2,1)S(1)}, u32[]{:S(2)}, u32[]{:S(2)}) %collective-permute-start.2) | collective-permute-done | bytes 393248 | tf_op jit(solution)/shard_map/ppermute | solution.py:774
  102.5 1.7 join_columns.1
  104.3 5.3 %collective-permute-start.5 = (s16[16,64,128]{2,1,0:T(8,128)(2,1)S(1)}, s16[16,64,128]{2,1,0:T(8,128)(2,1)S(1)}, u32[]{:S(2)}, u32[]{:S(2)}) collective-permute-start(s16[16,64,128]{2,1,0:T(8,128)(2,1)S(1)} %get-tuple-element.60), channel_id=1, source_target_pairs={{1,0},{2,1},{3,2},{4,3},{5,4},{6,5},{7,6},{8,7},{9,8},{10,9},{11,1... | collective-permute-start | bytes 786440 | tf_op jit(solution)/shard_map/ppermute | solution.py:775
  109.6 6.3 %collective-permute-done.4.from_low_ref = s16[16,64,128]{2,1,0:T(8,128)(2,1)S(1)} collective-permute-done((s16[16,64,128]{2,1,0:T(8,128)(2,1)S(1)}, s16[16,64,128]{2,1,0:T(8,128)(2,1)S(1)}, u32[]{:S(2)}, u32[]{:S(2)}) %collective-permute-start.4) | collective-permute-done | bytes 262176 | tf_op jit(solution)/shard_map/ppermute | solution.py:774
  115.9 16.5 %second.1 = (f32[16,64,128]{2,1,0:T(8,128)S(1)}, f32[16,64,128]{2,1,0:T(8,128)S(1)}, f32[16,64,128]{2,1,0:T(8,128)S(1)}, s16[16,64,128]{2,1,0:T(8,128)(2,1)S(1)}, s16[16,64,128]{2,1,0:T(8,128)(2,1)S(1)}) custom-call(f32[8]{0:T(128)} %offset_ref.9, f32[4]{0:T(128)} %add_convert_fusion.edge_ref, f32[2,1024,128]{2,1,0:T(8,128)S(1)} %get-tuple-element.57.part_main_ref, ...), custom_call_target="tpu_custom_call" | custom-call | tf_op jit(solution)/shard_map/second/pallas_call | solution.py:614
  132.5 2.9 %collective-permute-start.7 = (s16[16,64,128]{2,1,0:T(8,128)(2,1)S(1)}, s16[16,64,128]{2,1,0:T(8,128)(2,1)S(1)}, u32[]{:S(2)}, u32[]{:S(2)}) collective-permute-start(s16[16,64,128]{2,1,0:T(8,128)(2,1)S(1)} %get-tuple-element.68), channel_id=1, source_target_pairs={{16,0},{32,16},{48,32},{64,48},{80,64},{96,80},{112,96},{0,112},{1... | collective-permute-start | bytes 786440 | tf_op jit(solution)/shard_map/ppermute | solution.py:775
  135.4 4.1 %collective-permute-done.6.from_left_ref = s16[16,64,128]{2,1,0:T(8,128)(2,1)S(1)} collective-permute-done((s16[16,64,128]{2,1,0:T(8,128)(2,1)S(1)}, s16[16,64,128]{2,1,0:T(8,128)(2,1)S(1)}, u32[]{:S(2)}, u32[]{:S(2)}) %collective-permute-start.6) | collective-permute-done | bytes 262176 | tf_op jit(solution)/shard_map/ppermute | solution.py:774
  139.5 1.3 join_own.1
  140.9 5.3 %collective-permute-start.9 = (s16[4,64,128]{2,1,0:T(8,128)(2,1)S(1)}, s16[4,64,128]{2,1,0:T(8,128)(2,1)S(1)}, u32[]{:S(2)}, u32[]{:S(2)}) collective-permute-start(s16[4,64,128]{2,1,0:T(8,128)(2,1)S(1)} %get-tuple-element.71), channel_id=1, source_target_pairs={{1,0},{2,1},{3,2},{4,3},{5,4},{6,5},{7,6},{8,7},{9,8},{10,9},{11,1... | collective-permute-start | bytes 196616 | tf_op jit(solution)/shard_map/ppermute | solution.py:775
  146.2 2.2 %collective-permute-done.8.from_low_ref = s16[4,64,128]{2,1,0:T(8,128)(2,1)S(1)} collective-permute-done((s16[4,64,128]{2,1,0:T(8,128)(2,1)S(1)}, s16[4,64,128]{2,1,0:T(8,128)(2,1)S(1)}, u32[]{:S(2)}, u32[]{:S(2)}) %collective-permute-start.8) | collective-permute-done | bytes 65568 | tf_op jit(solution)/shard_map/ppermute | solution.py:774
  148.5 1.3 finish.1.refs_0_
  149.9 1.6 collective-permute-start.11
  151.5 2.5 %collective-permute-start.10 = (s16[1056,128]{1,0:T(8,128)(2,1)S(1)}, s16[1056,128]{1,0:T(8,128)(2,1)S(1)}, u32[]{:S(2)}, u32[]{:S(2)}) collective-permute-start(s16[1056,128]{1,0:T(8,128)(2,1)S(1)} %finish.1.refs_0_), channel_id=1, source_target_pairs={{32,0},{48,16},{64,32},{80,48},{96,64},{112,80},{0,96},{16,112},{3... | collective-permute-start | bytes 811016 | tf_op jit(solution)/shard_map/ppermute | solution.py:781
  154.1 5.8 %collective-permute-done.12.refs_3_ = s16[1056,128]{1,0:T(8,128)(2,1)S(1)} collective-permute-done((s16[1056,128]{1,0:T(8,128)(2,1)S(1)}, s16[1056,128]{1,0:T(8,128)(2,1)S(1)}, u32[]{:S(2)}, u32[]{:S(2)}) %collective-permute-start.12) | collective-permute-done | bytes 270368 | tf_op jit(solution)/shard_map/ppermute | solution.py:781
  159.8 3.6 %collective-permute-done.11.refs_2_ = s16[1056,128]{1,0:T(8,128)(2,1)S(1)} collective-permute-done((s16[1056,128]{1,0:T(8,128)(2,1)S(1)}, s16[1056,128]{1,0:T(8,128)(2,1)S(1)}, u32[]{:S(2)}, u32[]{:S(2)}) %collective-permute-start.11) | collective-permute-done | bytes 270368 | tf_op jit(solution)/shard_map/ppermute | solution.py:781
  163.4 1.0 collective-permute-start.15
  164.4 0.9 collective-permute-done.10.refs_1_
  165.2 0.3 collective-permute-done.15.refs_6_
  165.5 1.2 collective-permute-done.14.refs_5_
  166.8 3.8 %assemble.1 = f32[4,4,4,64,256]{4,3,2,1,0:T(8,128)} custom-call(s32[1]{0:T(128)} %bitcast.index_ref, s16[1056,128]{1,0:T(8,128)(2,1)S(1)} %finish.1.refs_0_, s16[1056,128]{1,0:T(8,128)(2,1)S(1)} %collective-permute-done.10.refs_1_, s16[1056,128]{1,0:T(8,128)(2,1)S(1)} %collective-permute-done.11.refs_2_, ...), custom_call_target="tpu_custom_call" | custom-call | tf_op jit(solution)/shard_map/assemble/pallas_call | solution.py:760
  (74 shorter events, 1.8 us)
Async XLA Ops:
  7.0 11.8 %copy-start.11 = (bf16[8,64,128]{2,1,0:T(8,128)(2,1)S(1)}, bf16[8,64,128]{2,1,0:T(8,128)(2,1)}, u32[]{:S(2)}) copy-start(bf16[8,64,128]{2,1,0:T(8,128)(2,1)} %get-tuple-element.43) | copy-start | bytes 393220
  7.1 12.7 %copy-start.10 = (bf16[8,64,128]{2,1,0:T(8,128)(2,1)S(1)}, bf16[8,64,128]{2,1,0:T(8,128)(2,1)}, u32[]{:S(2)}) copy-start(bf16[8,64,128]{2,1,0:T(8,128)(2,1)} %get-tuple-element.44) | copy-start | bytes 393220
  7.1 17.2 %copy-start.7 = (s32[8,256,1]{1,2,0:T(1,128)S(1)}, s32[8,256,1]{1,2,0:T(1,128)}, u32[]{:S(2)}) copy-start(s32[8,256,1]{1,2,0:T(1,128)} %param.9) | copy-start | bytes 24580
  7.1 17.2 %copy-start.8 = (s32[8,256]{1,0:T(8,128)S(1)}, s32[8,256]{1,0:T(8,128)}, u32[]{:S(2)}) copy-start(s32[8,256]{1,0:T(8,128)} %param.10) | copy-start | bytes 24580
  7.1 21.0 %copy-start.6 = (f32[8,3,21]{2,0,1:T(8,128)S(1)}, f32[8,3,21]{2,0,1:T(8,128)}, u32[]{:S(2)}) copy-start(f32[8,3,21]{2,0,1:T(8,128)} %param.12) | copy-start | bytes 6052
  7.1 21.3 %copy-start.9 = (s32[8,3]{0,1:T(4,128)S(1)}, s32[8,3]{0,1:T(4,128)}, u32[]{:S(2)}) copy-start(s32[8,3]{0,1:T(4,128)} %param.11) | copy-start | bytes 292
  7.1 75.8 %all-to-all-start = ((bf16[128,2,64,128]{3,2,1,0:T(8,128)(2,1)}), bf16[128,2,64,128]{3,2,1,0:T(8,128)(2,1)}, u32[]{:S(2)}, u32[]{:S(2)}) async-start(bf16[128,2,64,128]{3,2,1,0:T(8,128)(2,1)} %bitcast.36), calls=%async_computation | async-start | bytes 8388608 | tf_op jit(solution)/shard_map/all_to_all | solution.py:807
  18.8 53.0 %collective-permute-start = (bf16[8,64,128]{2,1,0:T(8,128)(2,1)S(1)}, bf16[8,64,128]{2,1,0:T(8,128)(2,1)S(1)}, u32[]{:S(2)}, u32[]{:S(2)}) collective-permute-start(bf16[8,64,128]{2,1,0:T(8,128)(2,1)S(1)} %copy-done.11), channel_id=1, source_target_pairs={{0,1},{1,2},{2,3},{3,4},{4,5},{5,6},{6,7},{7,8},{8,9},{9,10},{10,1... | collective-permute-start | bytes 393224 | tf_op jit(solution)/shard_map/ppermute | solution.py:774
  19.8 52.0 %collective-permute-start.1 = (bf16[8,64,128]{2,1,0:T(8,128)(2,1)S(1)}, bf16[8,64,128]{2,1,0:T(8,128)(2,1)S(1)}, u32[]{:S(2)}, u32[]{:S(2)}) collective-permute-start(bf16[8,64,128]{2,1,0:T(8,128)(2,1)S(1)} %copy-done.10), channel_id=1, source_target_pairs={{1,0},{2,1},{3,2},{4,3},{5,4},{6,5},{7,6},{8,7},{9,8},{10,9},{11,1... | collective-permute-start | bytes 393224 | tf_op jit(solution)/shard_map/ppermute | solution.py:775
  71.8 0.6 copy-start.4
  71.8 0.7 copy-start.5
  82.9 19.6 %copy-start = (f32[4]{0:T(128)S(1)}, f32[4]{0:T(128)}, u32[]{:S(2)}) copy-start(f32[4]{0:T(128)} %add_convert_fusion.edge_ref) | copy-start | bytes 52
  82.9 19.6 %copy-start.2 = (f32[8]{0:T(128)S(1)}, f32[8]{0:T(128)}, u32[]{:S(2)}) copy-start(f32[8]{0:T(128)} %offset_ref.9) | copy-start | bytes 100
  94.1 8.4 %collective-permute-start.2 = (s16[24,64,128]{2,1,0:T(8,128)(2,1)S(1)}, s16[24,64,128]{2,1,0:T(8,128)(2,1)S(1)}, u32[]{:S(2)}, u32[]{:S(2)}) collective-permute-start(s16[24,64,128]{2,1,0:T(8,128)(2,1)S(1)} %get-tuple-element.55), channel_id=1, source_target_pairs={{0,16},{16,32},{32,48},{48,64},{64,80},{80,96},{96,112},{112,0},{1... | collective-permute-start | bytes 1179656 | tf_op jit(solution)/shard_map/ppermute | solution.py:774
  94.1 8.4 %collective-permute-start.3 = (s16[24,64,128]{2,1,0:T(8,128)(2,1)S(1)}, s16[24,64,128]{2,1,0:T(8,128)(2,1)S(1)}, u32[]{:S(2)}, u32[]{:S(2)}) collective-permute-start(s16[24,64,128]{2,1,0:T(8,128)(2,1)S(1)} %get-tuple-element.56), channel_id=1, source_target_pairs={{16,0},{32,16},{48,32},{64,48},{80,64},{96,80},{112,96},{0,112},{1... | collective-permute-start | bytes 1179656 | tf_op jit(solution)/shard_map/ppermute | solution.py:775
  104.2 11.7 %collective-permute-start.4 = (s16[16,64,128]{2,1,0:T(8,128)(2,1)S(1)}, s16[16,64,128]{2,1,0:T(8,128)(2,1)S(1)}, u32[]{:S(2)}, u32[]{:S(2)}) collective-permute-start(s16[16,64,128]{2,1,0:T(8,128)(2,1)S(1)} %get-tuple-element.59), channel_id=1, source_target_pairs={{0,1},{1,2},{2,3},{3,4},{4,5},{5,6},{6,7},{7,8},{8,9},{9,10},{10,1... | collective-permute-start | bytes 786440 | tf_op jit(solution)/shard_map/ppermute | solution.py:774
  104.3 11.6 %collective-permute-start.5 = (s16[16,64,128]{2,1,0:T(8,128)(2,1)S(1)}, s16[16,64,128]{2,1,0:T(8,128)(2,1)S(1)}, u32[]{:S(2)}, u32[]{:S(2)}) collective-permute-start(s16[16,64,128]{2,1,0:T(8,128)(2,1)S(1)} %get-tuple-element.60), channel_id=1, source_target_pairs={{1,0},{2,1},{3,2},{4,3},{5,4},{6,5},{7,6},{8,7},{9,8},{10,9},{11,1... | collective-permute-start | bytes 786440 | tf_op jit(solution)/shard_map/ppermute | solution.py:775
  115.9 23.6 %copy-start.1 = (f32[4]{0:T(128)S(1)}, f32[4]{0:T(128)}, u32[]{:S(2)}) copy-start(f32[4]{0:T(128)} %add_convert_fusion.edge_ref) | copy-start | bytes 52
  115.9 23.6 %copy-start.3 = (f32[8]{0:T(128)S(1)}, f32[8]{0:T(128)}, u32[]{:S(2)}) copy-start(f32[8]{0:T(128)} %offset_ref.9) | copy-start | bytes 100
  132.4 7.0 %collective-permute-start.6 = (s16[16,64,128]{2,1,0:T(8,128)(2,1)S(1)}, s16[16,64,128]{2,1,0:T(8,128)(2,1)S(1)}, u32[]{:S(2)}, u32[]{:S(2)}) collective-permute-start(s16[16,64,128]{2,1,0:T(8,128)(2,1)S(1)} %get-tuple-element.67), channel_id=1, source_target_pairs={{0,16},{16,32},{32,48},{48,64},{64,80},{80,96},{96,112},{112,0},{1... | collective-permute-start | bytes 786440 | tf_op jit(solution)/shard_map/ppermute | solution.py:774
  132.5 7.0 %collective-permute-start.7 = (s16[16,64,128]{2,1,0:T(8,128)(2,1)S(1)}, s16[16,64,128]{2,1,0:T(8,128)(2,1)S(1)}, u32[]{:S(2)}, u32[]{:S(2)}) collective-permute-start(s16[16,64,128]{2,1,0:T(8,128)(2,1)S(1)} %get-tuple-element.68), channel_id=1, source_target_pairs={{16,0},{32,16},{48,32},{64,48},{80,64},{96,80},{112,96},{0,112},{1... | collective-permute-start | bytes 786440 | tf_op jit(solution)/shard_map/ppermute | solution.py:775
  140.8 7.7 %collective-permute-start.8 = (s16[4,64,128]{2,1,0:T(8,128)(2,1)S(1)}, s16[4,64,128]{2,1,0:T(8,128)(2,1)S(1)}, u32[]{:S(2)}, u32[]{:S(2)}) collective-permute-start(s16[4,64,128]{2,1,0:T(8,128)(2,1)S(1)} %get-tuple-element.70), channel_id=1, source_target_pairs={{0,1},{1,2},{2,3},{3,4},{4,5},{5,6},{6,7},{7,8},{8,9},{9,10},{10,1... | collective-permute-start | bytes 196616 | tf_op jit(solution)/shard_map/ppermute | solution.py:774
  140.9 7.6 %collective-permute-start.9 = (s16[4,64,128]{2,1,0:T(8,128)(2,1)S(1)}, s16[4,64,128]{2,1,0:T(8,128)(2,1)S(1)}, u32[]{:S(2)}, u32[]{:S(2)}) collective-permute-start(s16[4,64,128]{2,1,0:T(8,128)(2,1)S(1)} %get-tuple-element.71), channel_id=1, source_target_pairs={{1,0},{2,1},{3,2},{4,3},{5,4},{6,5},{7,6},{8,7},{9,8},{10,9},{11,1... | collective-permute-start | bytes 196616 | tf_op jit(solution)/shard_map/ppermute | solution.py:775
  149.8 10.0 %collective-permute-start.12 = (s16[1056,128]{1,0:T(8,128)(2,1)S(1)}, s16[1056,128]{1,0:T(8,128)(2,1)S(1)}, u32[]{:S(2)}, u32[]{:S(2)}) collective-permute-start(s16[1056,128]{1,0:T(8,128)(2,1)S(1)} %finish.1.refs_0_), channel_id=1, source_target_pairs={{96,0},{112,16},{0,32},{16,48},{32,64},{48,80},{64,96},{80,112},{9... | collective-permute-start | bytes 811016 | tf_op jit(solution)/shard_map/ppermute | solution.py:781
  149.9 13.5 %collective-permute-start.11 = (s16[1056,128]{1,0:T(8,128)(2,1)S(1)}, s16[1056,128]{1,0:T(8,128)(2,1)S(1)}, u32[]{:S(2)}, u32[]{:S(2)}) collective-permute-start(s16[1056,128]{1,0:T(8,128)(2,1)S(1)} %finish.1.refs_0_), channel_id=1, source_target_pairs={{64,0},{80,16},{96,32},{112,48},{0,64},{16,80},{32,96},{48,112},{6... | collective-permute-start | bytes 811016 | tf_op jit(solution)/shard_map/ppermute | solution.py:781
  151.5 13.7 %collective-permute-start.10 = (s16[1056,128]{1,0:T(8,128)(2,1)S(1)}, s16[1056,128]{1,0:T(8,128)(2,1)S(1)}, u32[]{:S(2)}, u32[]{:S(2)}) collective-permute-start(s16[1056,128]{1,0:T(8,128)(2,1)S(1)} %finish.1.refs_0_), channel_id=1, source_target_pairs={{32,0},{48,16},{64,32},{80,48},{96,64},{112,80},{0,96},{16,112},{3... | collective-permute-start | bytes 811016 | tf_op jit(solution)/shard_map/ppermute | solution.py:781
  154.1 11.2 %collective-permute-start.13 = (s16[1056,128]{1,0:T(8,128)(2,1)S(1)}, s16[1056,128]{1,0:T(8,128)(2,1)S(1)}, u32[]{:S(2)}, u32[]{:S(2)}) collective-permute-start(s16[1056,128]{1,0:T(8,128)(2,1)S(1)} %finish.1.refs_0_), channel_id=1, source_target_pairs={{0,16},{16,0},{32,48},{48,32},{64,80},{80,64},{96,112},{112,96},{1... | collective-permute-start | bytes 811016 | tf_op jit(solution)/shard_map/ppermute | solution.py:784
  159.8 5.4 %collective-permute-start.16 = (s16[1056,128]{1,0:T(8,128)(2,1)S(1)}, s16[1056,128]{1,0:T(8,128)(2,1)S(1)}, u32[]{:S(2)}, u32[]{:S(2)}) collective-permute-start(s16[1056,128]{1,0:T(8,128)(2,1)S(1)} %collective-permute-done.12.refs_3_), channel_id=1, source_target_pairs={{0,16},{16,0},{32,48},{48,32},{64,80},{80,64},{96,112},{112,96},{1... | collective-permute-start | bytes 811016 | tf_op jit(solution)/shard_map/ppermute | solution.py:784
  163.4 2.1 %collective-permute-start.15 = (s16[1056,128]{1,0:T(8,128)(2,1)S(1)}, s16[1056,128]{1,0:T(8,128)(2,1)S(1)}, u32[]{:S(2)}, u32[]{:S(2)}) collective-permute-start(s16[1056,128]{1,0:T(8,128)(2,1)S(1)} %collective-permute-done.11.refs_2_), channel_id=1, source_target_pairs={{0,16},{16,0},{32,48},{48,32},{64,80},{80,64},{96,112},{112,96},{1... | collective-permute-start | bytes 811016 | tf_op jit(solution)/shard_map/ppermute | solution.py:784
  165.2 1.5 collective-permute-start.14
